TPU v7x, 128 devices: a whole 4x4x4 slice. The times are simulated.
128 devices in a mesh: chan: 8 (over z, core), tm: 16 (over y, x).
Axes of the slice: x: 4, y: 4, z: 4, core: 2. Of those that a mesh axis runs over, the one named last changes fastest.
Arguments:
- voltages: bfloat16 [2, 64, 8, 1048576], P(None, 'tm', 'chan'), may hold values from -6 to 6
- antenna_gains: float32 [2, 64, 8], P(None, None, 'chan'), may hold values from -0.75 to 0.75
- chirp_phase: float32 [8, 131072], P('chan'), may hold values from -3.140625 to 3.140625
- offsets: int32 [8], P('chan'), may hold values from 0 to 4095, as said below
- flags: int32 [8, 1024], P('chan', 'tm'), may hold values 0 or 1
- sample_phase_bins: int32 [1048576], P('tm'), may hold values from 0 to 2047
Outputs:
- dedispersed: bfloat16 [2, 8, 1048576], P(None, 'chan', 'tm')
- sk_weight: float32 [8, 1024], P('chan', 'tm')
- profile: float32 [8, 2048], P('chan', 'tm')
- band_profile: float32 [2048], P('tm')
Inputs may be any that keep to these rules, and one draw needn't show every extreme that they name: `offsets`: some channel has the offset 4096 - 1.
All inputs are finite; a program needn't handle non-finite values. No bound on the sum of `flags` on one device may be relied on, other than what follows from the above.
Results may differ from a plain program's by a relative error of at most 0.0045.
Values may be sent and summed in bfloat16 or wider, within the bound.
No kernel may reach another device: no remote copies, remote signals or barrier semaphores. Data moves between devices by JAX's collectives and lax.ppermute only.
A program may use at most 192 MiB of HBM per device.

v0:
```python
import math

import jax
import jax.numpy as jnp
from jax import lax
from jax.sharding import PartitionSpec as P

NFFT = 131072
OFFSET_BOUND = 4096
SKW = 1024
BINS = 2048


SK_WIDTH = 0.05
EPSILON = 1e-06


def shifted(value, axis, steps):
    count = lax.axis_size(axis)
    first, last = (max(0, -steps), min(count, count - steps))
    return lax.ppermute(value, axis, [(source, source + steps) for source in range(first, last)])


def in_blocks(shard, dim, length):
    before, after = (shard.shape[:dim], shard.shape[dim + 1 :])
    return jnp.moveaxis(shard.reshape(*before, length, -1, *after), dim, 0)


def sum_at_owner(shard, axis, dim):
    pieces = in_blocks(shard, dim, lax.axis_size(axis))
    arrived = lax.all_to_all(pieces, axis, split_axis=0, concat_axis=0, tiled=True)
    return arrived.sum(axis=0)


def copy_for_each(shard, axis):
    length = lax.axis_size(axis)
    return lax.all_to_all(
        jnp.broadcast_to(shard[None], (length, *shard.shape)), axis, 0, 0, tiled=True
    )


def over_copies(shard, axis):
    everything = copy_for_each(shard, axis)
    return jnp.sum(everything, axis=0)


def dft_table(length, sign):
    index = jnp.arange(length, dtype=jnp.int32)
    turns = index[:, None] * index[None, :] % length
    angle = sign * 2.0 * math.pi / length * turns.astype(jnp.float32)
    return (jnp.cos(angle), jnp.sin(angle))


def twiddle_table(row_total, col_total, length, sign):
    row_index = jnp.arange(row_total, dtype=jnp.int32)
    col_index = jnp.arange(col_total, dtype=jnp.int32)
    turns = row_index[:, None] * col_index[None, :] % length
    angle = sign * 2.0 * math.pi / length * turns.astype(jnp.float32)
    return (jnp.cos(angle), jnp.sin(angle))


def left_product(table, pair):

    def matmul_left(matrix, stacked):
        return jnp.einsum("kn,cnm->ckm", matrix, stacked, precision=lax.Precision.HIGHEST)

    return (
        matmul_left(table[0], pair[0]) - matmul_left(table[1], pair[1]),
        matmul_left(table[0], pair[1]) + matmul_left(table[1], pair[0]),
    )


def right_product(pair, table):

    def matmul_right(stacked, matrix):
        return jnp.einsum("ckn,nm->ckm", stacked, matrix, precision=lax.Precision.HIGHEST)

    return (
        matmul_right(pair[0], table[0]) - matmul_right(pair[1], table[1]),
        matmul_right(pair[0], table[1]) + matmul_right(pair[1], table[0]),
    )


def complex_times(first_pair, second_pair):
    return (
        first_pair[0] * second_pair[0] - first_pair[1] * second_pair[1],
        first_pair[0] * second_pair[1] + first_pair[1] * second_pair[0],
    )


def beamform(samples, weights):
    weight_real = weights[0][:, :, None]
    weight_imag = weights[1][:, :, None]
    out_real = jnp.sum(weight_real * samples[0] - weight_imag * samples[1], axis=0)
    out_imag = jnp.sum(weight_real * samples[1] + weight_imag * samples[0], axis=0)
    return jnp.stack([out_real, out_imag])


def cut_segment(paired_rows, start_at):
    return lax.dynamic_slice_in_dim(paired_rows, start_at, NFFT, 1)


def on_device(voltages, antenna_gains, chirp_phase, offsets, flags, sample_phase_bins):
    shards = lax.axis_size("tm")
    my_index = lax.axis_index("tm")
    half_length = NFFT // 2
    channels_here = voltages.shape[2]
    antennas_here = voltages.shape[1]
    own_weights = lax.dynamic_slice_in_dim(
        antenna_gains, my_index * antennas_here, antennas_here, 1
    )
    summed = beamform(voltages, own_weights)
    beam_sum = lax.psum_scatter(
        jnp.moveaxis(summed.reshape(2, channels_here, 1 * lax.axis_size("tm"), half_length), 2, 0),
        "tm",
        scatter_dimension=0,
        tiled=True,
    )[0]
    earlier = shifted(beam_sum, "tm", 1)
    later = shifted(beam_sum[:, :, :OFFSET_BOUND], "tm", -1)
    widened_samples = jnp.concatenate([earlier, beam_sum, later], axis=-1)
    segments = jax.vmap(cut_segment, in_axes=(1, 0), out_axes=1)(widened_samples, offsets)
    first_size = 1 << (NFFT.bit_length() - 1) // 2
    second_size = NFFT // first_size
    signal = (
        segments[0].reshape(channels_here, second_size, first_size),
        segments[1].reshape(channels_here, second_size, first_size),
    )
    outer_forward = dft_table(second_size, -1.0)
    inner_forward = dft_table(first_size, -1.0)
    twist_forward = twiddle_table(second_size, first_size, NFFT, -1.0)
    outer_inverse = dft_table(second_size, 1.0)
    inner_inverse = dft_table(first_size, 1.0)
    twist_inverse = twiddle_table(second_size, first_size, NFFT, 1.0)
    section_one = left_product(outer_forward, signal)
    section_two = complex_times(section_one, twist_forward)
    spectrum = right_product(section_two, inner_forward)
    phase_grid = jnp.transpose(
        chirp_phase.reshape(channels_here, first_size, second_size), (0, 2, 1)
    )
    filtered = complex_times(spectrum, (jnp.cos(phase_grid), jnp.sin(phase_grid)))
    back_one = right_product(filtered, inner_inverse)
    back_two = complex_times(back_one, twist_inverse)
    restored = left_product(outer_inverse, back_two)
    out_real = restored[0].reshape(channels_here, NFFT)[:, half_length:] / NFFT
    out_imag = restored[1].reshape(channels_here, NFFT)[:, half_length:] / NFFT
    dedispersed = jnp.stack([out_real, out_imag]).astype(jnp.bfloat16)
    power = out_real * out_real + out_imag * out_imag
    windows = power.reshape(channels_here, half_length // SKW, SKW)
    first_sum = jnp.sum(windows, axis=-1)
    second_sum = jnp.sum(windows * windows, axis=-1)
    kurtosis = (
        (SKW + 1.0) / (SKW - 1.0) * (SKW * second_sum / (first_sum * first_sum + EPSILON) - 1.0)
    )
    keep = (1 - flags).astype(jnp.float32)
    sk_weight = keep / (1.0 + ((kurtosis - 1.0) / SK_WIDTH) ** 2)
    weighted = (
        (sk_weight[:, :, None] * windows).reshape(channels_here, half_length).astype(jnp.bfloat16)
    )
    low_count = 128
    high_count = BINS // low_count
    bin_high = sample_phase_bins // low_count
    bin_low = sample_phase_bins % low_count
    low_onehot = (bin_low[:, None] == jnp.arange(low_count, dtype=jnp.int32)[None, :]).astype(
        jnp.bfloat16
    )
    high_mask = bin_high[None, :] == jnp.arange(high_count, dtype=jnp.int32)[:, None]
    spread = jnp.where(high_mask[None, :, :], weighted[:, None, :], jnp.zeros((), jnp.bfloat16))
    spread = spread.reshape(channels_here * high_count, half_length)
    folded = jnp.dot(spread, low_onehot, preferred_element_type=jnp.float32)
    partial_profile = folded.reshape(channels_here, BINS)
    profile = sum_at_owner(partial_profile, "tm", 1) * (BINS / (half_length * shards))
    band_profile = over_copies(jnp.sum(profile, axis=0), "chan")
    return (dedispersed, sk_weight, profile, band_profile)


def solution(mesh):
    placed = (
        P(None, "tm", "chan", None),
        P(None, None, "chan"),
        P("chan", None),
        P("chan"),
        P("chan", "tm"),
        P("tm"),
    )
    return jax.shard_map(
        on_device,
        mesh=mesh,
        in_specs=placed,
        out_specs=(P(None, "chan", "tm"), P("chan", "tm"), P("chan", "tm"), P("tm")),
        check_vma=False,
    )
```

profile of v0, /device:TPU:1, one launch (start us, length us, event | category | flops | bytes accessed | tf_op | source)
XLA Modules:
  0.0 401.6 jit_solution(3592292465170240676)
XLA Ops:
  7.2 0.7 fusion.115
  8.0 69.1 %fusion.2 = (f32[1048576]{0:T(1024)}, f32[1048576]{0:T(1024)}) fusion(f32[4]{0:T(128)S(1)} %get-tuple-element.31, f32[4]{0:T(128)S(1)} %get-tuple-element.30, bf16[2,4,1,1048576]{3,1,2,0:T(4,128)(2,1)} %param.6), kind=kLoop, calls=%fused_computation.7 | loop fusion | flops 39845888 | bytes 25165856 | tf_op jit(solution)/shard_map/reduce_sum | solution.py:94
  77.0 9.9 %maximum_bitcast_fusion = f32[16,2,1,65536]{3,1,2,0:T(2,128)} fusion(f32[1,1,16,65536]{3,0,1,2:T(1,128)} %bitcast.105, f32[1,1,16,65536]{3,0,1,2:T(1,128)} %bitcast.104), kind=kLoop, calls=%fused_computation.11 | loop fusion | flops 2097152 | bytes 16777216 | tf_op jit(solution)/shard_map/transpose | solution.py:114
  87.0 0.6 copy-done.5
  87.6 0.6 dynamic-slice.5
  88.2 143.0 %all-reduce.3.cloned.1.call-done = f32[16,2,1,65536]{3,1,2,0:T(2,128)} async-done(((f32[16,2,1,65536]{3,1,2,0:T(2,128)}), f32[16,2,1,65536]{3,1,2,0:T(2,128)}) %all-reduce.3.cloned.1.call-update) | async-done | bytes 8388624
  231.1 1.7 dynamic-slice_bitcast_fusion
  232.9 2.0 collective-permute-start
  234.8 0.9 add_select_fusion.4
  235.8 1.7 collective-permute-start.1
  237.5 17.2 %cosine_reduce_fusion = (f32[131072]{0:T(1024)S(1)}, f32[131072]{0:T(1024)S(1)}) fusion(f32[1,131072]{1,0:T(1,128)S(1)} %copy-done), kind=kLoop, calls=%fused_computation.95 | loop fusion | bytes 1572864 | tf_op jit(solution)/shard_map/cos | solution.py:141
  255.4 0.2 copy.24
  255.7 0.2 copy.25
  256.0 3.9 fusion.17
  259.9 2.7 slice_reduce_fusion.1
  262.8 5.8 %fusion.26 = f32[256,512]{1,0:T(8,128)S(1)} fusion(f32[512,256]{1,0:T(8,128)S(1)} %reshape.524), kind=kOutput, calls=%fused_computation.50 | convolution fusion | flops 808976384 | bytes 1048576 | tf_op jit(solution)/shard_map/kn,cnm->ckm/dot_general | solution.py:65
  268.8 6.0 %fusion.25 = f32[256,512]{1,0:T(8,128)S(1)} fusion(f32[512,256]{1,0:T(8,128)S(1)} %reshape.525), kind=kOutput, calls=%fused_computation.49 | convolution fusion | flops 808976384 | bytes 1048576 | tf_op jit(solution)/shard_map/kn,cnm->ckm/dot_general | solution.py:65
  274.8 5.9 %fusion.12 = f32[1,512,256]{1,2,0:T(8,128)S(1)} fusion(f32[256,512]{1,0:T(8,128)S(1)} %fusion.26, f32[512,256]{1,0:T(8,128)S(1)} %reshape.525), kind=kOutput, calls=%fused_computation.25 | convolution fusion | flops 809107456 | bytes 1572864 | tf_op jit(solution)/shard_map/kn,cnm->ckm/dot_general | solution.py:65
  280.6 6.1 %fusion.11 = f32[1,512,256]{1,2,0:T(8,128)S(1)} fusion(f32[256,512]{1,0:T(8,128)S(1)} %fusion.25, f32[512,256]{1,0:T(8,128)S(1)} %reshape.524), kind=kOutput, calls=%fused_computation.23 | convolution fusion | flops 809107456 | bytes 1572864 | tf_op jit(solution)/shard_map/kn,cnm->ckm/dot_general | solution.py:65
  286.7 3.9 fusion.47
  290.6 3.9 fusion.45
  294.5 4.3 %fusion.13 = f32[1,512,256]{2,1,0:T(8,128)S(1)} fusion(f32[512,256]{1,0:T(8,128)S(1)} %fusion.45, f32[1,512,256]{1,2,0:T(8,128)S(1)} %fusion.11, f32[1,512,256]{1,2,0:T(8,128)S(1)} %fusion.12), kind=kOutput, calls=%fused_computation.29 | convolution fusion | flops 405929984 | bytes 2097152 | tf_op jit(solution)/shard_map/ckn,nm->ckm/dot_general | solution.py:76
  298.8 3.9 fusion.42
  302.7 1.6 fusion.39
  304.3 1.6 fusion.37
  305.8 1.6 convolution_subtract_fusion.2
  307.4 1.6 convolution_add_fusion.2
  309.0 7.8 %fusion.28 = f32[256,512]{1,0:T(8,128)S(1)} fusion(f32[512,256]{1,0:T(8,128)S(1)} %convolution_add_fusion.2, f32[512,256]{1,0:T(8,128)S(1)} %convolution_subtract_fusion.2), kind=kOutput, calls=%fused_computation.52 | convolution fusion | flops 811204608 | bytes 1572864 | tf_op jit(solution)/shard_map/kn,cnm->ckm/dot_general | solution.py:65
  316.8 8.0 %fusion.27 = f32[256,512]{1,0:T(8,128)S(1)} fusion(f32[512,256]{1,0:T(8,128)S(1)} %convolution_add_fusion.2, f32[512,256]{1,0:T(8,128)S(1)} %convolution_subtract_fusion.2), kind=kOutput, calls=%fused_computation.51 | convolution fusion | flops 811204608 | bytes 1572864 | tf_op jit(solution)/shard_map/kn,cnm->ckm/dot_general | solution.py:65
  324.8 7.7 %fusion.10 = f32[1,512,256]{1,2,0:T(8,128)S(1)} fusion(f32[256,512]{1,0:T(8,128)S(1)} %fusion.28, f32[512,256]{1,0:T(8,128)S(1)} %convolution_add_fusion.2, f32[512,256]{1,0:T(8,128)S(1)} %convolution_subtract_fusion.2), kind=kOutput, calls=%fused_computation.21 | convolution fusion | flops 811335680 | bytes 2097152 | tf_op jit(solution)/shard_map/kn,cnm->ckm/dot_general | solution.py:65
  332.5 0.2 copy.26
  332.7 0.5 copy.30
  333.3 7.8 %fusion.9 = f32[1,512,256]{1,2,0:T(8,128)S(1)} fusion(f32[256,512]{1,0:T(8,128)S(1)} %fusion.27, f32[512,256]{1,0:T(8,128)S(1)} %convolution_add_fusion.2, f32[512,256]{1,0:T(8,128)S(1)} %convolution_subtract_fusion.2), kind=kOutput, calls=%fused_computation.19 | convolution fusion | flops 811335680 | bytes 2097152 | tf_op jit(solution)/shard_map/kn,cnm->ckm/dot_general | solution.py:65
  341.1 0.2 copy.27
  341.3 0.5 copy.31
  341.8 0.5 broadcast.462
  342.4 2.3 multiply_reduce_fusion
  345.2 0.3 copy.32
  345.4 1.0 convert_reduce_fusion
  346.4 0.4 fusion.197
  346.9 20.9 %fusion = f32[16,128]{1,0:T(8,128)S(1)} fusion(s32[65536]{0:T(1024)S(1)} %copy-done.2, bf16[16,65536]{1,0:T(8,128)(2,1)S(1)} %fusion.197), kind=kOutput, calls=%fused_computation.1 | convolution fusion | flops 276824064 | bytes 2367488 | tf_op jit(solution)/shard_map/dot_general | solution.py:170
  367.8 13.0 %all_to_all.11 = f32[16,1,128]{2,1,0:T(1,128)S(1)} all-to-all(f32[16,1,128]{2,1,0:T(1,128)S(1)} %bitcast.112), channel_id=1, replica_groups=mesh['chan'=8,'tm'=16] {'tm'}, dimensions={0} | all-to-all | bytes 16384 | tf_op jit(solution)/shard_map/all_to_all | solution.py:31
  380.8 0.5 broadcast_multiply_fusion
  381.3 0.6 broadcast_in_dim.15
  381.9 7.6 %all-to-all-start.1 = ((f32[8,1,128]{2,1,0:T(1,128)}), f32[8,1,128]{2,1,0:T(1,128)S(1)}, u32[]{:S(2)}, u32[]{:S(2)}) async-start(f32[8,1,128]{2,1,0:T(1,128)} %broadcast_in_dim.15), calls=%async_computation.1 | async-start | bytes 8192 | tf_op jit(solution)/shard_map/all_to_all | solution.py:37
  389.5 1.3 pad_maximum_fusion
  390.8 3.3 all-to-all-done.1
  394.1 0.5 reduce_sum.63
  (27 shorter events, 1.0 us)
Async XLA Ops:
  7.2 224.0 %all-reduce.3.cloned.1.call-start = ((), (), s32[]{:S(2)}) async-start(), calls=%async_computation.2 | async-start | bytes 16777216
  86.9 0.7 copy-start.5
  86.9 147.9 %copy-start.1 = (s32[65536]{0:T(1024)S(1)}, s32[65536]{0:T(1024)}, u32[]{:S(2)}) copy-start(s32[65536]{0:T(1024)} %param.11) | copy-start | bytes 786436
  86.9 150.6 %copy-start = (f32[1,131072]{1,0:T(1,128)S(1)}, f32[1,131072]{1,0:T(1,128)}, u32[]{:S(2)}) copy-start(f32[1,131072]{1,0:T(1,128)} %param.8) | copy-start | bytes 1572868
  232.9 23.1 %collective-permute-start = (f32[2,1,65536]{2,0,1:T(2,128)S(1)}, f32[2,1,65536]{2,0,1:T(2,128)S(1)}, u32[]{:S(2)}, u32[]{:S(2)}) collective-permute-start(f32[2,1,65536]{2,0,1:T(2,128)S(1)} %dynamic-slice_bitcast_fusion), channel_id=1, source_target_pairs={{0,1},{1,2},{2,3},{3,4},{4,5},{5,6},{6,7},{7,8},{8,9},{9,10},{10,1... | collective-permute-start | bytes 1572872 | tf_op jit(solution)/shard_map/ppermute | solution.py:21
  235.8 20.2 %collective-permute-start.1 = (f32[2,1,4096]{2,0,1:T(2,128)S(1)}, f32[2,1,4096]{2,0,1:T(2,128)S(1)}, u32[]{:S(2)}, u32[]{:S(2)}) collective-permute-start(f32[2,1,4096]{2,0,1:T(2,128)S(1)} %slice.56), channel_id=1, source_target_pairs={{1,0},{2,1},{3,2},{4,3},{5,4},{6,5},{7,6},{8,7},{9,8},{10,9},{11,1... | collective-permute-start | bytes 98312 | tf_op jit(solution)/shard_map/ppermute | solution.py:21
  332.5 12.6 %copy-start.4 = (s32[1,64]{1,0:T(1,128)S(1)}, s32[1,64]{1,0:T(1,128)}, u32[]{:S(2)}) copy-start(s32[1,64]{1,0:T(1,128)} %param.10) | copy-start | bytes 772
  333.2 13.6 %copy-start.2 = (s32[65536]{0:T(1024)S(1)}, s32[65536]{0:T(1024)}, u32[]{:S(2)}) copy-start(s32[65536]{0:T(1024)} %get-tuple-element.29) | copy-start | bytes 786436
  345.1 45.7 %copy-start.3 = (f32[1,64]{1,0:T(1,128)}, f32[1,64]{1,0:T(1,128)S(1)}, u32[]{:S(2)}) copy-start(f32[1,64]{1,0:T(1,128)S(1)} %bitcast_divide_fusion) | copy-start | bytes 772
  381.9 12.1 %all-to-all-start.1 = ((f32[8,1,128]{2,1,0:T(1,128)}), f32[8,1,128]{2,1,0:T(1,128)S(1)}, u32[]{:S(2)}, u32[]{:S(2)}) async-start(f32[8,1,128]{2,1,0:T(1,128)} %broadcast_in_dim.15), calls=%async_computation.1 | async-start | bytes 8192 | tf_op jit(solution)/shard_map/all_to_all | solution.py:37
Sparse Core Ops, SparseCore 0:
  87.1 143.9 all-reduce.2
where the time goes:
time: 409 us; the launch traced here: 402 us
  waiting for transfers between devices  146 us (36%)
  matrix products  98.2 us (24%)
  other arithmetic  90.2 us (22%)
  local copies, waits for them, and re-layouts  27.5 us (7%)
  between operations  15.3 us (4%)
  blocking collectives  13 us (3%)
  starting transfers between devices  11.3 us (3%)
    unnamed x2, waiting for transfers between devices  143 us
    reduce_sum x1, other arithmetic, beamform(): jnp.sum(weight_real * samples[0] - weight_imag * samples[1], axis=0)  69.1 us
    dot_general x8, matrix products, matmul_left(): jnp.einsum('kn,cnm->ckm', matrix, stacked, precision=lax.Precision.HIGHEST)  55 us
    dot_general x8, matrix products, matmul_right(): jnp.einsum('ckn,nm->ckm', stacked, matrix, precision=lax.Precision.HIGHEST)  22.2 us
    dot_general x1, matrix products, on_device(): folded = jnp.dot(spread, low_onehot, preferred_element_type=jnp.float32)  20.9 us
    cos x3, local copies, waits for them, and re-layouts, on_device(): jnp.cos(phase_grid)  17.4 us
    all_to_all x1, blocking collectives, sum_at_owner(): lax.all_to_all(pieces, axis, split_axis=0, concat_axis=0, tiled=True)  13 us
    transpose x1, other arithmetic, on_device(): jnp.moveaxis(summed.reshape(2, channels_here, 1 * lax.axis_size('tm'), ha...  9.91 us
  transfers between devices with their start and end apart: 4, of which 2 were waited for; matrix products, arithmetic and copies ran while one was open for 5% of the time, Pallas kernels for 0%

commit v1 on v0

v1 whole, which is shorter than its diff:
```python
import math

import jax
import jax.numpy as jnp
import ml_dtypes
import numpy as np
from jax import lax
from jax.experimental import pallas as pl
from jax.experimental.pallas import tpu as pltpu
from jax.sharding import PartitionSpec as P

NFFT = 131072
HALF = NFFT // 2
SIDE = 256
OFFSET_BOUND = 4096
SKW = 1024
BINS = 2048
SK_WIDTH = 0.05
EPSILON = 1e-06
GRID_SIDE = 4
N_TM = 16
LANES = 128
BEAM_SCALE = 64.0

F32 = jnp.float32
BF16 = jnp.bfloat16
WIRE = jnp.float16


def split_table(table):
    high = table.astype(np.float32).astype(ml_dtypes.bfloat16)
    low = (table - high.astype(np.float64)).astype(np.float32).astype(ml_dtypes.bfloat16)
    return np.stack([high, low])


def circle(turns, length):
    angle = 2.0 * math.pi / length * (turns % length)
    return np.cos(angle), np.sin(angle)


def make_tables():
    index = np.arange(SIDE, dtype=np.int64)
    even = circle(index[:, None] * index[None, :], SIDE)
    odd = circle((2 * index[:, None] + 1) * index[None, :], 2 * SIDE)
    odd_back = (odd[0].T, odd[1].T)
    left_even = split_table(np.concatenate(even, axis=1))
    left_odd = split_table(np.concatenate(odd, axis=1))
    left_back = split_table(np.concatenate(odd_back, axis=1))
    right = split_table(np.concatenate(even, axis=0))
    twist = []
    for parity in (0, 1):
        row = 2 * index[:, None] + parity
        twist.append(np.stack(circle(row * index[None, :], NFFT)))
    twist = np.stack(twist).astype(np.float32)
    group = (index[:, None] // 4 == index[None, :] // 4).astype(np.float32)
    return left_even, left_odd, left_back, right, twist, group


def steps(down, across):
    side = GRID_SIDE
    return [
        (s, (s // side + down) % side * side + (s % side + across) % side)
        for s in range(side * side)
    ]


def beam_body(blocks, gains, samples, out, table):
    @pl.when(pl.program_id(0) == 0)
    def build():
        shape = (128, 256)
        row = lax.broadcasted_iota(jnp.int32, shape, 0)
        col = lax.broadcasted_iota(jnp.int32, shape, 1)
        part = row // 64
        imag_out = row // 32 % 2
        slot = row % 32
        chunk = jnp.where(slot < 16, 2 * slot, 2 * (slot - 16) + 1)
        from_imag = col // 128
        source = col % 128 // 4
        antenna = col % 4
        real = jnp.zeros(shape, F32)
        imag = jnp.zeros(shape, F32)
        for a in range(4):
            real = jnp.where(antenna == a, gains[0, a], real)
            imag = jnp.where(antenna == a, gains[1, a], imag)
        cross = jnp.where(imag_out == 1, imag, -imag)
        value = jnp.where(imag_out == from_imag, real, cross) * BEAM_SCALE
        value = jnp.where(chunk == source, value, 0.0)
        high = value.astype(BF16).astype(F32)
        table[...] = jnp.where(part == 0, high, value - high).astype(BF16)

    weights = table[...]
    for pair in range(4):
        columns = []
        for group in (2 * pair, 2 * pair + 1):
            rows = pl.ds(group * 128, 128)
            columns.append(jnp.concatenate([samples[0, rows, :], samples[1, rows, :]], axis=0))
        product = jnp.dot(
            weights, jnp.concatenate(columns, axis=1), preferred_element_type=F32
        )
        both = product[:64] + product[64:]
        for which in (0, 1):
            group = 2 * pair + which
            lanes = slice(which * 128, which * 128 + 128)
            rows = pl.ds(group * 16, 16)
            for comp in (0, 1):
                base = comp * 32
                out[0, comp, rows, 0:128] = both[base : base + 16, lanes]
                out[0, comp, rows, 128:256] = both[base + 16 : base + 32, lanes]


def beamform(blocks, gains, samples):
    grid_spec = pltpu.PrefetchScalarGridSpec(
        num_scalar_prefetch=1,
        grid=(4,),
        in_specs=[
            pl.BlockSpec(memory_space=pltpu.SMEM),
            pl.BlockSpec((2, 1024, LANES), lambda i, blocks: (0, blocks[i], 0)),
        ],
        out_specs=pl.BlockSpec((1, 2, 128, SIDE), lambda i, blocks: (i, 0, 0, 0)),
        scratch_shapes=[pltpu.VMEM((128, 256), BF16)],
    )
    return pl.pallas_call(
        beam_body,
        grid_spec=grid_spec,
        out_shape=jax.ShapeDtypeStruct((4, 2, 128, SIDE), F32),
        name="beamform",
    )(blocks, gains, samples)


def response_body(offset, phase, out):
    row = lax.broadcasted_iota(jnp.int32, (SIDE, SIDE), 0)
    col = lax.broadcasted_iota(jnp.int32, (SIDE, SIDE), 1)
    for parity in (0, 1):
        bin_index = 2 * row + parity + 512 * col
        turns = jnp.bitwise_and(bin_index * offset[0], NFFT - 1)
        turns = jnp.where(turns >= HALF, turns - NFFT, turns)
        angle = phase[parity] + turns.astype(F32) * (2.0 * math.pi / NFFT)
        out[parity, 0] = jnp.cos(angle)
        out[parity, 1] = jnp.sin(angle)


def make_response(offset, phase):
    return pl.pallas_call(
        response_body,
        in_specs=[pl.BlockSpec(memory_space=pltpu.SMEM), pl.BlockSpec(memory_space=pltpu.VMEM)],
        out_shape=jax.ShapeDtypeStruct((2, 2, SIDE, SIDE), F32),
        name="response",
    )(offset, phase)


def halves(value):
    high = value.astype(BF16)
    return high, (value - high.astype(F32)).astype(BF16)


def from_left(table, real, imag, sign):
    crossed = (imag, -real) if sign > 0 else (-imag, real)
    top = jnp.concatenate([real, imag], axis=1)
    bottom = jnp.concatenate(crossed, axis=1)
    high, low = halves(jnp.concatenate([top, bottom], axis=0))
    first, second = table[0], table[1]
    product = (
        jnp.dot(first, high, preferred_element_type=F32)
        + jnp.dot(first, low, preferred_element_type=F32)
        + jnp.dot(second, high, preferred_element_type=F32)
    )
    return product[:, :SIDE], product[:, SIDE:]


def from_right(real, imag, table, sign):
    crossed = (imag, -real) if sign > 0 else (-imag, real)
    left = jnp.concatenate([real, imag], axis=0)
    right = jnp.concatenate(crossed, axis=0)
    high, low = halves(jnp.concatenate([left, right], axis=1))
    first, second = table[0], table[1]
    product = (
        jnp.dot(high, first, preferred_element_type=F32)
        + jnp.dot(low, first, preferred_element_type=F32)
        + jnp.dot(high, second, preferred_element_type=F32)
    )
    return product[:SIDE], product[SIDE:]


def times(real, imag, other_real, other_imag):
    return real * other_real - imag * other_imag, real * other_imag + imag * other_real


def main_body(
    offset,
    own_ref,
    before_ref,
    after_ref,
    response,
    keep_ref,
    bins_ref,
    left_even,
    left_odd,
    left_back,
    right,
    twist,
    group,
    out_ref,
    weight_ref,
    profile_ref,
    high_ref,
    low_ref,
    value_ref,
):
    own = [own_ref[0], own_ref[1]]
    row = lax.broadcasted_iota(jnp.int32, (16, SIDE), 0)
    col = lax.broadcasted_iota(jnp.int32, (16, SIDE), 1)
    wrapped = row * SIDE + col < offset[0]
    before = []
    for comp in (0, 1):
        head = jnp.where(wrapped, after_ref[comp], before_ref[comp, 0:16, :])
        before.append(jnp.concatenate([head, before_ref[comp, 16:, :]], axis=0))
    back = []
    for parity, table in ((0, left_even), (1, left_odd)):
        sign = 1.0 if parity == 0 else -1.0
        real, imag = from_left(
            table, before[0] + sign * own[0], before[1] + sign * own[1], 1
        )
        cos, sin = twist[parity, 0], twist[parity, 1]
        real, imag = times(real, imag, cos, -sin)
        real, imag = from_right(real, imag, right, 1)
        real, imag = times(real, imag, response[parity, 0], response[parity, 1])
        real, imag = from_right(real, imag, right, -1)
        real, imag = times(real, imag, cos, sin)
        back.append(from_left(left_even if parity == 0 else left_back, real, imag, -1))
    scale = 1.0 / (NFFT * BEAM_SCALE)
    real = (back[0][0] - back[1][0]) * scale
    imag = (back[0][1] - back[1][1]) * scale
    out_ref[0] = real.astype(BF16)
    out_ref[1] = imag.astype(BF16)

    power = real * real + imag * imag
    row_one = jnp.broadcast_to(jnp.sum(power, axis=1, keepdims=True), (SIDE, LANES))
    row_two = jnp.broadcast_to(jnp.sum(power * power, axis=1, keepdims=True), (SIDE, LANES))
    rows = jnp.concatenate([row_one, row_two], axis=1)
    sums = jnp.dot(
        group[...], rows, preferred_element_type=F32, precision=lax.Precision.HIGHEST
    )
    first_sum, second_sum = sums[:, :LANES], sums[:, LANES:]
    kurtosis = (
        (SKW + 1.0) / (SKW - 1.0) * (SKW * second_sum / (first_sum * first_sum + EPSILON) - 1.0)
    )
    weight = keep_ref[...] / (1.0 + ((kurtosis - 1.0) / SK_WIDTH) ** 2)
    weight_ref[...] = weight
    value_ref[...] = (
        jnp.concatenate([weight, weight], axis=1) * power
    ).astype(BF16).astype(F32)

    bins = bins_ref[...]
    high_ref[...] = (bins // LANES).astype(F32)
    low_ref[...] = (bins % LANES).astype(F32)

    per_step = 8
    high_rows = lax.broadcasted_iota(jnp.int32, (16, SIDE), 0).astype(F32).astype(BF16)
    low_rows = lax.broadcasted_iota(jnp.int32, (LANES, SIDE), 0).astype(F32).astype(BF16)
    one, zero = jnp.ones((), BF16), jnp.zeros((), BF16)

    def fold(step, total):
        start = pl.multiple_of(step * per_step, per_step)
        high_block = high_ref[pl.ds(start, per_step), :]
        low_block = low_ref[pl.ds(start, per_step), :]
        value_block = value_ref[pl.ds(start, per_step), :]
        spreads, marks = [], []
        for r in range(per_step):
            high = jnp.broadcast_to(high_block[r : r + 1], (16, SIDE)).astype(BF16)
            value = jnp.broadcast_to(value_block[r : r + 1], (16, SIDE)).astype(BF16)
            spreads.append(jnp.where(high == high_rows, value, zero))
            low = jnp.broadcast_to(low_block[r : r + 1], (LANES, SIDE)).astype(BF16)
            marks.append(jnp.where(low == low_rows, one, zero))
        return total + lax.dot_general(
            jnp.concatenate(spreads, axis=1),
            jnp.concatenate(marks, axis=1),
            (((1,), (1,)), ((), ())),
            preferred_element_type=F32,
        )

    total = lax.fori_loop(0, SIDE // per_step, fold, jnp.zeros((16, LANES), F32))
    profile_ref[...] = total * (BINS / (HALF * N_TM))


def filter_and_fold(offset, own, before, after, response, keep, bins, tables):
    vmem = pl.BlockSpec(memory_space=pltpu.VMEM)
    return pl.pallas_call(
        main_body,
        in_specs=[pl.BlockSpec(memory_space=pltpu.SMEM)] + [vmem] * (6 + len(tables)),
        out_shape=(
            jax.ShapeDtypeStruct((2, SIDE, SIDE), BF16),
            jax.ShapeDtypeStruct((SIDE, LANES), F32),
            jax.ShapeDtypeStruct((16, LANES), F32),
        ),
        scratch_shapes=[pltpu.VMEM((SIDE, SIDE), F32)] * 3,
        compiler_params=pltpu.CompilerParams(vmem_limit_bytes=48 * 1024 * 1024),
        name="filter_and_fold",
    )(offset, own, before, after, response, keep, bins, *tables)


def send(value, down, across):
    return lax.ppermute(value, "tm", steps(down, across))


def sum_of(parts):
    total = parts[0].astype(F32)
    for part in parts[1:]:
        total = total + part.astype(F32)
    return total


def on_device(voltages, antenna_gains, chirp_phase, offsets, flags, sample_phase_bins):
    tables = make_tables()
    my_index = lax.axis_index("tm")
    down_at, across_at = my_index // GRID_SIDE, my_index % GRID_SIDE
    samples = (
        voltages.reshape(2, 4, TIME_CHUNKS, LANES)
        .transpose(0, 2, 1, 3)
        .reshape(2, TIME_CHUNKS * 4, LANES)
    )
    gains = lax.dynamic_slice_in_dim(antenna_gains[:, :, 0], my_index * 4, 4, 1)
    around = jnp.arange(GRID_SIDE, dtype=jnp.int32)

    order = (2, 1, 3, 0)
    partial = []
    for half in (0, 1):
        got = []
        for first in order:
            if half == 0:
                rows, cols = (down_at + first) % GRID_SIDE, (across_at + around) % GRID_SIDE
            else:
                rows, cols = (down_at + around) % GRID_SIDE, (across_at + first) % GRID_SIDE
            blocks = ((rows * GRID_SIDE + cols) * 2 + half).astype(jnp.int32)
            message = beamform(blocks, gains, samples)
            if first:
                wire = message.astype(WIRE)
                message = send(wire, first, 0) if half == 0 else send(wire, 0, first)
            got.append(message)
        partial.append(got)
    beam = []
    for half in (0, 1):
        got = []
        for second in order:
            part = sum_of([message[second] for message in partial[half]])
            if second:
                wire = part.astype(WIRE)
                part = send(wire, 0, second) if half == 0 else send(wire, second, 0)
            got.append(part)
        beam.append(sum_of(got))
    shards = N_TM
    ahead = [(s, s + 1) for s in range(shards - 1)]
    behind = [(s + 1, s) for s in range(shards - 1)]
    before = [lax.ppermute(part.astype(WIRE), "tm", ahead) for part in beam]
    after = lax.ppermute(beam[0][:, :16].astype(WIRE), "tm", behind)
    own = jnp.concatenate(beam, axis=1)
    before = jnp.concatenate(before, axis=1).astype(F32)
    after = after.astype(F32)

    phase = jnp.transpose(chirp_phase.reshape(SIDE, 2 * SIDE), (1, 0))
    phase = phase.reshape(SIDE, 2, SIDE).transpose(1, 0, 2)
    response = make_response(offsets, phase)
    keep = jnp.broadcast_to((1 - flags).astype(F32).reshape(64, 1, 1), (64, 4, LANES))
    keep = keep.reshape(SIDE, LANES)
    bins = sample_phase_bins.reshape(SIDE, SIDE)
    filtered, weight, partial_profile = filter_and_fold(
        offsets, own, before, after, response, keep, bins, tables
    )
    dedispersed = filtered.reshape(2, 1, HALF)
    sk_weight = weight.reshape(64, 4, LANES)[:, 0, 0].reshape(1, 64)
    channels = lax.axis_size("chan")
    pieces = jnp.broadcast_to(partial_profile[None], (channels, N_TM, LANES))
    arrived = lax.all_to_all(
        pieces.reshape(channels * N_TM, LANES), ("chan", "tm"), 0, 0, tiled=True
    ).reshape(channels, N_TM, LANES)
    by_channel = jnp.sum(arrived, axis=1)
    profile = lax.dynamic_slice_in_dim(by_channel, lax.axis_index("chan"), 1, 0)
    band_profile = jnp.sum(by_channel, axis=0)
    return (dedispersed, sk_weight, profile, band_profile)


TIME_CHUNKS = 1048576 // LANES


def solution(mesh):
    placed = (
        P(None, "tm", "chan", None),
        P(None, None, "chan"),
        P("chan", None),
        P("chan"),
        P("chan", "tm"),
        P("tm"),
    )
    return jax.shard_map(
        on_device,
        mesh=mesh,
        in_specs=placed,
        out_specs=(P(None, "chan", "tm"), P("chan", "tm"), P("chan", "tm"), P("tm")),
        check_vma=False,
    )
```

time: 409 us -> 149 us (0.36); the launches traced: 402 us -> 147 us
  waiting for transfers between devices: 146 us -> 10.4 us
  matrix products: 98.2 us -> 0 us
  other arithmetic: 90.2 us -> 27.5 us
  Pallas kernels: 0 us -> 58.5 us
  starting transfers between devices: 11.3 us -> 41.1 us
  local copies, waits for them, and re-layouts: 27.5 us -> 8.34 us
  between operations: 15.3 us -> 1.57 us
  blocking collectives: 13 us -> 0 us
    unnamed x2 -> x0, waiting for transfers between devices: 143 us -> none
    dot_general x17 -> x0, matrix products: 98.2 us -> none  [the longest x8 55 us: matmul_left(): jnp.einsum('kn,cnm->ckm', matrix, stacked, precision=lax.Precision.HIGHEST)]
    reduce_sum x5 -> x2, other arithmetic: 69.9 us -> 0.67 us  [the longest x1 0.66 us: on_device(): band_profile = jnp.sum(by_channel, axis=0)]
    pallas_call x0 -> x10, Pallas kernels: none -> 58.5 us  [the longest x8 38.2 us: beamform(): pl.pallas_call(beam_body, grid_spec=grid_spec, out_shape=jax.ShapeDtypeSt...]
    ppermute x2 -> x15, starting transfers between devices: 3.71 us -> 24.7 us  [the longest x12 17.5 us: send(): return lax.ppermute(value, 'tm', steps(down, across))]
    cos x3 -> x0, local copies, waits for them, and re-layouts: 17.4 us -> none  [on_device(): jnp.cos(phase_grid)]
    convert_element_type x1 -> x10, other arithmetic: 0.99 us -> 16.8 us  [the longest x6 11.8 us: on_device(): wire = message.astype(WIRE)]
    all_to_all x1 -> x0, blocking collectives: 13 us -> none  [sum_at_owner(): lax.all_to_all(pieces, axis, split_axis=0, concat_axis=0, tiled=True)]
  transfers between devices with their start and end apart: 4 -> 16, of which waited for: 2 -> 2; matrix products, arithmetic and copies ran while one was open for 5% -> 19% of each run, Pallas kernels for 0% -> 25%
where the time goes in v1:
time: 149 us; the launch traced here: 147 us
  Pallas kernels  58.5 us (39%)
  starting transfers between devices  41.1 us (28%)
  other arithmetic  27.5 us (18%)
  waiting for transfers between devices  10.4 us (7%)
  local copies, waits for them, and re-layouts  8.34 us (6%)
  between operations  1.57 us (1%)
    pallas_call x8, Pallas kernels, beamform(): pl.pallas_call(beam_body, grid_spec=grid_spec, out_shape=jax.ShapeDtypeSt...  38.2 us
    ppermute x12, starting transfers between devices, send(): return lax.ppermute(value, 'tm', steps(down, across))  17.5 us
    all_to_all x1, starting transfers between devices, on_device(): lax.all_to_all(pieces.reshape(channels * N_TM, LANES), ('chan', 'tm'), 0,...  16.4 us
    pallas_call x1, Pallas kernels, filter_and_fold(): pl.pallas_call(main_body, in_specs=[pl.BlockSpec(memory_space=pltpu.SMEM)...  16.2 us
    convert_element_type x6, other arithmetic, on_device(): wire = message.astype(WIRE)  11.8 us
    all_to_all x1, waiting for transfers between devices, on_device(): lax.all_to_all(pieces.reshape(channels * N_TM, LANES), ('chan', 'tm'), 0,...  8.18 us
    ppermute x2, starting transfers between devices, on_device(): before = [lax.ppermute(part.astype(WIRE), 'tm', ahead) for part in beam]  5.91 us
    pallas_call x1, Pallas kernels, make_response(): pl.pallas_call(response_body, in_specs=[pl.BlockSpec(memory_space=pltpu.S...  4.1 us
  transfers between devices with their start and end apart: 16, of which 2 were waited for; matrix products, arithmetic and copies ran while one was open for 19% of the time, Pallas kernels for 25%

profile of v1, /device:TPU:1, one launch (start us, length us, event | category | flops | bytes accessed | tf_op | source)
XLA Modules:
  0.0 147.3 jit_solution(12899705758313838892)
XLA Ops:
  0.7 0.6 copy-done
  1.3 0.6 constant_dynamic-slice_fusion.1
  2.5 4.8 %beamform.8 = f32[4,2,128,256]{3,2,1,0:T(8,128)} custom-call(s32[4]{0:T(128)} %get-tuple-element.25.blocks, f32[2,4]{1,0:T(2,128)} %bitcast.52, bf16[2,32768,128]{2,1,0:T(8,128)(2,1)} %bitcast.41), custom_call_target="tpu_custom_call" | custom-call | tf_op jit(solution)/shard_map/beamform/pallas_call | solution.py:122
  7.2 1.3 convert_element_type.154
  8.5 3.8 %collective-permute-start = (f16[4,2,128,256]{3,2,1,0:T(8,128)(2,1)S(1)}, f16[4,2,128,256]{3,2,1,0:T(8,128)(2,1)S(1)}, u32[]{:S(2)}, u32[]{:S(2)}) collective-permute-start(f16[4,2,128,256]{3,2,1,0:T(8,128)(2,1)S(1)} %convert_element_type.154), channel_id=1, source_target_pairs={{0,8},{1,9},{2,10},{3,11},{4,12},{5,13},{6,14},{7,15},{8,0},{9,1},... | collective-permute-start | bytes 1572872 | tf_op jit(solution)/shard_map/ppermute | solution.py:302
  12.4 4.8 %beamform.9 = f32[4,2,128,256]{3,2,1,0:T(8,128)} custom-call(s32[4]{0:T(128)} %get-tuple-element.24.blocks, f32[2,4]{1,0:T(2,128)} %bitcast.53, bf16[2,32768,128]{2,1,0:T(8,128)(2,1)} %bitcast.42), custom_call_target="tpu_custom_call" | custom-call | tf_op jit(solution)/shard_map/beamform/pallas_call | solution.py:122
  17.1 2.1 %convert_element_type.156 = f16[4,2,128,256]{3,2,1,0:T(8,128)(2,1)} convert(f32[4,2,128,256]{3,2,1,0:T(8,128)} %beamform.9) | non-fusion elementwise | flops 262144 | bytes 1572864 | tf_op jit(solution)/shard_map/convert_element_type | solution.py:336
  19.6 0.5 multiply_add_fusion.3
  20.1 4.8 %beamform.10 = f32[4,2,128,256]{3,2,1,0:T(8,128)} custom-call(s32[4]{0:T(128)} %get-tuple-element.23.blocks, f32[2,4]{1,0:T(2,128)} %bitcast.54, bf16[2,32768,128]{2,1,0:T(8,128)(2,1)} %bitcast.43), custom_call_target="tpu_custom_call" | custom-call | tf_op jit(solution)/shard_map/beamform/pallas_call | solution.py:122
  24.9 2.1 %convert_element_type.158 = f16[4,2,128,256]{3,2,1,0:T(8,128)(2,1)} convert(f32[4,2,128,256]{3,2,1,0:T(8,128)} %beamform.10) | non-fusion elementwise | flops 262144 | bytes 1572864 | tf_op jit(solution)/shard_map/convert_element_type | solution.py:336
  27.0 2.3 %collective-permute-start.2 = (f16[4,2,128,256]{3,2,1,0:T(8,128)(2,1)}, f16[4,2,128,256]{3,2,1,0:T(8,128)(2,1)}, u32[]{:S(2)}, u32[]{:S(2)}) collective-permute-start(f16[4,2,128,256]{3,2,1,0:T(8,128)(2,1)} %convert_element_type.158), channel_id=1, source_target_pairs={{0,12},{1,13},{2,14},{3,15},{4,0},{5,1},{6,2},{7,3},{8,4},{9,5},{1... | collective-permute-start | bytes 1572872 | tf_op jit(solution)/shard_map/ppermute | solution.py:302
  29.3 4.8 %beamform.12 = f32[4,2,128,256]{3,2,1,0:T(8,128)} custom-call(s32[4]{0:T(128)} %get-tuple-element.22.blocks, f32[2,4]{1,0:T(2,128)} %bitcast.55, bf16[2,32768,128]{2,1,0:T(8,128)(2,1)} %bitcast.44), custom_call_target="tpu_custom_call" | custom-call | tf_op jit(solution)/shard_map/beamform/pallas_call | solution.py:122
  34.0 2.1 %convert_element_type.172 = f16[4,2,128,256]{3,2,1,0:T(8,128)(2,1)} convert(f32[4,2,128,256]{3,2,1,0:T(8,128)} %beamform.12) | non-fusion elementwise | flops 262144 | bytes 1572864 | tf_op jit(solution)/shard_map/convert_element_type | solution.py:336
  36.1 2.7 %collective-permute-start.6 = (f16[4,2,128,256]{3,2,1,0:T(8,128)(2,1)}, f16[4,2,128,256]{3,2,1,0:T(8,128)(2,1)}, u32[]{:S(2)}, u32[]{:S(2)}) collective-permute-start(f16[4,2,128,256]{3,2,1,0:T(8,128)(2,1)} %convert_element_type.172), channel_id=1, source_target_pairs={{0,2},{1,3},{2,0},{3,1},{4,6},{5,7},{6,4},{7,5},{8,10},{9,11},{10,... | collective-permute-start | bytes 1572872 | tf_op jit(solution)/shard_map/ppermute | solution.py:302
  38.9 0.5 multiply_add_fusion.1
  39.4 4.8 %beamform.13 = f32[4,2,128,256]{3,2,1,0:T(8,128)} custom-call(s32[4]{0:T(128)} %get-tuple-element.21.blocks, f32[2,4]{1,0:T(2,128)} %bitcast.56, bf16[2,32768,128]{2,1,0:T(8,128)(2,1)} %bitcast.45), custom_call_target="tpu_custom_call" | custom-call | tf_op jit(solution)/shard_map/beamform/pallas_call | solution.py:122
  44.2 2.1 %convert_element_type.174 = f16[4,2,128,256]{3,2,1,0:T(8,128)(2,1)} convert(f32[4,2,128,256]{3,2,1,0:T(8,128)} %beamform.13) | non-fusion elementwise | flops 262144 | bytes 1572864 | tf_op jit(solution)/shard_map/convert_element_type | solution.py:336
  46.6 4.8 %beamform.14 = f32[4,2,128,256]{3,2,1,0:T(8,128)} custom-call(s32[4]{0:T(128)} %get-tuple-element.20.blocks, f32[2,4]{1,0:T(2,128)} %bitcast.57, bf16[2,32768,128]{2,1,0:T(8,128)(2,1)} %bitcast.46), custom_call_target="tpu_custom_call" | custom-call | tf_op jit(solution)/shard_map/beamform/pallas_call | solution.py:122
  51.4 2.1 %convert_element_type.176 = f16[4,2,128,256]{3,2,1,0:T(8,128)(2,1)} convert(f32[4,2,128,256]{3,2,1,0:T(8,128)} %beamform.14) | non-fusion elementwise | flops 262144 | bytes 1572864 | tf_op jit(solution)/shard_map/convert_element_type | solution.py:336
  53.5 2.4 %collective-permute-start.8 = (f16[4,2,128,256]{3,2,1,0:T(8,128)(2,1)}, f16[4,2,128,256]{3,2,1,0:T(8,128)(2,1)}, u32[]{:S(2)}, u32[]{:S(2)}) collective-permute-start(f16[4,2,128,256]{3,2,1,0:T(8,128)(2,1)} %convert_element_type.176), channel_id=1, source_target_pairs={{0,3},{1,0},{2,1},{3,2},{4,7},{5,4},{6,5},{7,6},{8,11},{9,8},{10,9... | collective-permute-start | bytes 1572872 | tf_op jit(solution)/shard_map/ppermute | solution.py:302
  56.4 4.8 %beamform.11 = f32[4,2,128,256]{3,2,1,0:T(8,128)} custom-call(s32[4]{0:T(128)} %add_multiply_fusion.blocks, f32[2,4]{1,0:T(2,128)} %bitcast.58, bf16[2,32768,128]{2,1,0:T(8,128)(2,1)} %bitcast.47), custom_call_target="tpu_custom_call" | custom-call | tf_op jit(solution)/shard_map/beamform/pallas_call | solution.py:122
  61.1 0.5 multiply_add_fusion.blocks
  61.7 4.9 %beamform.15 = f32[4,2,128,256]{3,2,1,0:T(8,128)} custom-call(s32[4]{0:T(128)} %multiply_add_fusion.blocks, f32[2,4]{1,0:T(2,128)} %bitcast.59, bf16[2,32768,128]{2,1,0:T(8,128)(2,1)} %bitcast.48), custom_call_target="tpu_custom_call" | custom-call | tf_op jit(solution)/shard_map/beamform/pallas_call | solution.py:122
  66.6 1.6 %fusion.10 = (f16[2,128,256]{2,1,0:T(8,128)(2,1)S(1)}, f16[2,128,256]{2,1,0:T(8,128)(2,1)S(1)}, f16[2,128,256]{2,1,0:T(8,128)(2,1)S(1)}) fusion(f32[4,2,128,256]{3,2,1,0:T(8,128)S(1)} %copy-done.7, f16[4,2,128,256]{3,2,1,0:T(8,128)(2,1)} %collective-permute-done.2, f16[4,2,128,256]{3,2,1,0:T(8,128)(2,1)} %collective-permute-done.1, ...), kind=kLoop, calls=%fused_computation.21 | loop fusion | flops 1376256 | bytes 2359296 | tf_op jit(solution)/shard_map/add | solution.py:308
  68.3 0.7 collective-permute-start.4
  68.9 2.1 %collective-permute-start.5 = (f16[2,128,256]{2,1,0:T(8,128)(2,1)S(1)}, f16[2,128,256]{2,1,0:T(8,128)(2,1)S(1)}, u32[]{:S(2)}, u32[]{:S(2)}) collective-permute-start(f16[2,128,256]{2,1,0:T(8,128)(2,1)S(1)} %get-tuple-element.15), channel_id=1, source_target_pairs={{0,3},{1,0},{2,1},{3,2},{4,7},{5,4},{6,5},{7,6},{8,11},{9,8},{10,9... | collective-permute-start | bytes 393224 | tf_op jit(solution)/shard_map/ppermute | solution.py:302
  71.0 1.7 %fusion.13 = (f16[2,128,256]{2,1,0:T(8,128)(2,1)S(1)}, f16[2,128,256]{2,1,0:T(8,128)(2,1)S(1)}, f16[2,128,256]{2,1,0:T(8,128)(2,1)S(1)}) fusion(f32[4,2,128,256]{3,2,1,0:T(8,128)} %beamform.15, f16[4,2,128,256]{3,2,1,0:T(8,128)(2,1)} %collective-permute-done.8, f16[4,2,128,256]{3,2,1,0:T(8,128)(2,1)} %collective-permute-done.7, ...), kind=kLoop, calls=%fused_computation.24 | loop fusion | flops 1376256 | bytes 2359296 | tf_op jit(solution)/shard_map/add | solution.py:308
  72.8 2.7 %collective-permute-start.11 = (f16[2,128,256]{2,1,0:T(8,128)(2,1)S(1)}, f16[2,128,256]{2,1,0:T(8,128)(2,1)S(1)}, u32[]{:S(2)}, u32[]{:S(2)}) collective-permute-start(f16[2,128,256]{2,1,0:T(8,128)(2,1)S(1)} %get-tuple-element.18), channel_id=1, source_target_pairs={{0,12},{1,13},{2,14},{3,15},{4,0},{5,1},{6,2},{7,3},{8,4},{9,5},{1... | collective-permute-start | bytes 393224 | tf_op jit(solution)/shard_map/ppermute | solution.py:302
  75.5 2.0 %fusion.19 = (f16[2,128,256]{2,1,0:T(8,128)(2,1)S(1)}, f32[2,128,256]{2,1,0:T(8,128)}) fusion(f32[4,2,128,256]{3,2,1,0:T(8,128)S(1)} %copy-done.7, f16[4,2,128,256]{3,2,1,0:T(8,128)(2,1)} %collective-permute-done.2, f16[4,2,128,256]{3,2,1,0:T(8,128)(2,1)} %collective-permute-done.1, f16[4,2,128,256]{3,2,1,0:T(8,128)(2,1)} %copy-done.8, ...), kind=kLoop, calls=%fused_computation.48 | loop fusion | flops 851968 | bytes 1441792 | tf_op jit(solution)/shard_map/convert_element_type | solution.py:353
  77.5 3.5 %collective-permute-start.12 = (f16[2,128,256]{2,1,0:T(8,128)(2,1)S(1)}, f16[2,128,256]{2,1,0:T(8,128)(2,1)}, u32[]{:S(2)}, u32[]{:S(2)}) collective-permute-start(f16[2,128,256]{2,1,0:T(8,128)(2,1)S(1)} %get-tuple-element.10), channel_id=1, source_target_pairs={{0,1},{1,2},{2,3},{3,4},{4,5},{5,6},{6,7},{7,8},{8,9},{9,10},{10,1... | collective-permute-start | bytes 393224 | tf_op jit(solution)/shard_map/ppermute | solution.py:353
  81.0 2.0 %fusion.21 = (f16[2,128,256]{2,1,0:T(8,128)(2,1)}, f32[2,128,256]{2,1,0:T(8,128)}) fusion(f32[4,2,128,256]{3,2,1,0:T(8,128)} %beamform.15, f16[4,2,128,256]{3,2,1,0:T(8,128)(2,1)} %collective-permute-done.8, f16[4,2,128,256]{3,2,1,0:T(8,128)(2,1)} %collective-permute-done.7, f16[4,2,128,256]{3,2,1,0:T(8,128)(2,1)} %collective-permute-done.6, ...), kind=kLoop, calls=%fused_computation.49 | loop fusion | flops 851968 | bytes 1441792 | tf_op jit(solution)/shard_map/convert_element_type | solution.py:353
  83.0 2.5 %collective-permute-start.13 = (f16[2,128,256]{2,1,0:T(8,128)(2,1)}, f16[2,128,256]{2,1,0:T(8,128)(2,1)}, u32[]{:S(2)}, u32[]{:S(2)}) collective-permute-start(f16[2,128,256]{2,1,0:T(8,128)(2,1)} %get-tuple-element.12), channel_id=1, source_target_pairs={{0,1},{1,2},{2,3},{3,4},{4,5},{5,6},{6,7},{7,8},{8,9},{9,10},{10,1... | collective-permute-start | bytes 393224 | tf_op jit(solution)/shard_map/ppermute | solution.py:353
  86.6 3.0 %reduce.6 = f32[131072]{0:T(1024)S(1)} reduce(f32[1,131072]{1,0:T(1,128)} %param.14, f32[]{:T(128)} %broadcast.71), dimensions={0}, to_apply=%param.14.reduce_sub_computation.3 | reduce | bytes 1048580 | tf_op args[2]
  90.2 0.9 copy.28
  91.0 1.0 reshape.101.bins_ref
  92.3 4.1 %response.1 = f32[2,2,256,256]{3,2,1,0:T(8,128)} custom-call(s32[1]{0:T(128)S(6)} %copy.29.offset, f32[2,256,256]{2,1,0:T(8,128)} %bitcast.49), custom_call_target="tpu_custom_call" | custom-call | tf_op jit(solution)/shard_map/response/pallas_call | solution.py:143
  96.4 1.3 collective-permute-start.14
  97.7 1.1 pad_maximum_fusion.own_ref
  98.7 2.1 %collective-permute-done.14 = f16[2,16,256]{2,1,0:T(8,128)(2,1)S(1)} collective-permute-done((f16[2,16,256]{2,1,0:T(8,128)(2,1)S(1)}, f16[2,16,256]{2,1,0:T(8,128)(2,1)S(1)}, u32[]{:S(2)}, u32[]{:S(2)}) %collective-permute-start.14) | collective-permute-done | bytes 16416 | tf_op jit(solution)/shard_map/ppermute | solution.py:354
  100.9 1.0 maximum_convert_fusion.before_ref
  102.0 1.2 copy-done.1
  103.3 16.2 %filter_and_fold.1 = (bf16[2,256,256]{2,1,0:T(8,128)(2,1)S(1)}, f32[256,128]{1,0:T(8,128)S(1)}, f32[16,128]{1,0:T(8,128)S(1)}) custom-call(s32[1]{0:T(128)S(6)} %copy.29.offset, f32[2,256,256]{2,1,0:T(8,128)S(1)} %pad_maximum_fusion.own_ref, f32[2,256,256]{2,1,0:T(8,128)S(1)} %maximum_convert_fusion.before_ref, ...), custom_call_target="tpu_custom_call" | custom-call | tf_op jit(solution)/shard_map/filter_and_fold/pallas_call | solution.py:287
  119.5 0.7 broadcast_in_dim.21
  120.1 16.4 %all-to-all-start = ((f32[128,1,128]{2,1,0:T(1,128)}), f32[128,1,128]{2,1,0:T(1,128)S(1)}, u32[]{:S(2)}, u32[]{:S(2)}) async-start(f32[128,1,128]{2,1,0:T(1,128)} %bitcast.19), calls=%async_computation | async-start | bytes 131072 | tf_op jit(solution)/shard_map/all_to_all | solution.py:372
  136.5 0.8 reshape.102
  137.3 0.6 copy.26
  137.9 8.2 %all-to-all-done = f32[128,1,128]{2,1,0:T(1,128)S(1)} async-done(((f32[128,1,128]{2,1,0:T(1,128)}), f32[128,1,128]{2,1,0:T(1,128)S(1)}, u32[]{:S(2)}, u32[]{:S(2)}) %all-to-all-start) | async-done | bytes 65568 | tf_op jit(solution)/shard_map/all_to_all | solution.py:372
  146.6 0.7 reduce_sum.19
  (52 shorter events, 4.0 us)
Async XLA Ops:
  0.6 0.7 copy-start
  8.5 44.9 %collective-permute-start = (f16[4,2,128,256]{3,2,1,0:T(8,128)(2,1)S(1)}, f16[4,2,128,256]{3,2,1,0:T(8,128)(2,1)S(1)}, u32[]{:S(2)}, u32[]{:S(2)}) collective-permute-start(f16[4,2,128,256]{3,2,1,0:T(8,128)(2,1)S(1)} %convert_element_type.154), channel_id=1, source_target_pairs={{0,8},{1,9},{2,10},{3,11},{4,12},{5,13},{6,14},{7,15},{8,0},{9,1},... | collective-permute-start | bytes 1572872 | tf_op jit(solution)/shard_map/ppermute | solution.py:302
  19.2 47.4 %collective-permute-start.1 = (f16[4,2,128,256]{3,2,1,0:T(8,128)(2,1)}, f16[4,2,128,256]{3,2,1,0:T(8,128)(2,1)}, u32[]{:S(2)}, u32[]{:S(2)}) collective-permute-start(f16[4,2,128,256]{3,2,1,0:T(8,128)(2,1)} %convert_element_type.156), channel_id=1, source_target_pairs={{0,4},{1,5},{2,6},{3,7},{4,8},{5,9},{6,10},{7,11},{8,12},{9,13},{1... | collective-permute-start | bytes 1572872 | tf_op jit(solution)/shard_map/ppermute | solution.py:302
  27.0 39.6 %collective-permute-start.2 = (f16[4,2,128,256]{3,2,1,0:T(8,128)(2,1)}, f16[4,2,128,256]{3,2,1,0:T(8,128)(2,1)}, u32[]{:S(2)}, u32[]{:S(2)}) collective-permute-start(f16[4,2,128,256]{3,2,1,0:T(8,128)(2,1)} %convert_element_type.158), channel_id=1, source_target_pairs={{0,12},{1,13},{2,14},{3,15},{4,0},{5,1},{6,2},{7,3},{8,4},{9,5},{1... | collective-permute-start | bytes 1572872 | tf_op jit(solution)/shard_map/ppermute | solution.py:302
  36.1 32.8 %collective-permute-start.6 = (f16[4,2,128,256]{3,2,1,0:T(8,128)(2,1)}, f16[4,2,128,256]{3,2,1,0:T(8,128)(2,1)}, u32[]{:S(2)}, u32[]{:S(2)}) collective-permute-start(f16[4,2,128,256]{3,2,1,0:T(8,128)(2,1)} %convert_element_type.172), channel_id=1, source_target_pairs={{0,2},{1,3},{2,0},{3,1},{4,6},{5,7},{6,4},{7,5},{8,10},{9,11},{10,... | collective-permute-start | bytes 1572872 | tf_op jit(solution)/shard_map/ppermute | solution.py:302
  46.3 24.7 %collective-permute-start.7 = (f16[4,2,128,256]{3,2,1,0:T(8,128)(2,1)}, f16[4,2,128,256]{3,2,1,0:T(8,128)(2,1)}, u32[]{:S(2)}, u32[]{:S(2)}) collective-permute-start(f16[4,2,128,256]{3,2,1,0:T(8,128)(2,1)} %convert_element_type.174), channel_id=1, source_target_pairs={{0,1},{1,2},{2,3},{3,0},{4,5},{5,6},{6,7},{7,4},{8,9},{9,10},{10,1... | collective-permute-start | bytes 1572872 | tf_op jit(solution)/shard_map/ppermute | solution.py:302
  53.5 7.7 %copy-start.8 = (f16[4,2,128,256]{3,2,1,0:T(8,128)(2,1)}, f16[4,2,128,256]{3,2,1,0:T(8,128)(2,1)S(1)}, u32[]{:S(2)}) copy-start(f16[4,2,128,256]{3,2,1,0:T(8,128)(2,1)S(1)} %collective-permute-done) | copy-start | bytes 1572868
  53.5 17.6 %collective-permute-start.8 = (f16[4,2,128,256]{3,2,1,0:T(8,128)(2,1)}, f16[4,2,128,256]{3,2,1,0:T(8,128)(2,1)}, u32[]{:S(2)}, u32[]{:S(2)}) collective-permute-start(f16[4,2,128,256]{3,2,1,0:T(8,128)(2,1)} %convert_element_type.176), channel_id=1, source_target_pairs={{0,3},{1,0},{2,1},{3,2},{4,7},{5,4},{6,5},{7,6},{8,11},{9,8},{10,9... | collective-permute-start | bytes 1572872 | tf_op jit(solution)/shard_map/ppermute | solution.py:302
  61.1 5.5 %copy-start.7 = (f32[4,2,128,256]{3,2,1,0:T(8,128)S(1)}, f32[4,2,128,256]{3,2,1,0:T(8,128)}, u32[]{:S(2)}) copy-start(f32[4,2,128,256]{3,2,1,0:T(8,128)} %beamform.11) | copy-start | bytes 3145732
  61.1 24.3 %copy-start.9 = (s32[1,64]{1,0:T(1,128)S(1)}, s32[1,64]{1,0:T(1,128)}, u32[]{:S(2)}) copy-start(s32[1,64]{1,0:T(1,128)} %param.16) | copy-start | bytes 772
  61.6 40.3 %copy-start.2 = (bf16[2,256,512]{2,1,0:T(8,128)(2,1)S(1)}, bf16[2,256,512]{2,1,0:T(8,128)(2,1)}, u32[]{:S(2)}) copy-start(bf16[2,256,512]{2,1,0:T(8,128)(2,1)} %constant.125.clone.left_even) | copy-start | bytes 1572868
  61.6 40.3 %copy-start.3 = (bf16[2,256,512]{2,1,0:T(8,128)(2,1)S(1)}, bf16[2,256,512]{2,1,0:T(8,128)(2,1)}, u32[]{:S(2)}) copy-start(bf16[2,256,512]{2,1,0:T(8,128)(2,1)} %constant.126.clone.left_odd) | copy-start | bytes 1572868
  61.6 40.3 %copy-start.4 = (bf16[2,256,512]{2,1,0:T(8,128)(2,1)S(1)}, bf16[2,256,512]{2,1,0:T(8,128)(2,1)}, u32[]{:S(2)}) copy-start(bf16[2,256,512]{2,1,0:T(8,128)(2,1)} %constant.127.clone.left_back) | copy-start | bytes 1572868
  61.7 40.4 %copy-start.5 = (bf16[2,512,256]{2,1,0:T(8,128)(2,1)S(1)}, bf16[2,512,256]{2,1,0:T(8,128)(2,1)}, u32[]{:S(2)}) copy-start(bf16[2,512,256]{2,1,0:T(8,128)(2,1)} %constant.128.clone.right) | copy-start | bytes 1572868
  61.7 40.4 %copy-start.6 = (f32[256,256]{1,0:T(8,128)S(1)}, f32[256,256]{1,0:T(8,128)}, u32[]{:S(2)}) copy-start(f32[256,256]{1,0:T(8,128)} %constant.130.clone.group) | copy-start | bytes 786436
  68.2 7.3 %collective-permute-start.3 = (f16[2,128,256]{2,1,0:T(8,128)(2,1)S(1)}, f16[2,128,256]{2,1,0:T(8,128)(2,1)S(1)}, u32[]{:S(2)}, u32[]{:S(2)}) collective-permute-start(f16[2,128,256]{2,1,0:T(8,128)(2,1)S(1)} %get-tuple-element.14), channel_id=1, source_target_pairs={{0,2},{1,3},{2,0},{3,1},{4,6},{5,7},{6,4},{7,5},{8,10},{9,11},{10,... | collective-permute-start | bytes 393224 | tf_op jit(solution)/shard_map/ppermute | solution.py:302
  68.3 7.2 %collective-permute-start.4 = (f16[2,128,256]{2,1,0:T(8,128)(2,1)S(1)}, f16[2,128,256]{2,1,0:T(8,128)(2,1)S(1)}, u32[]{:S(2)}, u32[]{:S(2)}) collective-permute-start(f16[2,128,256]{2,1,0:T(8,128)(2,1)S(1)} %get-tuple-element.16), channel_id=1, source_target_pairs={{0,1},{1,2},{2,3},{3,0},{4,5},{5,6},{6,7},{7,4},{8,9},{9,10},{10,1... | collective-permute-start | bytes 393224 | tf_op jit(solution)/shard_map/ppermute | solution.py:302
  68.9 6.6 %collective-permute-start.5 = (f16[2,128,256]{2,1,0:T(8,128)(2,1)S(1)}, f16[2,128,256]{2,1,0:T(8,128)(2,1)S(1)}, u32[]{:S(2)}, u32[]{:S(2)}) collective-permute-start(f16[2,128,256]{2,1,0:T(8,128)(2,1)S(1)} %get-tuple-element.15), channel_id=1, source_target_pairs={{0,3},{1,0},{2,1},{3,2},{4,7},{5,4},{6,5},{7,6},{8,11},{9,8},{10,9... | collective-permute-start | bytes 393224 | tf_op jit(solution)/shard_map/ppermute | solution.py:302
  72.8 8.2 %collective-permute-start.10 = (f16[2,128,256]{2,1,0:T(8,128)(2,1)S(1)}, f16[2,128,256]{2,1,0:T(8,128)(2,1)S(1)}, u32[]{:S(2)}, u32[]{:S(2)}) collective-permute-start(f16[2,128,256]{2,1,0:T(8,128)(2,1)S(1)} %get-tuple-element.19), channel_id=1, source_target_pairs={{0,4},{1,5},{2,6},{3,7},{4,8},{5,9},{6,10},{7,11},{8,12},{9,13},{1... | collective-permute-start | bytes 393224 | tf_op jit(solution)/shard_map/ppermute | solution.py:302
  72.8 8.1 %collective-permute-start.11 = (f16[2,128,256]{2,1,0:T(8,128)(2,1)S(1)}, f16[2,128,256]{2,1,0:T(8,128)(2,1)S(1)}, u32[]{:S(2)}, u32[]{:S(2)}) collective-permute-start(f16[2,128,256]{2,1,0:T(8,128)(2,1)S(1)} %get-tuple-element.18), channel_id=1, source_target_pairs={{0,12},{1,13},{2,14},{3,15},{4,0},{5,1},{6,2},{7,3},{8,4},{9,5},{1... | collective-permute-start | bytes 393224 | tf_op jit(solution)/shard_map/ppermute | solution.py:302
  75.5 5.5 %collective-permute-start.9 = (f16[2,128,256]{2,1,0:T(8,128)(2,1)S(1)}, f16[2,128,256]{2,1,0:T(8,128)(2,1)S(1)}, u32[]{:S(2)}, u32[]{:S(2)}) collective-permute-start(f16[2,128,256]{2,1,0:T(8,128)(2,1)S(1)} %get-tuple-element.17), channel_id=1, source_target_pairs={{0,8},{1,9},{2,10},{3,11},{4,12},{5,13},{6,14},{7,15},{8,0},{9,1},... | collective-permute-start | bytes 393224 | tf_op jit(solution)/shard_map/ppermute | solution.py:302
  77.5 23.4 %collective-permute-start.12 = (f16[2,128,256]{2,1,0:T(8,128)(2,1)S(1)}, f16[2,128,256]{2,1,0:T(8,128)(2,1)}, u32[]{:S(2)}, u32[]{:S(2)}) collective-permute-start(f16[2,128,256]{2,1,0:T(8,128)(2,1)S(1)} %get-tuple-element.10), channel_id=1, source_target_pairs={{0,1},{1,2},{2,3},{3,4},{4,5},{5,6},{6,7},{7,8},{8,9},{9,10},{10,1... | collective-permute-start | bytes 393224 | tf_op jit(solution)/shard_map/ppermute | solution.py:353
  83.0 17.9 %collective-permute-start.13 = (f16[2,128,256]{2,1,0:T(8,128)(2,1)}, f16[2,128,256]{2,1,0:T(8,128)(2,1)}, u32[]{:S(2)}, u32[]{:S(2)}) collective-permute-start(f16[2,128,256]{2,1,0:T(8,128)(2,1)} %get-tuple-element.12), channel_id=1, source_target_pairs={{0,1},{1,2},{2,3},{3,4},{4,5},{5,6},{6,7},{7,8},{8,9},{9,10},{10,1... | collective-permute-start | bytes 393224 | tf_op jit(solution)/shard_map/ppermute | solution.py:353
  96.4 4.5 %collective-permute-start.14 = (f16[2,16,256]{2,1,0:T(8,128)(2,1)S(1)}, f16[2,16,256]{2,1,0:T(8,128)(2,1)S(1)}, u32[]{:S(2)}, u32[]{:S(2)}) collective-permute-start(f16[2,16,256]{2,1,0:T(8,128)(2,1)S(1)} %slice.169), channel_id=1, source_target_pairs={{1,0},{2,1},{3,2},{4,3},{5,4},{6,5},{7,6},{8,7},{9,8},{10,9},{11,1... | collective-permute-start | bytes 49160 | tf_op jit(solution)/shard_map/ppermute | solution.py:354
  102.0 1.2 copy-start.1
  120.1 26.0 %all-to-all-start = ((f32[128,1,128]{2,1,0:T(1,128)}), f32[128,1,128]{2,1,0:T(1,128)S(1)}, u32[]{:S(2)}, u32[]{:S(2)}) async-start(f32[128,1,128]{2,1,0:T(1,128)} %bitcast.19), calls=%async_computation | async-start | bytes 131072 | tf_op jit(solution)/shard_map/all_to_all | solution.py:372

commit v2 on v1

--- a/solution.py
+++ b/solution.py
@@ -20,11 +20,9 @@
 GRID_SIDE = 4
 N_TM = 16
 LANES = 128
-BEAM_SCALE = 64.0
 
 F32 = jnp.float32
 BF16 = jnp.bfloat16
-WIRE = jnp.float16
 
 
 def split_table(table):
@@ -64,67 +62,175 @@
     ]
 
 
-def beam_body(blocks, gains, samples, out, table):
-    @pl.when(pl.program_id(0) == 0)
-    def build():
-        shape = (128, 256)
-        row = lax.broadcasted_iota(jnp.int32, shape, 0)
-        col = lax.broadcasted_iota(jnp.int32, shape, 1)
-        part = row // 64
-        imag_out = row // 32 % 2
-        slot = row % 32
-        chunk = jnp.where(slot < 16, 2 * slot, 2 * (slot - 16) + 1)
-        from_imag = col // 128
-        source = col % 128 // 4
-        antenna = col % 4
-        real = jnp.zeros(shape, F32)
-        imag = jnp.zeros(shape, F32)
-        for a in range(4):
-            real = jnp.where(antenna == a, gains[0, a], real)
-            imag = jnp.where(antenna == a, gains[1, a], imag)
-        cross = jnp.where(imag_out == 1, imag, -imag)
-        value = jnp.where(imag_out == from_imag, real, cross) * BEAM_SCALE
-        value = jnp.where(chunk == source, value, 0.0)
-        high = value.astype(BF16).astype(F32)
-        table[...] = jnp.where(part == 0, high, value - high).astype(BF16)
-
-    weights = table[...]
-    for pair in range(4):
-        columns = []
-        for group in (2 * pair, 2 * pair + 1):
-            rows = pl.ds(group * 128, 128)
-            columns.append(jnp.concatenate([samples[0, rows, :], samples[1, rows, :]], axis=0))
-        product = jnp.dot(
-            weights, jnp.concatenate(columns, axis=1), preferred_element_type=F32
+CODE_TOP = 32000.0
+HEADER = 16
+ROWS = 2 * 128 + HEADER
+
+
+def encode(real, imag):
+    top = jnp.maximum(jnp.max(jnp.abs(real), axis=0, keepdims=True), jnp.max(jnp.abs(imag), axis=0, keepdims=True))
+    top = jnp.broadcast_to(jnp.max(top, axis=1, keepdims=True), (8, SIDE))
+    level = jnp.floor(4.0 * jnp.log2(CODE_TOP / jnp.maximum(top, 1e-30)))
+    scale = jnp.exp2(0.25 * level)[0:1]
+    whole = lambda value: jnp.round(value).astype(jnp.int32).astype(jnp.int16)
+    header = jnp.concatenate([level, level], axis=0)
+    return whole(real * scale), whole(imag * scale), whole(header)
+
+
+def decode(block_ref, *lead):
+    level = block_ref[(*lead, pl.ds(2 * 128, HEADER), slice(None))].astype(jnp.int32).astype(F32)
+    step = jnp.exp2(-0.25 * level)[0:1]
+    parts = []
+    for comp in (0, 1):
+        code = block_ref[(*lead, pl.ds(comp * 128, 128), slice(None))]
+        parts.append(code.astype(jnp.int32).astype(F32) * step)
+    return parts
+
+
+def beam_body(messages, index, gains, samples, *refs):
+    outs = refs[: len(messages)]
+    table, buffer, arrived = refs[len(messages) :]
+    down_at = index[0] // GRID_SIDE
+    across_at = index[0] % GRID_SIDE
+
+    def copy_of(slot, half, step, j):
+        if half == 0:
+            rows, cols = down_at + step, across_at + j
+        else:
+            rows, cols = down_at + j, across_at + step
+        block = (rows % GRID_SIDE * GRID_SIDE + cols % GRID_SIDE) * 2 + half
+        first = pl.multiple_of(block * 1024, 1024)
+        return pltpu.make_async_copy(
+            samples.at[:, pl.ds(first, 1024), :], buffer.at[slot], arrived.at[slot]
         )
-        both = product[:64] + product[64:]
-        for which in (0, 1):
-            group = 2 * pair + which
-            lanes = slice(which * 128, which * 128 + 128)
-            rows = pl.ds(group * 16, 16)
+
+    copies = []
+    for number, (half, step) in enumerate(messages):
+        copies.append([copy_of(number * 4 + j, half, step, j) for j in range(4)])
+        for copy in copies[-1]:
+            copy.start()
+
+    shape = (128, 256)
+    row = lax.broadcasted_iota(jnp.int32, shape, 0)
+    col = lax.broadcasted_iota(jnp.int32, shape, 1)
+    part = row // 64
+    imag_out = row // 32 % 2
+    slot = row % 32
+    chunk = jnp.where(slot < 16, 2 * slot, 2 * (slot - 16) + 1)
+    from_imag = col // 128
+    source = col % 128 // 4
+    antenna = col % 4
+    real = jnp.zeros(shape, F32)
+    imag = jnp.zeros(shape, F32)
+    for a in range(4):
+        real = jnp.where(antenna == a, gains[0, 0, index[0] * 4 + a], real)
+        imag = jnp.where(antenna == a, gains[1, 0, index[0] * 4 + a], imag)
+    cross = jnp.where(imag_out == 1, imag, -imag)
+    value = jnp.where(imag_out == from_imag, real, cross)
+    value = jnp.where(chunk == source, value, 0.0)
+    high = value.astype(BF16).astype(F32)
+    table[...] = jnp.where(part == 0, high, value - high).astype(BF16)
+
+    for number in range(len(messages)):
+        for j in range(4):
+            copies[number][j].wait()
+            weights = table[...]
+            at = number * 4 + j
+            columns = []
+            for group in range(8):
+                rows = pl.ds(group * 128, 128)
+                columns.append(
+                    jnp.concatenate([buffer[at, 0, rows, :], buffer[at, 1, rows, :]], axis=0)
+                )
+            product = jnp.dot(
+                weights, jnp.concatenate(columns, axis=1), preferred_element_type=F32
+            )
+            both = product[:64] + product[64:]
+            planes = []
             for comp in (0, 1):
-                base = comp * 32
-                out[0, comp, rows, 0:128] = both[base : base + 16, lanes]
-                out[0, comp, rows, 128:256] = both[base + 16 : base + 32, lanes]
-
-
-def beamform(blocks, gains, samples):
-    grid_spec = pltpu.PrefetchScalarGridSpec(
-        num_scalar_prefetch=1,
-        grid=(4,),
+                lanes = lambda base: jnp.concatenate(
+                    [both[base : base + 16, g * 128 : g * 128 + 128] for g in range(8)], axis=0
+                )
+                planes.append(
+                    jnp.concatenate([lanes(comp * 32), lanes(comp * 32 + 16)], axis=1)
+                )
+            out = outs[number]
+            out[j, 0:128], out[j, 128:256], out[j, 256:272] = encode(*planes)
+
+
+def beamform(index, gains, samples, messages):
+    count = len(messages)
+    return pl.pallas_call(
+        lambda *refs: beam_body(messages, *refs),
         in_specs=[
             pl.BlockSpec(memory_space=pltpu.SMEM),
-            pl.BlockSpec((2, 1024, LANES), lambda i, blocks: (0, blocks[i], 0)),
+            pl.BlockSpec(memory_space=pltpu.SMEM),
+            pl.BlockSpec(memory_space=pl.ANY),
         ],
-        out_specs=pl.BlockSpec((1, 2, 128, SIDE), lambda i, blocks: (i, 0, 0, 0)),
-        scratch_shapes=[pltpu.VMEM((128, 256), BF16)],
-    )
+        out_shape=tuple(jax.ShapeDtypeStruct((4, ROWS, SIDE), jnp.int16) for _ in messages),
+        scratch_shapes=[
+            pltpu.VMEM((128, 256), BF16),
+            pltpu.VMEM((count * 4, 2, 1024, LANES), BF16),
+            pltpu.SemaphoreType.DMA((count * 4,)),
+        ],
+        compiler_params=pltpu.CompilerParams(vmem_limit_bytes=(count * 2 + 16) * 1024 * 1024),
+        name="beamform",
+    )(index, gains, samples)
+
+
+def middle_body(order, *refs):
+    parts, outs = refs[:4], refs[4:]
+    for second, out in zip(order, outs):
+        total = decode(parts[0], second)
+        for part in parts[1:]:
+            more = decode(part, second)
+            total = [total[0] + more[0], total[1] + more[1]]
+        if second:
+            out[0:128], out[128:256], out[256:272] = encode(*total)
+        else:
+            out[0], out[1] = total
+
+
+def middle(parts, order):
     return pl.pallas_call(
-        beam_body,
-        grid_spec=grid_spec,
-        out_shape=jax.ShapeDtypeStruct((4, 2, 128, SIDE), F32),
-        name="beamform",
-    )(blocks, gains, samples)
+        lambda *refs: middle_body(order, *refs),
+        out_shape=tuple(
+            jax.ShapeDtypeStruct((ROWS, SIDE), jnp.int16)
+            if second
+            else jax.ShapeDtypeStruct((2, 128, SIDE), F32)
+            for second in order
+        ),
+        compiler_params=pltpu.CompilerParams(vmem_limit_bytes=16 * 1024 * 1024),
+        name="middle",
+    )(*parts)
+
+
+def last_body(*refs):
+    parts, (own, ahead, behind) = refs[:8], refs[8:]
+    for half in (0, 1):
+        mine = parts[half * 4]
+        total = [mine[0], mine[1]]
+        for part in parts[half * 4 + 1 : half * 4 + 4]:
+            more = decode(part)
+            total = [total[0] + more[0], total[1] + more[1]]
+        rows = pl.ds(half * 128, 128)
+        own[0, rows], own[1, rows] = total
+        ahead[half, 0:128], ahead[half, 128:256], ahead[half, 256:272] = encode(*total)
+        if half == 0:
+            behind[0], behind[1] = total[0][0:16], total[1][0:16]
+
+
+def last(parts):
+    return pl.pallas_call(
+        last_body,
+        out_shape=(
+            jax.ShapeDtypeStruct((2, SIDE, SIDE), F32),
+            jax.ShapeDtypeStruct((2, ROWS, SIDE), jnp.int16),
+            jax.ShapeDtypeStruct((2, 16, SIDE), F32),
+        ),
+        compiler_params=pltpu.CompilerParams(vmem_limit_bytes=16 * 1024 * 1024),
+        name="last",
+    )(*parts)
 
 
 def response_body(offset, phase, out):
@@ -210,10 +316,11 @@
     row = lax.broadcasted_iota(jnp.int32, (16, SIDE), 0)
     col = lax.broadcasted_iota(jnp.int32, (16, SIDE), 1)
     wrapped = row * SIDE + col < offset[0]
+    earlier = [decode(before_ref, 0), decode(before_ref, 1)]
     before = []
     for comp in (0, 1):
-        head = jnp.where(wrapped, after_ref[comp], before_ref[comp, 0:16, :])
-        before.append(jnp.concatenate([head, before_ref[comp, 16:, :]], axis=0))
+        head = jnp.where(wrapped, after_ref[comp], earlier[0][comp][0:16])
+        before.append(jnp.concatenate([head, earlier[0][comp][16:], earlier[1][comp]], axis=0))
     back = []
     for parity, table in ((0, left_even), (1, left_odd)):
         sign = 1.0 if parity == 0 else -1.0
@@ -227,7 +334,7 @@
         real, imag = from_right(real, imag, right, -1)
         real, imag = times(real, imag, cos, sin)
         back.append(from_left(left_even if parity == 0 else left_back, real, imag, -1))
-    scale = 1.0 / (NFFT * BEAM_SCALE)
+    scale = 1.0 / NFFT
     real = (back[0][0] - back[1][0]) * scale
     imag = (back[0][1] - back[1][1]) * scale
     out_ref[0] = real.astype(BF16)
@@ -302,59 +409,36 @@
     return lax.ppermute(value, "tm", steps(down, across))
 
 
-def sum_of(parts):
-    total = parts[0].astype(F32)
-    for part in parts[1:]:
-        total = total + part.astype(F32)
-    return total
-
-
 def on_device(voltages, antenna_gains, chirp_phase, offsets, flags, sample_phase_bins):
     tables = make_tables()
-    my_index = lax.axis_index("tm")
-    down_at, across_at = my_index // GRID_SIDE, my_index % GRID_SIDE
+    index = lax.axis_index("tm").astype(jnp.int32).reshape(1)
     samples = (
         voltages.reshape(2, 4, TIME_CHUNKS, LANES)
         .transpose(0, 2, 1, 3)
         .reshape(2, TIME_CHUNKS * 4, LANES)
     )
-    gains = lax.dynamic_slice_in_dim(antenna_gains[:, :, 0], my_index * 4, 4, 1)
-    around = jnp.arange(GRID_SIDE, dtype=jnp.int32)
-
+    gains = antenna_gains.transpose(0, 2, 1)
     order = (2, 1, 3, 0)
-    partial = []
+
+    def first_send(half, step, value):
+        return send(value, step, 0) if half == 0 else send(value, 0, step)
+
+    def second_send(half, step, value):
+        return send(value, 0, step) if half == 0 else send(value, step, 0)
+
+    got = [[], []]
+    for messages in (((0, 2), (1, 2)), ((0, 1), (1, 1), (0, 3), (1, 3)), ((0, 0), (1, 0))):
+        made = beamform(index, gains, samples, messages)
+        for (half, step), value in zip(messages, made):
+            got[half].append(first_send(half, step, value) if step else value)
+    landed = [[], []]
     for half in (0, 1):
-        got = []
-        for first in order:
-            if half == 0:
-                rows, cols = (down_at + first) % GRID_SIDE, (across_at + around) % GRID_SIDE
-            else:
-                rows, cols = (down_at + around) % GRID_SIDE, (across_at + first) % GRID_SIDE
-            blocks = ((rows * GRID_SIDE + cols) * 2 + half).astype(jnp.int32)
-            message = beamform(blocks, gains, samples)
-            if first:
-                wire = message.astype(WIRE)
-                message = send(wire, first, 0) if half == 0 else send(wire, 0, first)
-            got.append(message)
-        partial.append(got)
-    beam = []
-    for half in (0, 1):
-        got = []
-        for second in order:
-            part = sum_of([message[second] for message in partial[half]])
-            if second:
-                wire = part.astype(WIRE)
-                part = send(wire, 0, second) if half == 0 else send(wire, second, 0)
-            got.append(part)
-        beam.append(sum_of(got))
-    shards = N_TM
-    ahead = [(s, s + 1) for s in range(shards - 1)]
-    behind = [(s + 1, s) for s in range(shards - 1)]
-    before = [lax.ppermute(part.astype(WIRE), "tm", ahead) for part in beam]
-    after = lax.ppermute(beam[0][:, :16].astype(WIRE), "tm", behind)
-    own = jnp.concatenate(beam, axis=1)
-    before = jnp.concatenate(before, axis=1).astype(F32)
-    after = after.astype(F32)
+        made = middle(got[half], order)
+        for step, value in zip(order, made):
+            landed[half].append(second_send(half, step, value) if step else value)
+    own, ahead, behind = last([landed[half][i] for half in (0, 1) for i in (3, 0, 1, 2)])
+    before = lax.ppermute(ahead, "tm", [(s, s + 1) for s in range(N_TM - 1)])
+    after = lax.ppermute(behind, "tm", [(s + 1, s) for s in range(N_TM - 1)])
 
     phase = jnp.transpose(chirp_phase.reshape(SIDE, 2 * SIDE), (1, 0))
     phase = phase.reshape(SIDE, 2, SIDE).transpose(1, 0, 2)

time: 149 us -> 132 us (0.89)
  other arithmetic: 27.5 us -> 4.42 us
  Pallas kernels: 58.5 us -> 37.8 us
  local copies, waits for them, and re-layouts: 8.34 us -> 26.1 us
  waiting for transfers between devices: 10.4 us -> 27.1 us
  starting transfers between devices: 41.1 us -> 34 us
    ppermute x12, waiting for transfers between devices: 0.06 us -> 20.8 us  [send(): return lax.ppermute(value, 'tm', steps(down, across))]
    pallas_call x8 -> x6, Pallas kernels: 38.2 us -> 17.8 us  [the longest x3 15.2 us: beamform(): pl.pallas_call(lambda *refs: beam_body(messages, *refs), in_specs=[pl.Blo...]
    convert_element_type x10 -> x0, other arithmetic: 16.8 us -> none  [the longest x6 11.8 us: on_device(): wire = message.astype(WIRE)]
    unnamed x22 -> x32, local copies, waits for them, and re-layouts: 2.97 us -> 13 us
    add x5 -> x0, other arithmetic: 4.9 us -> none  [the longest x2 3.32 us: sum_of(): total = total + part.astype(F32)]
    all_to_all x1, starting transfers between devices: 16.4 us -> 12.6 us  [on_device(): lax.all_to_all(pieces.reshape(channels * N_TM, LANES), ('chan', 'tm'), 0,...]
    ppermute x3 -> x2, starting transfers between devices: 7.19 us -> 3.39 us  [the longest x1 2.11 us: on_device(): before = lax.ppermute(ahead, 'tm', [(s, s + 1) for s in range(N_TM - 1)])]
    reshape x2, local copies, waits for them, and re-layouts: 0.28 us -> 3.98 us  [on_device(): phase = jnp.transpose(chirp_phase.reshape(SIDE, 2 * SIDE), (1, 0))]
  transfers between devices with their start and end apart: 16 -> 15, of which waited for: 2 -> 7; matrix products, arithmetic and copies ran while one was open for 19% -> 13% of each run, Pallas kernels for 25% -> 10%
where the time goes in v2:
time: 132 us; the launch traced here: 131 us
  Pallas kernels  37.8 us (29%)
  starting transfers between devices  34 us (26%)
  waiting for transfers between devices  27.1 us (21%)
  local copies, waits for them, and re-layouts  26.1 us (20%)
  other arithmetic  4.42 us (3%)
  between operations  1.51 us (1%)
    ppermute x12, waiting for transfers between devices, send(): return lax.ppermute(value, 'tm', steps(down, across))  20.8 us
    ppermute x12, starting transfers between devices, send(): return lax.ppermute(value, 'tm', steps(down, across))  18 us
    pallas_call x1, Pallas kernels, filter_and_fold(): pl.pallas_call(main_body, in_specs=[pl.BlockSpec(memory_space=pltpu.SMEM)...  15.9 us
    pallas_call x3, Pallas kernels, beamform(): pl.pallas_call(lambda *refs: beam_body(messages, *refs), in_specs=[pl.Blo...  15.2 us
    unnamed x32, local copies, waits for them, and re-layouts  13 us
    all_to_all x1, starting transfers between devices, on_device(): lax.all_to_all(pieces.reshape(channels * N_TM, LANES), ('chan', 'tm'), 0,...  12.6 us
    all_to_all x1, waiting for transfers between devices, on_device(): lax.all_to_all(pieces.reshape(channels * N_TM, LANES), ('chan', 'tm'), 0,...  6.32 us
    pallas_call x1, Pallas kernels, make_response(): pl.pallas_call(response_body, in_specs=[pl.BlockSpec(memory_space=pltpu.S...  4.07 us
  transfers between devices with their start and end apart: 15, of which 7 were waited for; matrix products, arithmetic and copies ran while one was open for 13% of the time, Pallas kernels for 10%

profile of v2, /device:TPU:1, one launch (start us, length us, event | category | flops | bytes accessed | tf_op | source)
XLA Modules:
  0.0 130.9 jit_solution(4618605361094782320)
XLA Ops:
  0.6 5.8 %copy-done = bf16[2,4,1,1048576]{3,1,2,0:T(4,128)(2,1)S(1)} copy-done((bf16[2,4,1,1048576]{3,1,2,0:T(4,128)(2,1)S(1)}, bf16[2,4,1,1048576]{3,1,2,0:T(4,128)(2,1)}, u32[]{:S(2)}) %copy-start) | copy-done | bytes 16777240
  6.4 0.7 copy-done.12
  7.1 7.3 %beamform.4 = (s16[4,272,256]{2,1,0:T(8,128)(2,1)S(1)}, s16[4,272,256]{2,1,0:T(8,128)(2,1)S(1)}, s16[4,272,256]{2,1,0:T(8,128)(2,1)S(1)}, s16[4,272,256]{2,1,0:T(8,128)(2,1)S(1)}) custom-call(s32[1]{0:T(128)} %bitcast.refs_0_, f32[2,1,64]{2,1,0:T(1,128)S(1)} %bitcast.24, bf16[2,32768,128]{2,1,0:T(8,128)(2,1)S(1)} %bitcast.21), custom_call_target="tpu_custom_call" | custom-call | tf_op jit(solution)/shard_map/beamform/pallas_call | solution.py:163
  14.4 2.1 %collective-permute-start.7 = (s16[4,272,256]{2,1,0:T(8,128)(2,1)S(1)}, s16[4,272,256]{2,1,0:T(8,128)(2,1)S(1)}, u32[]{:S(2)}, u32[]{:S(2)}) collective-permute-start(s16[4,272,256]{2,1,0:T(8,128)(2,1)S(1)} %get-tuple-element.35), channel_id=1, source_target_pairs={{0,1},{1,2},{2,3},{3,0},{4,5},{5,6},{6,7},{7,4},{8,9},{9,10},{10,1... | collective-permute-start | bytes 1671176 | tf_op jit(solution)/shard_map/ppermute | solution.py:409
  16.5 1.4 %collective-permute-start.8 = (s16[4,272,256]{2,1,0:T(8,128)(2,1)S(1)}, s16[4,272,256]{2,1,0:T(8,128)(2,1)S(1)}, u32[]{:S(2)}, u32[]{:S(2)}) collective-permute-start(s16[4,272,256]{2,1,0:T(8,128)(2,1)S(1)} %get-tuple-element.36), channel_id=1, source_target_pairs={{0,3},{1,0},{2,1},{3,2},{4,7},{5,4},{6,5},{7,6},{8,11},{9,8},{10,9... | collective-permute-start | bytes 1671176 | tf_op jit(solution)/shard_map/ppermute | solution.py:409
  17.8 4.0 %beamform.3 = (s16[4,272,256]{2,1,0:T(8,128)(2,1)S(1)}, s16[4,272,256]{2,1,0:T(8,128)(2,1)S(1)}) custom-call(s32[1]{0:T(128)} %bitcast.refs_0_, f32[2,1,64]{2,1,0:T(1,128)S(1)} %bitcast.25, bf16[2,32768,128]{2,1,0:T(8,128)(2,1)S(1)} %bitcast.22), custom_call_target="tpu_custom_call" | custom-call | tf_op jit(solution)/shard_map/beamform/pallas_call | solution.py:163
  21.9 1.7 %collective-permute-start.6 = (s16[4,272,256]{2,1,0:T(8,128)(2,1)S(1)}, s16[4,272,256]{2,1,0:T(8,128)(2,1)S(1)}, u32[]{:S(2)}, u32[]{:S(2)}) collective-permute-start(s16[4,272,256]{2,1,0:T(8,128)(2,1)S(1)} %get-tuple-element.34), channel_id=1, source_target_pairs={{0,2},{1,3},{2,0},{3,1},{4,6},{5,7},{6,4},{7,5},{8,10},{9,11},{10,... | collective-permute-start | bytes 1671176 | tf_op jit(solution)/shard_map/ppermute | solution.py:409
  23.6 1.3 collective-permute-start.1
  24.9 1.4 %collective-permute-start.2 = (s16[4,272,256]{2,1,0:T(8,128)(2,1)S(1)}, s16[4,272,256]{2,1,0:T(8,128)(2,1)S(1)}, u32[]{:S(2)}, u32[]{:S(2)}) collective-permute-start(s16[4,272,256]{2,1,0:T(8,128)(2,1)S(1)} %get-tuple-element.28), channel_id=1, source_target_pairs={{0,12},{1,13},{2,14},{3,15},{4,0},{5,1},{6,2},{7,3},{8,4},{9,5},{1... | collective-permute-start | bytes 1671176 | tf_op jit(solution)/shard_map/ppermute | solution.py:409
  26.3 3.3 %collective-permute-done.7.refs_1_ = s16[4,272,256]{2,1,0:T(8,128)(2,1)S(1)} collective-permute-done((s16[4,272,256]{2,1,0:T(8,128)(2,1)S(1)}, s16[4,272,256]{2,1,0:T(8,128)(2,1)S(1)}, u32[]{:S(2)}, u32[]{:S(2)}) %collective-permute-start.7) | collective-permute-done | bytes 557088 | tf_op jit(solution)/shard_map/ppermute | solution.py:409
  29.7 3.2 %collective-permute-start = (s16[4,272,256]{2,1,0:T(8,128)(2,1)S(1)}, s16[4,272,256]{2,1,0:T(8,128)(2,1)S(1)}, u32[]{:S(2)}, u32[]{:S(2)}) collective-permute-start(s16[4,272,256]{2,1,0:T(8,128)(2,1)S(1)} %get-tuple-element.26), channel_id=1, source_target_pairs={{0,8},{1,9},{2,10},{3,11},{4,12},{5,13},{6,14},{7,15},{8,0},{9,1},... | collective-permute-start | bytes 1671176 | tf_op jit(solution)/shard_map/ppermute | solution.py:409
  32.9 4.0 %beamform.5 = (s16[4,272,256]{2,1,0:T(8,128)(2,1)S(1)}, s16[4,272,256]{2,1,0:T(8,128)(2,1)S(1)}) custom-call(s32[1]{0:T(128)} %bitcast.refs_0_, f32[2,1,64]{2,1,0:T(1,128)S(1)} %bitcast.26, bf16[2,32768,128]{2,1,0:T(8,128)(2,1)S(1)} %bitcast.23), custom_call_target="tpu_custom_call" | custom-call | tf_op jit(solution)/shard_map/beamform/pallas_call | solution.py:163
  36.9 6.0 %collective-permute-done.6.refs_0_ = s16[4,272,256]{2,1,0:T(8,128)(2,1)S(1)} collective-permute-done((s16[4,272,256]{2,1,0:T(8,128)(2,1)S(1)}, s16[4,272,256]{2,1,0:T(8,128)(2,1)S(1)}, u32[]{:S(2)}, u32[]{:S(2)}) %collective-permute-start.6) | collective-permute-done | bytes 557088 | tf_op jit(solution)/shard_map/ppermute | solution.py:409
  42.9 0.8 middle.3
  43.7 1.4 %collective-permute-start.10 = (s16[272,256]{1,0:T(8,128)(2,1)S(1)}, s16[272,256]{1,0:T(8,128)(2,1)S(1)}, u32[]{:S(2)}, u32[]{:S(2)}) collective-permute-start(s16[272,256]{1,0:T(8,128)(2,1)S(1)} %get-tuple-element.40), channel_id=1, source_target_pairs={{0,4},{1,5},{2,6},{3,7},{4,8},{5,9},{6,10},{7,11},{8,12},{9,13},{1... | collective-permute-start | bytes 417800 | tf_op jit(solution)/shard_map/ppermute | solution.py:409
  45.0 1.5 %collective-permute-start.11 = (s16[272,256]{1,0:T(8,128)(2,1)S(1)}, s16[272,256]{1,0:T(8,128)(2,1)S(1)}, u32[]{:S(2)}, u32[]{:S(2)}) collective-permute-start(s16[272,256]{1,0:T(8,128)(2,1)S(1)} %get-tuple-element.41), channel_id=1, source_target_pairs={{0,12},{1,13},{2,14},{3,15},{4,0},{5,1},{6,2},{7,3},{8,4},{9,5},{1... | collective-permute-start | bytes 417800 | tf_op jit(solution)/shard_map/ppermute | solution.py:409
  46.5 1.6 %collective-permute-start.9 = (s16[272,256]{1,0:T(8,128)(2,1)S(1)}, s16[272,256]{1,0:T(8,128)(2,1)S(1)}, u32[]{:S(2)}, u32[]{:S(2)}) collective-permute-start(s16[272,256]{1,0:T(8,128)(2,1)S(1)} %get-tuple-element.39), channel_id=1, source_target_pairs={{0,8},{1,9},{2,10},{3,11},{4,12},{5,13},{6,14},{7,15},{8,0},{9,1},... | collective-permute-start | bytes 417800 | tf_op jit(solution)/shard_map/ppermute | solution.py:409
  48.1 2.5 %collective-permute-done.refs_0_ = s16[4,272,256]{2,1,0:T(8,128)(2,1)S(1)} collective-permute-done((s16[4,272,256]{2,1,0:T(8,128)(2,1)S(1)}, s16[4,272,256]{2,1,0:T(8,128)(2,1)S(1)}, u32[]{:S(2)}, u32[]{:S(2)}) %collective-permute-start) | collective-permute-done | bytes 557088 | tf_op jit(solution)/shard_map/ppermute | solution.py:409
  50.6 0.8 middle.2
  51.4 1.5 %collective-permute-start.3 = (s16[272,256]{1,0:T(8,128)(2,1)S(1)}, s16[272,256]{1,0:T(8,128)(2,1)S(1)}, u32[]{:S(2)}, u32[]{:S(2)}) collective-permute-start(s16[272,256]{1,0:T(8,128)(2,1)S(1)} %get-tuple-element.31), channel_id=1, source_target_pairs={{0,2},{1,3},{2,0},{3,1},{4,6},{5,7},{6,4},{7,5},{8,10},{9,11},{10,... | collective-permute-start | bytes 417800 | tf_op jit(solution)/shard_map/ppermute | solution.py:409
  52.9 4.1 %collective-permute-done.10.refs_6_ = s16[272,256]{1,0:T(8,128)(2,1)S(1)} collective-permute-done((s16[272,256]{1,0:T(8,128)(2,1)S(1)}, s16[272,256]{1,0:T(8,128)(2,1)S(1)}, u32[]{:S(2)}, u32[]{:S(2)}) %collective-permute-start.10) | collective-permute-done | bytes 139296 | tf_op jit(solution)/shard_map/ppermute | solution.py:409
  57.0 0.9 collective-permute-start.5
  57.9 0.8 collective-permute-done.4.refs_2_
  58.6 4.0 %collective-permute-done.5.refs_3_ = s16[272,256]{1,0:T(8,128)(2,1)S(1)} collective-permute-done((s16[272,256]{1,0:T(8,128)(2,1)S(1)}, s16[272,256]{1,0:T(8,128)(2,1)S(1)}, u32[]{:S(2)}, u32[]{:S(2)}) %collective-permute-start.5) | collective-permute-done | bytes 139296 | tf_op jit(solution)/shard_map/ppermute | solution.py:409
  62.6 1.1 last.1
  63.8 0.8 copy-done.8
  64.6 2.1 %collective-permute-start.12 = (s16[2,272,256]{2,1,0:T(8,128)(2,1)}, s16[2,272,256]{2,1,0:T(8,128)(2,1)}, u32[]{:S(2)}, u32[]{:S(2)}) collective-permute-start(s16[2,272,256]{2,1,0:T(8,128)(2,1)} %get-tuple-element.43), channel_id=1, source_target_pairs={{0,1},{1,2},{2,3},{3,4},{4,5},{5,6},{6,7},{7,8},{8,9},{9,10},{10,1... | collective-permute-start | bytes 835592 | tf_op jit(solution)/shard_map/ppermute | solution.py:440
  66.7 1.3 collective-permute-start.13
  69.1 3.7 %reduce.6 = f32[131072]{0:T(1024)} reduce(f32[1,131072]{1,0:T(1,128)} %param.14, f32[]{:T(128)} %broadcast.6), dimensions={0}, to_apply=%param.14.reduce_sub_computation.3 | reduce | bytes 1048580 | tf_op args[2]
  72.9 1.9 %reshape.48 = f32[256,512]{1,0:T(8,128)} reshape(f32[131072]{0:T(1024)} %reduce.6) | data formatting | bytes 1048576 | tf_op jit(solution)/shard_map/reshape | solution.py:443
  74.8 2.1 %copy.32 = f32[256,512]{0,1:T(8,128)} copy(f32[256,512]{1,0:T(8,128)} %reshape.48) | data formatting | bytes 1048576 | tf_op jit(solution)/shard_map/reshape | solution.py:443
  76.9 2.2 %reshape.49 = f32[256,2,256]{2,1,0:T(2,128)} reshape(f32[512,256]{1,0:T(8,128)} %bitcast.29) | data formatting | bytes 1048576 | tf_op jit(solution)/shard_map/reshape | solution.py:444
  79.0 1.9 %copy.37 = f32[256,2,256]{2,0,1:T(8,128)} copy(f32[256,2,256]{2,1,0:T(2,128)} %reshape.49) | data formatting | bytes 1048576 | tf_op jit(solution)/shard_map/reshape | solution.py:444
  80.9 1.0 reshape.50.bins_ref
  82.1 4.1 %response.1 = f32[2,2,256,256]{3,2,1,0:T(8,128)} custom-call(s32[1]{0:T(128)S(6)} %copy.38.offset, f32[2,256,256]{2,1,0:T(8,128)} %bitcast.28), custom_call_target="tpu_custom_call" | custom-call | tf_op jit(solution)/shard_map/response/pallas_call | solution.py:249
  86.4 1.2 copy-done.2
  87.6 1.0 copy-done.9
  88.6 0.9 copy-done.10
  89.6 15.9 %filter_and_fold.1 = (bf16[2,256,256]{2,1,0:T(8,128)(2,1)S(1)}, f32[256,128]{1,0:T(8,128)S(1)}, f32[16,128]{1,0:T(8,128)S(1)}) custom-call(s32[1]{0:T(128)S(6)} %copy.38.offset, f32[2,256,256]{2,1,0:T(8,128)S(1)} %copy-done.9, s16[2,272,256]{2,1,0:T(8,128)(2,1)} %collective-permute-done.12.before_ref, f32[2,16,256]{2,1,0:T(8,128)S(1)} %collective-permute-done.13.after_ref, ...), custom_call_target="tpu_custom_call" | custom-call | tf_op jit(solution)/shard_map/filter_and_fold/pallas_call | solution.py:394
  105.5 0.7 copy-done.11
  106.2 0.6 copy-done.13
  106.9 0.6 broadcast_in_dim.21
  107.5 12.6 %all-to-all-start = ((f32[128,1,128]{2,1,0:T(1,128)}), f32[128,1,128]{2,1,0:T(1,128)S(1)}, u32[]{:S(2)}, u32[]{:S(2)}) async-start(f32[128,1,128]{2,1,0:T(1,128)} %bitcast.14), calls=%async_computation | async-start | bytes 131072 | tf_op jit(solution)/shard_map/all_to_all | solution.py:456
  120.1 1.7 %reshape.51 = bf16[2,1,65536]{2,0,1:T(2,128)(2,1)} reshape(bf16[2,256,256]{2,1,0:T(8,128)(2,1)} %copy-done.11) | data formatting | bytes 524288 | tf_op jit(solution)/shard_map/reshape | solution.py:452
  121.8 0.9 slice.4
  122.7 0.6 copy.35
  123.3 6.3 %all-to-all-done = f32[128,1,128]{2,1,0:T(1,128)S(1)} async-done(((f32[128,1,128]{2,1,0:T(1,128)}), f32[128,1,128]{2,1,0:T(1,128)S(1)}, u32[]{:S(2)}, u32[]{:S(2)}) %all-to-all-start) | async-done | bytes 65568 | tf_op jit(solution)/shard_map/all_to_all | solution.py:456
  130.2 0.7 reduce_sum.19
  (38 shorter events, 1.4 us)
Async XLA Ops:
  0.6 5.8 %copy-start = (bf16[2,4,1,1048576]{3,1,2,0:T(4,128)(2,1)S(1)}, bf16[2,4,1,1048576]{3,1,2,0:T(4,128)(2,1)}, u32[]{:S(2)}) copy-start(bf16[2,4,1,1048576]{3,1,2,0:T(4,128)(2,1)} %param.12) | copy-start | bytes 50331652
  6.4 0.7 copy-start.12
  7.1 10.8 %copy-start.1 = (bf16[2,4,1,1048576]{3,1,2,0:T(4,128)(2,1)S(1)}, bf16[2,4,1,1048576]{3,1,2,0:T(4,128)(2,1)}, u32[]{:S(2)}) copy-start(bf16[2,4,1,1048576]{3,1,2,0:T(4,128)(2,1)} %param.12) | copy-start | bytes 50331652
  14.4 15.3 %collective-permute-start.7 = (s16[4,272,256]{2,1,0:T(8,128)(2,1)S(1)}, s16[4,272,256]{2,1,0:T(8,128)(2,1)S(1)}, u32[]{:S(2)}, u32[]{:S(2)}) collective-permute-start(s16[4,272,256]{2,1,0:T(8,128)(2,1)S(1)} %get-tuple-element.35), channel_id=1, source_target_pairs={{0,1},{1,2},{2,3},{3,0},{4,5},{5,6},{6,7},{7,4},{8,9},{9,10},{10,1... | collective-permute-start | bytes 1671176 | tf_op jit(solution)/shard_map/ppermute | solution.py:409
  16.5 51.5 %copy-start.14 = (s32[1,64]{1,0:T(1,128)S(1)}, s32[1,64]{1,0:T(1,128)}, u32[]{:S(2)}) copy-start(s32[1,64]{1,0:T(1,128)} %param.16) | copy-start | bytes 772
  16.5 20.4 %collective-permute-start.8 = (s16[4,272,256]{2,1,0:T(8,128)(2,1)S(1)}, s16[4,272,256]{2,1,0:T(8,128)(2,1)S(1)}, u32[]{:S(2)}, u32[]{:S(2)}) collective-permute-start(s16[4,272,256]{2,1,0:T(8,128)(2,1)S(1)} %get-tuple-element.36), channel_id=1, source_target_pairs={{0,3},{1,0},{2,1},{3,2},{4,7},{5,4},{6,5},{7,6},{8,11},{9,8},{10,9... | collective-permute-start | bytes 1671176 | tf_op jit(solution)/shard_map/ppermute | solution.py:409
  21.8 64.5 %copy-start.3 = (f32[2,2,256,256]{3,2,1,0:T(8,128)S(1)}, f32[2,2,256,256]{3,2,1,0:T(8,128)}, u32[]{:S(2)}) copy-start(f32[2,2,256,256]{3,2,1,0:T(8,128)} %constant.33.clone.twist) | copy-start | bytes 3145732
  21.8 64.5 %copy-start.4 = (bf16[2,256,512]{2,1,0:T(8,128)(2,1)S(1)}, bf16[2,256,512]{2,1,0:T(8,128)(2,1)}, u32[]{:S(2)}) copy-start(bf16[2,256,512]{2,1,0:T(8,128)(2,1)} %constant.29.clone.left_even) | copy-start | bytes 1572868
  21.8 64.5 %copy-start.5 = (bf16[2,256,512]{2,1,0:T(8,128)(2,1)S(1)}, bf16[2,256,512]{2,1,0:T(8,128)(2,1)}, u32[]{:S(2)}) copy-start(bf16[2,256,512]{2,1,0:T(8,128)(2,1)} %constant.30.clone.left_odd) | copy-start | bytes 1572868
  21.8 64.5 %copy-start.6 = (bf16[2,256,512]{2,1,0:T(8,128)(2,1)S(1)}, bf16[2,256,512]{2,1,0:T(8,128)(2,1)}, u32[]{:S(2)}) copy-start(bf16[2,256,512]{2,1,0:T(8,128)(2,1)} %constant.31.clone.left_back) | copy-start | bytes 1572868
  21.9 64.5 %copy-start.7 = (bf16[2,512,256]{2,1,0:T(8,128)(2,1)S(1)}, bf16[2,512,256]{2,1,0:T(8,128)(2,1)}, u32[]{:S(2)}) copy-start(bf16[2,512,256]{2,1,0:T(8,128)(2,1)} %constant.32.clone.right) | copy-start | bytes 1572868
  21.9 21.0 %collective-permute-start.6 = (s16[4,272,256]{2,1,0:T(8,128)(2,1)S(1)}, s16[4,272,256]{2,1,0:T(8,128)(2,1)S(1)}, u32[]{:S(2)}, u32[]{:S(2)}) collective-permute-start(s16[4,272,256]{2,1,0:T(8,128)(2,1)S(1)} %get-tuple-element.34), channel_id=1, source_target_pairs={{0,2},{1,3},{2,0},{3,1},{4,6},{5,7},{6,4},{7,5},{8,10},{9,11},{10,... | collective-permute-start | bytes 1671176 | tf_op jit(solution)/shard_map/ppermute | solution.py:409
  23.6 23.0 %collective-permute-start.1 = (s16[4,272,256]{2,1,0:T(8,128)(2,1)S(1)}, s16[4,272,256]{2,1,0:T(8,128)(2,1)S(1)}, u32[]{:S(2)}, u32[]{:S(2)}) collective-permute-start(s16[4,272,256]{2,1,0:T(8,128)(2,1)S(1)} %get-tuple-element.27), channel_id=1, source_target_pairs={{0,4},{1,5},{2,6},{3,7},{4,8},{5,9},{6,10},{7,11},{8,12},{9,13},{1... | collective-permute-start | bytes 1671176 | tf_op jit(solution)/shard_map/ppermute | solution.py:409
  24.9 23.2 %collective-permute-start.2 = (s16[4,272,256]{2,1,0:T(8,128)(2,1)S(1)}, s16[4,272,256]{2,1,0:T(8,128)(2,1)S(1)}, u32[]{:S(2)}, u32[]{:S(2)}) collective-permute-start(s16[4,272,256]{2,1,0:T(8,128)(2,1)S(1)} %get-tuple-element.28), channel_id=1, source_target_pairs={{0,12},{1,13},{2,14},{3,15},{4,0},{5,1},{6,2},{7,3},{8,4},{9,5},{1... | collective-permute-start | bytes 1671176 | tf_op jit(solution)/shard_map/ppermute | solution.py:409
  29.7 21.0 %collective-permute-start = (s16[4,272,256]{2,1,0:T(8,128)(2,1)S(1)}, s16[4,272,256]{2,1,0:T(8,128)(2,1)S(1)}, u32[]{:S(2)}, u32[]{:S(2)}) collective-permute-start(s16[4,272,256]{2,1,0:T(8,128)(2,1)S(1)} %get-tuple-element.26), channel_id=1, source_target_pairs={{0,8},{1,9},{2,10},{3,11},{4,12},{5,13},{6,14},{7,15},{8,0},{9,1},... | collective-permute-start | bytes 1671176 | tf_op jit(solution)/shard_map/ppermute | solution.py:409
  43.7 13.3 %collective-permute-start.10 = (s16[272,256]{1,0:T(8,128)(2,1)S(1)}, s16[272,256]{1,0:T(8,128)(2,1)S(1)}, u32[]{:S(2)}, u32[]{:S(2)}) collective-permute-start(s16[272,256]{1,0:T(8,128)(2,1)S(1)} %get-tuple-element.40), channel_id=1, source_target_pairs={{0,4},{1,5},{2,6},{3,7},{4,8},{5,9},{6,10},{7,11},{8,12},{9,13},{1... | collective-permute-start | bytes 417800 | tf_op jit(solution)/shard_map/ppermute | solution.py:409
  45.0 12.8 %collective-permute-start.11 = (s16[272,256]{1,0:T(8,128)(2,1)S(1)}, s16[272,256]{1,0:T(8,128)(2,1)S(1)}, u32[]{:S(2)}, u32[]{:S(2)}) collective-permute-start(s16[272,256]{1,0:T(8,128)(2,1)S(1)} %get-tuple-element.41), channel_id=1, source_target_pairs={{0,12},{1,13},{2,14},{3,15},{4,0},{5,1},{6,2},{7,3},{8,4},{9,5},{1... | collective-permute-start | bytes 417800 | tf_op jit(solution)/shard_map/ppermute | solution.py:409
  46.5 11.3 %collective-permute-start.9 = (s16[272,256]{1,0:T(8,128)(2,1)S(1)}, s16[272,256]{1,0:T(8,128)(2,1)S(1)}, u32[]{:S(2)}, u32[]{:S(2)}) collective-permute-start(s16[272,256]{1,0:T(8,128)(2,1)S(1)} %get-tuple-element.39), channel_id=1, source_target_pairs={{0,8},{1,9},{2,10},{3,11},{4,12},{5,13},{6,14},{7,15},{8,0},{9,1},... | collective-permute-start | bytes 417800 | tf_op jit(solution)/shard_map/ppermute | solution.py:409
  51.4 6.5 %collective-permute-start.3 = (s16[272,256]{1,0:T(8,128)(2,1)S(1)}, s16[272,256]{1,0:T(8,128)(2,1)S(1)}, u32[]{:S(2)}, u32[]{:S(2)}) collective-permute-start(s16[272,256]{1,0:T(8,128)(2,1)S(1)} %get-tuple-element.31), channel_id=1, source_target_pairs={{0,2},{1,3},{2,0},{3,1},{4,6},{5,7},{6,4},{7,5},{8,10},{9,11},{10,... | collective-permute-start | bytes 417800 | tf_op jit(solution)/shard_map/ppermute | solution.py:409
  52.9 5.7 %collective-permute-start.4 = (s16[272,256]{1,0:T(8,128)(2,1)S(1)}, s16[272,256]{1,0:T(8,128)(2,1)S(1)}, u32[]{:S(2)}, u32[]{:S(2)}) collective-permute-start(s16[272,256]{1,0:T(8,128)(2,1)S(1)} %get-tuple-element.32), channel_id=1, source_target_pairs={{0,1},{1,2},{2,3},{3,0},{4,5},{5,6},{6,7},{7,4},{8,9},{9,10},{10,1... | collective-permute-start | bytes 417800 | tf_op jit(solution)/shard_map/ppermute | solution.py:409
  57.0 5.6 %collective-permute-start.5 = (s16[272,256]{1,0:T(8,128)(2,1)S(1)}, s16[272,256]{1,0:T(8,128)(2,1)S(1)}, u32[]{:S(2)}, u32[]{:S(2)}) collective-permute-start(s16[272,256]{1,0:T(8,128)(2,1)S(1)} %get-tuple-element.33), channel_id=1, source_target_pairs={{0,3},{1,0},{2,1},{3,2},{4,7},{5,4},{6,5},{7,6},{8,11},{9,8},{10,9... | collective-permute-start | bytes 417800 | tf_op jit(solution)/shard_map/ppermute | solution.py:409
  63.8 0.8 copy-start.8
  64.6 21.6 %collective-permute-start.12 = (s16[2,272,256]{2,1,0:T(8,128)(2,1)}, s16[2,272,256]{2,1,0:T(8,128)(2,1)}, u32[]{:S(2)}, u32[]{:S(2)}) collective-permute-start(s16[2,272,256]{2,1,0:T(8,128)(2,1)} %get-tuple-element.43), channel_id=1, source_target_pairs={{0,1},{1,2},{2,3},{3,4},{4,5},{5,6},{6,7},{7,8},{8,9},{9,10},{10,1... | collective-permute-start | bytes 835592 | tf_op jit(solution)/shard_map/ppermute | solution.py:440
  66.7 19.5 %collective-permute-start.13 = (f32[2,16,256]{2,1,0:T(8,128)S(1)}, f32[2,16,256]{2,1,0:T(8,128)S(1)}, u32[]{:S(2)}, u32[]{:S(2)}) collective-permute-start(f32[2,16,256]{2,1,0:T(8,128)S(1)} %get-tuple-element.44), channel_id=1, source_target_pairs={{1,0},{2,1},{3,2},{4,3},{5,4},{6,5},{7,6},{8,7},{9,8},{10,9},{11,1... | collective-permute-start | bytes 98312 | tf_op jit(solution)/shard_map/ppermute | solution.py:441
  86.3 1.2 copy-start.2
  87.6 1.0 copy-start.9
  88.6 0.9 copy-start.10
  105.5 0.7 copy-start.11
  106.2 0.6 copy-start.13
  107.5 22.2 %all-to-all-start = ((f32[128,1,128]{2,1,0:T(1,128)}), f32[128,1,128]{2,1,0:T(1,128)S(1)}, u32[]{:S(2)}, u32[]{:S(2)}) async-start(f32[128,1,128]{2,1,0:T(1,128)} %bitcast.14), calls=%async_computation | async-start | bytes 131072 | tf_op jit(solution)/shard_map/all_to_all | solution.py:456

commit v3 on v2

--- a/solution.py
+++ b/solution.py
@@ -15,11 +15,15 @@
 OFFSET_BOUND = 4096
 SKW = 1024
 BINS = 2048
+LOW_BINS = 64
+HIGH_BINS = BINS // LOW_BINS
 SK_WIDTH = 0.05
 EPSILON = 1e-06
 GRID_SIDE = 4
 N_TM = 16
+CHANNELS = 8
 LANES = 128
+QUARTER = 128
 
 F32 = jnp.float32
 BF16 = jnp.bfloat16
@@ -36,22 +40,33 @@
     return np.cos(angle), np.sin(angle)
 
 
+def real_form(cos, sin):
+    return split_table(np.block([[cos, sin], [-sin, cos]]))
+
+
 def make_tables():
-    index = np.arange(SIDE, dtype=np.int64)
-    even = circle(index[:, None] * index[None, :], SIDE)
-    odd = circle((2 * index[:, None] + 1) * index[None, :], 2 * SIDE)
-    odd_back = (odd[0].T, odd[1].T)
-    left_even = split_table(np.concatenate(even, axis=1))
-    left_odd = split_table(np.concatenate(odd, axis=1))
-    left_back = split_table(np.concatenate(odd_back, axis=1))
-    right = split_table(np.concatenate(even, axis=0))
-    twist = []
-    for parity in (0, 1):
-        row = 2 * index[:, None] + parity
-        twist.append(np.stack(circle(row * index[None, :], NFFT)))
-    twist = np.stack(twist).astype(np.float32)
-    group = (index[:, None] // 4 == index[None, :] // 4).astype(np.float32)
-    return left_even, left_odd, left_back, right, twist, group
+    index = np.arange(QUARTER, dtype=np.int64)
+    rows_forward, rows_back, twist = [], [], []
+    lanes = np.arange(SIDE, dtype=np.int64)
+    for r in range(4):
+        cos, sin = circle((4 * index[:, None] + r) * index[None, :], 2 * SIDE)
+        rows_forward.append(real_form(cos, sin))
+        rows_back.append(real_form(cos.T, -sin.T))
+        twist.append(np.stack(circle((4 * index[:, None] + r) * lanes[None, :], NFFT)))
+    columns_forward, columns_back = [], []
+    for s in range(2):
+        cos, sin = circle(index[:, None] * (2 * index[None, :] + s), SIDE)
+        columns_forward.append(real_form(cos, -sin))
+        columns_back.append(real_form(cos.T, sin.T))
+    group = (lanes[:, None] // 4 == lanes[None, :] // 4).astype(np.float32)
+    return (
+        np.stack(rows_forward),
+        np.stack(columns_forward),
+        np.stack(columns_back),
+        np.stack(rows_back),
+        np.stack(twist).astype(np.float32),
+        group,
+    )
 
 
 def steps(down, across):
@@ -87,11 +102,13 @@
     return parts
 
 
-def beam_body(messages, index, gains, samples, *refs):
-    outs = refs[: len(messages)]
-    table, buffer, arrived = refs[len(messages) :]
-    down_at = index[0] // GRID_SIDE
-    across_at = index[0] % GRID_SIDE
+def beam_body(messages, gains, samples, *refs):
+    table, buffer, arrived = refs[-3:]
+    outs = refs[-4 - len(messages) : -4]
+    refs[-4][...] = jnp.zeros((8, LANES), F32)
+    index = lax.axis_index("tm").astype(jnp.int32)
+    down_at = index // GRID_SIDE
+    across_at = index % GRID_SIDE
 
     def copy_of(slot, half, step, j):
         if half == 0:
@@ -120,11 +137,14 @@
     from_imag = col // 128
     source = col % 128 // 4
     antenna = col % 4
+    antennas = lax.broadcasted_iota(jnp.int32, (1, 64), 1)
     real = jnp.zeros(shape, F32)
     imag = jnp.zeros(shape, F32)
     for a in range(4):
-        real = jnp.where(antenna == a, gains[0, 0, index[0] * 4 + a], real)
-        imag = jnp.where(antenna == a, gains[1, 0, index[0] * 4 + a], imag)
+        own = antennas == index * 4 + a
+        pick = lambda comp: jnp.sum(jnp.where(own, gains[comp], 0.0), axis=1, keepdims=True)
+        real = jnp.where(antenna == a, pick(0), real)
+        imag = jnp.where(antenna == a, pick(1), imag)
     cross = jnp.where(imag_out == 1, imag, -imag)
     value = jnp.where(imag_out == from_imag, real, cross)
     value = jnp.where(chunk == source, value, 0.0)
@@ -158,24 +178,25 @@
             out[j, 0:128], out[j, 128:256], out[j, 256:272] = encode(*planes)
 
 
-def beamform(index, gains, samples, messages):
+def beamform(gains, samples, messages, ready=()):
     count = len(messages)
     return pl.pallas_call(
         lambda *refs: beam_body(messages, *refs),
         in_specs=[
-            pl.BlockSpec(memory_space=pltpu.SMEM),
-            pl.BlockSpec(memory_space=pltpu.SMEM),
-            pl.BlockSpec(memory_space=pl.ANY),
-        ],
-        out_shape=tuple(jax.ShapeDtypeStruct((4, ROWS, SIDE), jnp.int16) for _ in messages),
+            pl.BlockSpec(memory_space=pltpu.VMEM),
+            pl.BlockSpec(memory_space=pltpu.HBM),
+        ]
+        + [pl.BlockSpec(memory_space=pltpu.VMEM)] * len(ready),
+        out_shape=tuple(jax.ShapeDtypeStruct((4, ROWS, SIDE), jnp.int16) for _ in messages)
+        + (jax.ShapeDtypeStruct((8, LANES), F32),),
         scratch_shapes=[
             pltpu.VMEM((128, 256), BF16),
             pltpu.VMEM((count * 4, 2, 1024, LANES), BF16),
             pltpu.SemaphoreType.DMA((count * 4,)),
         ],
-        compiler_params=pltpu.CompilerParams(vmem_limit_bytes=(count * 2 + 16) * 1024 * 1024),
+        compiler_params=pltpu.CompilerParams(vmem_limit_bytes=50 * 1024 * 1024),
         name="beamform",
-    )(index, gains, samples)
+    )(gains, samples, *ready)
 
 
 def middle_body(order, *refs):
@@ -233,23 +254,31 @@
     )(*parts)
 
 
-def response_body(offset, phase, out):
-    row = lax.broadcasted_iota(jnp.int32, (SIDE, SIDE), 0)
-    col = lax.broadcasted_iota(jnp.int32, (SIDE, SIDE), 1)
-    for parity in (0, 1):
-        bin_index = 2 * row + parity + 512 * col
-        turns = jnp.bitwise_and(bin_index * offset[0], NFFT - 1)
-        turns = jnp.where(turns >= HALF, turns - NFFT, turns)
-        angle = phase[parity] + turns.astype(F32) * (2.0 * math.pi / NFFT)
-        out[parity, 0] = jnp.cos(angle)
-        out[parity, 1] = jnp.sin(angle)
+def response_body(offset, phase, out, turned):
+    row = lax.broadcasted_iota(jnp.int32, (QUARTER, LANES), 0)
+    col = lax.broadcasted_iota(jnp.int32, (QUARTER, LANES), 1)
+    for s in (0, 1):
+        for part in range(4):
+            block = phase[pl.ds(part + 4 * s, LANES, stride=8), :]
+            turned[s, pl.ds(part * LANES, LANES), :] = jnp.transpose(block)
+        for r in range(4):
+            bin_index = 4 * row + r + 512 * (2 * col + s)
+            turns = jnp.bitwise_and(bin_index * offset[0], NFFT - 1)
+            turns = jnp.where(turns >= HALF, turns - NFFT, turns)
+            angle = turned[s, pl.ds(r, QUARTER, stride=4), :]
+            angle = angle + turns.astype(F32) * (2.0 * math.pi / NFFT)
+            rows = pl.ds(r * QUARTER, QUARTER)
+            out[s, 0, rows, :] = jnp.cos(angle)
+            out[s, 1, rows, :] = jnp.sin(angle)
 
 
 def make_response(offset, phase):
     return pl.pallas_call(
         response_body,
         in_specs=[pl.BlockSpec(memory_space=pltpu.SMEM), pl.BlockSpec(memory_space=pltpu.VMEM)],
-        out_shape=jax.ShapeDtypeStruct((2, 2, SIDE, SIDE), F32),
+        out_shape=jax.ShapeDtypeStruct((2, 2, 2 * SIDE, LANES), F32),
+        scratch_shapes=[pltpu.VMEM((2, 2 * SIDE, LANES), F32)],
+        compiler_params=pltpu.CompilerParams(vmem_limit_bytes=16 * 1024 * 1024),
         name="response",
     )(offset, phase)
 
@@ -259,32 +288,44 @@
     return high, (value - high.astype(F32)).astype(BF16)
 
 
-def from_left(table, real, imag, sign):
-    crossed = (imag, -real) if sign > 0 else (-imag, real)
-    top = jnp.concatenate([real, imag], axis=1)
-    bottom = jnp.concatenate(crossed, axis=1)
-    high, low = halves(jnp.concatenate([top, bottom], axis=0))
+def from_left(table, value):
+    high, low = halves(value)
     first, second = table[0], table[1]
-    product = (
+    return (
         jnp.dot(first, high, preferred_element_type=F32)
         + jnp.dot(first, low, preferred_element_type=F32)
         + jnp.dot(second, high, preferred_element_type=F32)
     )
-    return product[:, :SIDE], product[:, SIDE:]
-
-
-def from_right(real, imag, table, sign):
-    crossed = (imag, -real) if sign > 0 else (-imag, real)
-    left = jnp.concatenate([real, imag], axis=0)
-    right = jnp.concatenate(crossed, axis=0)
-    high, low = halves(jnp.concatenate([left, right], axis=1))
+
+
+def from_right(value, table):
+    high, low = halves(value)
     first, second = table[0], table[1]
-    product = (
+    return (
         jnp.dot(high, first, preferred_element_type=F32)
         + jnp.dot(low, first, preferred_element_type=F32)
         + jnp.dot(high, second, preferred_element_type=F32)
     )
-    return product[:SIDE], product[SIDE:]
+
+
+def quarter_turn(pair, count):
+    real, imag = pair
+    return ((real, imag), (-imag, real), (-real, -imag), (imag, -real))[count % 4]
+
+
+def add(first, second):
+    return first[0] + second[0], first[1] + second[1]
+
+
+def four_point(parts, sign):
+    even = add(parts[0], parts[2]), add(parts[1], parts[3])
+    odd = add(parts[0], quarter_turn(parts[2], 2)), add(parts[1], quarter_turn(parts[3], 2))
+    return (
+        add(even[0], even[1]),
+        add(odd[0], quarter_turn(odd[1], sign)),
+        add(even[0], quarter_turn(even[1], 2)),
+        add(odd[0], quarter_turn(odd[1], -sign)),
+    )
 
 
 def times(real, imag, other_real, other_imag):
@@ -297,12 +338,12 @@
     before_ref,
     after_ref,
     response,
-    keep_ref,
+    flags_ref,
     bins_ref,
-    left_even,
-    left_odd,
-    left_back,
-    right,
+    rows_forward,
+    columns_forward,
+    columns_back,
+    rows_back,
     twist,
     group,
     out_ref,
@@ -311,6 +352,7 @@
     high_ref,
     low_ref,
     value_ref,
+    total_ref,
 ):
     own = [own_ref[0], own_ref[1]]
     row = lax.broadcasted_iota(jnp.int32, (16, SIDE), 0)
@@ -320,23 +362,38 @@
     before = []
     for comp in (0, 1):
         head = jnp.where(wrapped, after_ref[comp], earlier[0][comp][0:16])
-        before.append(jnp.concatenate([head, earlier[0][comp][16:], earlier[1][comp]], axis=0))
+        before.append(jnp.concatenate([head, earlier[0][comp][16:]], axis=0))
+    quarters = [
+        tuple(before),
+        tuple(earlier[1]),
+        (own_ref[0, 0:QUARTER, :], own_ref[1, 0:QUARTER, :]),
+        (own_ref[0, QUARTER:, :], own_ref[1, QUARTER:, :]),
+    ]
+    sums, differences = [], []
+    for r, pair in enumerate(four_point(quarters, -1)):
+        product = from_left(rows_forward[r], jnp.concatenate(pair, axis=0))
+        real, imag = times(product[:QUARTER], product[QUARTER:], twist[r, 0], -twist[r, 1])
+        ends = [(part[:, :LANES], part[:, LANES:]) for part in (real, imag)]
+        sums.append(jnp.concatenate([first + second for first, second in ends], axis=1))
+        differences.append(jnp.concatenate([first - second for first, second in ends], axis=1))
     back = []
-    for parity, table in ((0, left_even), (1, left_odd)):
-        sign = 1.0 if parity == 0 else -1.0
-        real, imag = from_left(
-            table, before[0] + sign * own[0], before[1] + sign * own[1], 1
-        )
-        cos, sin = twist[parity, 0], twist[parity, 1]
-        real, imag = times(real, imag, cos, -sin)
-        real, imag = from_right(real, imag, right, 1)
-        real, imag = times(real, imag, response[parity, 0], response[parity, 1])
-        real, imag = from_right(real, imag, right, -1)
-        real, imag = times(real, imag, cos, sin)
-        back.append(from_left(left_even if parity == 0 else left_back, real, imag, -1))
+    for s, inputs in enumerate((sums, differences)):
+        product = from_right(jnp.concatenate(inputs, axis=0), columns_forward[s])
+        pair = times(product[:, :LANES], product[:, LANES:], response[s, 0], response[s, 1])
+        back.append(from_right(jnp.concatenate(pair, axis=1), columns_back[s]))
+    ends = back[0] + back[1], back[0] - back[1]
+    restored = []
+    for r in range(4):
+        rows = slice(r * QUARTER, r * QUARTER + QUARTER)
+        real = jnp.concatenate([end[rows, :LANES] for end in ends], axis=1)
+        imag = jnp.concatenate([end[rows, LANES:] for end in ends], axis=1)
+        pair = times(real, imag, twist[r, 0], twist[r, 1])
+        product = from_left(rows_back[r], jnp.concatenate(pair, axis=0))
+        restored.append((product[:QUARTER], product[QUARTER:]))
+    wanted = four_point(restored, 1)[2:]
     scale = 1.0 / NFFT
-    real = (back[0][0] - back[1][0]) * scale
-    imag = (back[0][1] - back[1][1]) * scale
+    real = jnp.concatenate([wanted[0][0], wanted[1][0]], axis=0) * scale
+    imag = jnp.concatenate([wanted[0][1], wanted[1][1]], axis=0) * scale
     out_ref[0] = real.astype(BF16)
     out_ref[1] = imag.astype(BF16)
 
@@ -351,33 +408,42 @@
     kurtosis = (
         (SKW + 1.0) / (SKW - 1.0) * (SKW * second_sum / (first_sum * first_sum + EPSILON) - 1.0)
     )
-    weight = keep_ref[...] / (1.0 + ((kurtosis - 1.0) / SK_WIDTH) ** 2)
-    weight_ref[...] = weight
+    at_row = lax.broadcasted_iota(jnp.int32, (SIDE, 64), 0) // 4
+    at_lane = lax.broadcasted_iota(jnp.int32, (SIDE, 64), 1)
+    kept = jnp.where(at_row == at_lane, (1 - flags_ref[...]).astype(F32), 0.0)
+    weight = jnp.sum(kept, axis=1, keepdims=True) / (1.0 + ((kurtosis - 1.0) / SK_WIDTH) ** 2)
+    row = lax.broadcasted_iota(jnp.int32, (SIDE, LANES), 0)
+    col = lax.broadcasted_iota(jnp.int32, (SIDE, LANES), 1)
+    weight_ref[...] = jnp.sum(jnp.where(row == 4 * col, weight, 0.0), axis=0, keepdims=True)
     value_ref[...] = (
         jnp.concatenate([weight, weight], axis=1) * power
     ).astype(BF16).astype(F32)
 
-    bins = bins_ref[...]
-    high_ref[...] = (bins // LANES).astype(F32)
-    low_ref[...] = (bins % LANES).astype(F32)
-
-    per_step = 8
-    high_rows = lax.broadcasted_iota(jnp.int32, (16, SIDE), 0).astype(F32).astype(BF16)
-    low_rows = lax.broadcasted_iota(jnp.int32, (LANES, SIDE), 0).astype(F32).astype(BF16)
+    for side in (0, 1):
+        bins = bins_ref[pl.ds(side, SIDE, stride=2), :]
+        lanes = slice(side * LANES, side * LANES + LANES)
+        high_ref[:, lanes] = (bins // LOW_BINS).astype(F32)
+        low_ref[:, lanes] = (bins % LOW_BINS).astype(F32)
+
+    per_step = 32
+    rows = lax.broadcasted_iota(jnp.int32, (LOW_BINS, SIDE), 0).astype(F32).astype(BF16)
     one, zero = jnp.ones((), BF16), jnp.zeros((), BF16)
 
     def fold(step, total):
         start = pl.multiple_of(step * per_step, per_step)
-        high_block = high_ref[pl.ds(start, per_step), :]
-        low_block = low_ref[pl.ds(start, per_step), :]
-        value_block = value_ref[pl.ds(start, per_step), :]
+        blocks = [
+            ref[pl.ds(start, per_step), :] for ref in (high_ref, low_ref, value_ref)
+        ]
         spreads, marks = [], []
         for r in range(per_step):
-            high = jnp.broadcast_to(high_block[r : r + 1], (16, SIDE)).astype(BF16)
-            value = jnp.broadcast_to(value_block[r : r + 1], (16, SIDE)).astype(BF16)
-            spreads.append(jnp.where(high == high_rows, value, zero))
-            low = jnp.broadcast_to(low_block[r : r + 1], (LANES, SIDE)).astype(BF16)
-            marks.append(jnp.where(low == low_rows, one, zero))
+            high, low, value = [
+                jnp.broadcast_to(block[r : r + 1], (16, SIDE)).astype(BF16) for block in blocks
+            ]
+            high = jnp.concatenate([high] * (HIGH_BINS // 16), axis=0)
+            value = jnp.concatenate([value] * (HIGH_BINS // 16), axis=0)
+            low = jnp.concatenate([low] * (LOW_BINS // 16), axis=0)
+            spreads.append(jnp.where(high == rows[:HIGH_BINS], value, zero))
+            marks.append(jnp.where(low == rows, one, zero))
         return total + lax.dot_general(
             jnp.concatenate(spreads, axis=1),
             jnp.concatenate(marks, axis=1),
@@ -385,24 +451,30 @@
             preferred_element_type=F32,
         )
 
-    total = lax.fori_loop(0, SIDE // per_step, fold, jnp.zeros((16, LANES), F32))
-    profile_ref[...] = total * (BINS / (HALF * N_TM))
-
-
-def filter_and_fold(offset, own, before, after, response, keep, bins, tables):
+    total = lax.fori_loop(0, SIDE // per_step, fold, jnp.zeros((HIGH_BINS, LOW_BINS), F32))
+    total = total * (BINS / (HALF * N_TM))
+    total_ref[...] = jnp.concatenate([total, jnp.zeros_like(total)], axis=1)
+    pair = [total_ref[pl.ds(side, N_TM, stride=2), :][:, :LOW_BINS] for side in (0, 1)]
+    own = jnp.concatenate(pair, axis=1)
+    for channel in range(CHANNELS):
+        profile_ref[pl.ds(channel * N_TM, N_TM), :] = own
+
+
+def filter_and_fold(offset, own, before, after, response, flags, bins, tables):
     vmem = pl.BlockSpec(memory_space=pltpu.VMEM)
     return pl.pallas_call(
         main_body,
         in_specs=[pl.BlockSpec(memory_space=pltpu.SMEM)] + [vmem] * (6 + len(tables)),
         out_shape=(
             jax.ShapeDtypeStruct((2, SIDE, SIDE), BF16),
-            jax.ShapeDtypeStruct((SIDE, LANES), F32),
-            jax.ShapeDtypeStruct((16, LANES), F32),
+            jax.ShapeDtypeStruct((1, LANES), F32),
+            jax.ShapeDtypeStruct((CHANNELS * N_TM, LANES), F32),
         ),
-        scratch_shapes=[pltpu.VMEM((SIDE, SIDE), F32)] * 3,
+        scratch_shapes=[pltpu.VMEM((SIDE, SIDE), F32)] * 3
+        + [pltpu.VMEM((HIGH_BINS, LANES), F32)],
         compiler_params=pltpu.CompilerParams(vmem_limit_bytes=48 * 1024 * 1024),
         name="filter_and_fold",
-    )(offset, own, before, after, response, keep, bins, *tables)
+    )(offset, own, before, after, response, flags, bins, *tables)
 
 
 def send(value, down, across):
@@ -411,7 +483,6 @@
 
 def on_device(voltages, antenna_gains, chirp_phase, offsets, flags, sample_phase_bins):
     tables = make_tables()
-    index = lax.axis_index("tm").astype(jnp.int32).reshape(1)
     samples = (
         voltages.reshape(2, 4, TIME_CHUNKS, LANES)
         .transpose(0, 2, 1, 3)
@@ -426,11 +497,15 @@
     def second_send(half, step, value):
         return send(value, 0, step) if half == 0 else send(value, step, 0)
 
+    response = make_response(offsets, chirp_phase.reshape(8 * LANES, LANES))
     got = [[], []]
+    ready = ()
     for messages in (((0, 2), (1, 2)), ((0, 1), (1, 1), (0, 3), (1, 3)), ((0, 0), (1, 0))):
-        made = beamform(index, gains, samples, messages)
+        made = beamform(gains, samples, messages, ready)
+        ready = (made[-1],)
         for (half, step), value in zip(messages, made):
             got[half].append(first_send(half, step, value) if step else value)
+    got, response = lax.optimization_barrier((got, response))
     landed = [[], []]
     for half in (0, 1):
         made = middle(got[half], order)
@@ -440,22 +515,14 @@
     before = lax.ppermute(ahead, "tm", [(s, s + 1) for s in range(N_TM - 1)])
     after = lax.ppermute(behind, "tm", [(s + 1, s) for s in range(N_TM - 1)])
 
-    phase = jnp.transpose(chirp_phase.reshape(SIDE, 2 * SIDE), (1, 0))
-    phase = phase.reshape(SIDE, 2, SIDE).transpose(1, 0, 2)
-    response = make_response(offsets, phase)
-    keep = jnp.broadcast_to((1 - flags).astype(F32).reshape(64, 1, 1), (64, 4, LANES))
-    keep = keep.reshape(SIDE, LANES)
-    bins = sample_phase_bins.reshape(SIDE, SIDE)
+    bins = sample_phase_bins.reshape(512, LANES)
     filtered, weight, partial_profile = filter_and_fold(
-        offsets, own, before, after, response, keep, bins, tables
+        offsets, own, before, after, response, flags, bins, tables
     )
     dedispersed = filtered.reshape(2, 1, HALF)
-    sk_weight = weight.reshape(64, 4, LANES)[:, 0, 0].reshape(1, 64)
-    channels = lax.axis_size("chan")
-    pieces = jnp.broadcast_to(partial_profile[None], (channels, N_TM, LANES))
-    arrived = lax.all_to_all(
-        pieces.reshape(channels * N_TM, LANES), ("chan", "tm"), 0, 0, tiled=True
-    ).reshape(channels, N_TM, LANES)
+    sk_weight = weight[:, :64]
+    arrived = lax.all_to_all(partial_profile, ("chan", "tm"), 0, 0, tiled=True)
+    arrived = arrived.reshape(CHANNELS, N_TM, LANES)
     by_channel = jnp.sum(arrived, axis=1)
     profile = lax.dynamic_slice_in_dim(by_channel, lax.axis_index("chan"), 1, 0)
     band_profile = jnp.sum(by_channel, axis=0)

time: 132 us -> 107 us (0.81)
  local copies, waits for them, and re-layouts: 26.1 us -> 2.02 us
  starting transfers between devices: 34 us -> 45.5 us
  Pallas kernels: 37.8 us -> 28.4 us
  other arithmetic: 4.42 us -> 0.67 us
    unnamed x32 -> x18, local copies, waits for them, and re-layouts: 13 us -> 0.73 us
    all_to_all x1, starting transfers between devices: 12.6 us -> 24.1 us  [on_device(): arrived = lax.all_to_all(partial_profile, ('chan', 'tm'), 0, 0, tiled=True)]
    reshape x5 -> x0, local copies, waits for them, and re-layouts: 9.04 us -> none  [the longest x2 4.03 us: on_device(): phase = phase.reshape(SIDE, 2, SIDE).transpose(1, 0, 2)]
    pallas_call x1, Pallas kernels: 15.9 us -> 8.77 us  [filter_and_fold(): pl.pallas_call(main_body, in_specs=[pl.BlockSpec(memory_space=pltpu.SMEM)...]
    ppermute x12, waiting for transfers between devices: 20.8 us -> 16.1 us  [send(): return lax.ppermute(value, 'tm', steps(down, across))]
    unnamed x1 -> x0, other arithmetic: 3.74 us -> none
    ppermute x1, waiting for transfers between devices: 0.01 us -> 3.36 us  [on_device(): after = lax.ppermute(behind, 'tm', [(s + 1, s) for s in range(N_TM - 1)])]
    all_to_all x1, waiting for transfers between devices: 6.32 us -> 8.79 us  [on_device(): arrived = lax.all_to_all(partial_profile, ('chan', 'tm'), 0, 0, tiled=True)]
  transfers between devices with their start and end apart: 15 -> 15, of which waited for: 7 -> 8; matrix products, arithmetic and copies ran while one was open for 13% -> 1% of each run, Pallas kernels for 10% -> 7%
where the time goes in v3:
time: 107 us; the launch traced here: 106 us
  starting transfers between devices  45.5 us (43%)
  Pallas kernels  28.4 us (27%)
  waiting for transfers between devices  28.3 us (26%)
  local copies, waits for them, and re-layouts  2.02 us (2%)
  between operations  1.52 us (1%)
    all_to_all x1, starting transfers between devices, on_device(): arrived = lax.all_to_all(partial_profile, ('chan', 'tm'), 0, 0, tiled=True)  24.1 us
    ppermute x12, starting transfers between devices, send(): return lax.ppermute(value, 'tm', steps(down, across))  17.6 us
    ppermute x12, waiting for transfers between devices, send(): return lax.ppermute(value, 'tm', steps(down, across))  16.1 us
    pallas_call x3, Pallas kernels, beamform(): pl.pallas_call(lambda *refs: beam_body(messages, *refs), in_specs=[pl.Blo...  15.7 us
    all_to_all x1, waiting for transfers between devices, on_device(): arrived = lax.all_to_all(partial_profile, ('chan', 'tm'), 0, 0, tiled=True)  8.79 us
    pallas_call x1, Pallas kernels, filter_and_fold(): pl.pallas_call(main_body, in_specs=[pl.BlockSpec(memory_space=pltpu.SMEM)...  8.77 us
    ppermute x1, waiting for transfers between devices, on_device(): after = lax.ppermute(behind, 'tm', [(s + 1, s) for s in range(N_TM - 1)])  3.36 us
    ppermute x1, starting transfers between devices, on_device(): before = lax.ppermute(ahead, 'tm', [(s, s + 1) for s in range(N_TM - 1)])  2.43 us
  transfers between devices with their start and end apart: 15, of which 8 were waited for; matrix products, arithmetic and copies ran while one was open for 1% of the time, Pallas kernels for 7%

profile of v3, /device:TPU:1, one launch (start us, length us, event | category | flops | bytes accessed | tf_op | source)
XLA Modules:
  0.0 106.3 jit_solution(12723744560384499388)
XLA Ops:
  0.6 0.7 copy-done.7
  1.3 4.1 %beamform.3 = (s16[4,272,256]{2,1,0:T(8,128)(2,1)S(1)}, s16[4,272,256]{2,1,0:T(8,128)(2,1)S(1)}, f32[8,128]{1,0:T(8,128)S(1)}) custom-call(f32[2,1,64]{2,1,0:T(1,128)S(1)} %bitcast.19, bf16[2,32768,128]{2,1,0:T(8,128)(2,1)} %bitcast.22), custom_call_target="tpu_custom_call" | custom-call | tf_op jit(solution)/shard_map/beamform/pallas_call | solution.py:183
  5.4 0.0 copy-start.2
  5.4 0.0 copy-start
  5.4 0.0 copy-start.1
  5.4 0.0 copy-start.3
  5.5 0.0 copy-start.4
  5.5 0.0 copy-start.5
  5.5 0.0 copy-start.6
  5.5 0.0 copy-start.8
  5.5 7.3 %beamform.4 = (s16[4,272,256]{2,1,0:T(8,128)(2,1)S(1)}, s16[4,272,256]{2,1,0:T(8,128)(2,1)S(1)}, s16[4,272,256]{2,1,0:T(8,128)(2,1)S(1)}, s16[4,272,256]{2,1,0:T(8,128)(2,1)S(1)}, f32[8,128]{1,0:T(8,128)S(1)}) custom-call(f32[2,1,64]{2,1,0:T(1,128)S(1)} %bitcast.20, bf16[2,32768,128]{2,1,0:T(8,128)(2,1)} %bitcast.23, f32[8,128]{1,0:T(8,128)S(1)} %get-tuple-element.38.refs_2_), custom_call_target="tpu_custom_call" | custom-call | tf_op jit(solution)/shard_map/beamform/pallas_call | solution.py:183
  12.8 2.2 %collective-permute-start.1 = (s16[4,272,256]{2,1,0:T(8,128)(2,1)S(1)}, s16[4,272,256]{2,1,0:T(8,128)(2,1)S(1)}, u32[]{:S(2)}, u32[]{:S(2)}) collective-permute-start(s16[4,272,256]{2,1,0:T(8,128)(2,1)S(1)} %get-tuple-element.39), channel_id=1, source_target_pairs={{0,4},{1,5},{2,6},{3,7},{4,8},{5,9},{6,10},{7,11},{8,12},{9,13},{1... | collective-permute-start | bytes 1671176 | tf_op jit(solution)/shard_map/ppermute | solution.py:481
  15.0 1.5 %collective-permute-start.2 = (s16[4,272,256]{2,1,0:T(8,128)(2,1)S(1)}, s16[4,272,256]{2,1,0:T(8,128)(2,1)S(1)}, u32[]{:S(2)}, u32[]{:S(2)}) collective-permute-start(s16[4,272,256]{2,1,0:T(8,128)(2,1)S(1)} %get-tuple-element.40), channel_id=1, source_target_pairs={{0,12},{1,13},{2,14},{3,15},{4,0},{5,1},{6,2},{7,3},{8,4},{9,5},{1... | collective-permute-start | bytes 1671176 | tf_op jit(solution)/shard_map/ppermute | solution.py:481
  16.5 1.2 %collective-permute-start.4 = (s16[4,272,256]{2,1,0:T(8,128)(2,1)S(1)}, s16[4,272,256]{2,1,0:T(8,128)(2,1)S(1)}, u32[]{:S(2)}, u32[]{:S(2)}) collective-permute-start(s16[4,272,256]{2,1,0:T(8,128)(2,1)S(1)} %get-tuple-element.44), channel_id=1, source_target_pairs={{0,1},{1,2},{2,3},{3,0},{4,5},{5,6},{6,7},{7,4},{8,9},{9,10},{10,1... | collective-permute-start | bytes 1671176 | tf_op jit(solution)/shard_map/ppermute | solution.py:481
  17.7 1.5 %collective-permute-start.5 = (s16[4,272,256]{2,1,0:T(8,128)(2,1)S(1)}, s16[4,272,256]{2,1,0:T(8,128)(2,1)S(1)}, u32[]{:S(2)}, u32[]{:S(2)}) collective-permute-start(s16[4,272,256]{2,1,0:T(8,128)(2,1)S(1)} %get-tuple-element.45), channel_id=1, source_target_pairs={{0,3},{1,0},{2,1},{3,2},{4,7},{5,4},{6,5},{7,6},{8,11},{9,8},{10,9... | collective-permute-start | bytes 1671176 | tf_op jit(solution)/shard_map/ppermute | solution.py:481
  19.2 1.6 %collective-permute-start = (s16[4,272,256]{2,1,0:T(8,128)(2,1)S(1)}, s16[4,272,256]{2,1,0:T(8,128)(2,1)S(1)}, u32[]{:S(2)}, u32[]{:S(2)}) collective-permute-start(s16[4,272,256]{2,1,0:T(8,128)(2,1)S(1)} %get-tuple-element.37), channel_id=1, source_target_pairs={{0,8},{1,9},{2,10},{3,11},{4,12},{5,13},{6,14},{7,15},{8,0},{9,1},... | collective-permute-start | bytes 1671176 | tf_op jit(solution)/shard_map/ppermute | solution.py:481
  20.7 7.9 %collective-permute-done.1.refs_1_ = s16[4,272,256]{2,1,0:T(8,128)(2,1)S(1)} collective-permute-done((s16[4,272,256]{2,1,0:T(8,128)(2,1)S(1)}, s16[4,272,256]{2,1,0:T(8,128)(2,1)S(1)}, u32[]{:S(2)}, u32[]{:S(2)}) %collective-permute-start.1) | collective-permute-done | bytes 557088 | tf_op jit(solution)/shard_map/ppermute | solution.py:481
  28.6 2.7 %collective-permute-start.3 = (s16[4,272,256]{2,1,0:T(8,128)(2,1)S(1)}, s16[4,272,256]{2,1,0:T(8,128)(2,1)S(1)}, u32[]{:S(2)}, u32[]{:S(2)}) collective-permute-start(s16[4,272,256]{2,1,0:T(8,128)(2,1)S(1)} %get-tuple-element.43), channel_id=1, source_target_pairs={{0,2},{1,3},{2,0},{3,1},{4,6},{5,7},{6,4},{7,5},{8,10},{9,11},{10,... | collective-permute-start | bytes 1671176 | tf_op jit(solution)/shard_map/ppermute | solution.py:481
  31.3 4.3 %beamform.5 = (s16[4,272,256]{2,1,0:T(8,128)(2,1)S(1)}, s16[4,272,256]{2,1,0:T(8,128)(2,1)S(1)}, f32[8,128]{1,0:T(8,128)}) custom-call(f32[2,1,64]{2,1,0:T(1,128)S(1)} %bitcast.21, bf16[2,32768,128]{2,1,0:T(8,128)(2,1)} %bitcast.24, f32[8,128]{1,0:T(8,128)S(1)} %get-tuple-element.41.refs_2_), custom_call_target="tpu_custom_call" | custom-call | tf_op jit(solution)/shard_map/beamform/pallas_call | solution.py:183
  36.2 2.1 %response.1 = f32[2,2,512,128]{3,2,1,0:T(8,128)S(1)} custom-call(s32[1]{0:T(128)S(6)} %copy.25.offset, f32[1024,128]{1,0:T(8,128)S(1)} %bitcast.17), custom_call_target="tpu_custom_call" | custom-call | tf_op jit(solution)/shard_map/response/pallas_call | solution.py:276
  38.3 0.0 collective-permute-done.2.refs_2_
  38.3 0.0 collective-permute-done.4.refs_1_
  38.3 0.0 collective-permute-done.5.refs_2_
  38.3 3.2 %collective-permute-done.refs_0_ = s16[4,272,256]{2,1,0:T(8,128)(2,1)S(1)} collective-permute-done((s16[4,272,256]{2,1,0:T(8,128)(2,1)S(1)}, s16[4,272,256]{2,1,0:T(8,128)(2,1)S(1)}, u32[]{:S(2)}, u32[]{:S(2)}) %collective-permute-start) | collective-permute-done | bytes 557088 | tf_op jit(solution)/shard_map/ppermute | solution.py:481
  41.6 2.3 %collective-permute-done.3.refs_0_ = s16[4,272,256]{2,1,0:T(8,128)(2,1)S(1)} collective-permute-done((s16[4,272,256]{2,1,0:T(8,128)(2,1)S(1)}, s16[4,272,256]{2,1,0:T(8,128)(2,1)S(1)}, u32[]{:S(2)}, u32[]{:S(2)}) %collective-permute-start.3) | collective-permute-done | bytes 557088 | tf_op jit(solution)/shard_map/ppermute | solution.py:481
  43.9 0.8 middle.3
  44.6 0.1 collective-permute-start.10
  44.7 2.7 %collective-permute-start.11 = (s16[272,256]{1,0:T(8,128)(2,1)S(1)}, s16[272,256]{1,0:T(8,128)(2,1)S(1)}, u32[]{:S(2)}, u32[]{:S(2)}) collective-permute-start(s16[272,256]{1,0:T(8,128)(2,1)S(1)} %get-tuple-element.62), channel_id=1, source_target_pairs={{0,12},{1,13},{2,14},{3,15},{4,0},{5,1},{6,2},{7,3},{8,4},{9,5},{1... | collective-permute-start | bytes 417800 | tf_op jit(solution)/shard_map/ppermute | solution.py:481
  47.4 0.0 collective-permute-start.9
  47.4 0.8 middle.2
  48.1 1.6 %collective-permute-start.6 = (s16[272,256]{1,0:T(8,128)(2,1)S(1)}, s16[272,256]{1,0:T(8,128)(2,1)S(1)}, u32[]{:S(2)}, u32[]{:S(2)}) collective-permute-start(s16[272,256]{1,0:T(8,128)(2,1)S(1)} %get-tuple-element.52), channel_id=1, source_target_pairs={{0,2},{1,3},{2,0},{3,1},{4,6},{5,7},{6,4},{7,5},{8,10},{9,11},{10,... | collective-permute-start | bytes 417800 | tf_op jit(solution)/shard_map/ppermute | solution.py:481
  49.8 0.3 collective-permute-start.7
  50.1 2.4 %collective-permute-start.8 = (s16[272,256]{1,0:T(8,128)(2,1)S(1)}, s16[272,256]{1,0:T(8,128)(2,1)S(1)}, u32[]{:S(2)}, u32[]{:S(2)}) collective-permute-start(s16[272,256]{1,0:T(8,128)(2,1)S(1)} %get-tuple-element.54), channel_id=1, source_target_pairs={{0,3},{1,0},{2,1},{3,2},{4,7},{5,4},{6,5},{7,6},{8,11},{9,8},{10,9... | collective-permute-start | bytes 417800 | tf_op jit(solution)/shard_map/ppermute | solution.py:481
  52.4 0.0 collective-permute-done.11.refs_7_
  52.4 0.5 collective-permute-done.9.refs_5_
  52.9 0.8 collective-permute-done.6.refs_1_
  53.6 1.5 %collective-permute-done.7.refs_2_ = s16[272,256]{1,0:T(8,128)(2,1)S(1)} collective-permute-done((s16[272,256]{1,0:T(8,128)(2,1)S(1)}, s16[272,256]{1,0:T(8,128)(2,1)S(1)}, u32[]{:S(2)}, u32[]{:S(2)}) %collective-permute-start.7) | collective-permute-done | bytes 139296 | tf_op jit(solution)/shard_map/ppermute | solution.py:481
  55.1 0.4 last.1
  55.5 2.4 %collective-permute-start.12 = (s16[2,272,256]{2,1,0:T(8,128)(2,1)S(1)}, s16[2,272,256]{2,1,0:T(8,128)(2,1)S(1)}, u32[]{:S(2)}, u32[]{:S(2)}) collective-permute-start(s16[2,272,256]{2,1,0:T(8,128)(2,1)S(1)} %get-tuple-element.64), channel_id=1, source_target_pairs={{0,1},{1,2},{2,3},{3,4},{4,5},{5,6},{6,7},{7,8},{8,9},{9,10},{10,1... | collective-permute-start | bytes 835592 | tf_op jit(solution)/shard_map/ppermute | solution.py:515
  57.9 1.3 %collective-permute-start.13 = (f32[2,16,256]{2,1,0:T(8,128)S(1)}, f32[2,16,256]{2,1,0:T(8,128)S(1)}, u32[]{:S(2)}, u32[]{:S(2)}) collective-permute-start(f32[2,16,256]{2,1,0:T(8,128)S(1)} %get-tuple-element.65), channel_id=1, source_target_pairs={{1,0},{2,1},{3,2},{4,3},{5,4},{6,5},{7,6},{8,7},{9,8},{10,9},{11,1... | collective-permute-start | bytes 98312 | tf_op jit(solution)/shard_map/ppermute | solution.py:516
  59.2 3.4 %collective-permute-done.13.after_ref = f32[2,16,256]{2,1,0:T(8,128)S(1)} collective-permute-done((f32[2,16,256]{2,1,0:T(8,128)S(1)}, f32[2,16,256]{2,1,0:T(8,128)S(1)}, u32[]{:S(2)}, u32[]{:S(2)}) %collective-permute-start.13) | collective-permute-done | bytes 32800 | tf_op jit(solution)/shard_map/ppermute | solution.py:516
  62.6 0.0 collective-permute-done.12.before_ref
  62.7 8.8 %filter_and_fold.1 = (bf16[2,256,256]{2,1,0:T(8,128)(2,1)S(1)}, f32[1,128]{1,0:T(1,128)}, f32[128,128]{1,0:T(8,128)}) custom-call(s32[1]{0:T(128)S(6)} %copy.25.offset, f32[2,256,256]{2,1,0:T(8,128)S(1)} %get-tuple-element.63.own_ref, s16[2,272,256]{2,1,0:T(8,128)(2,1)S(1)} %collective-permute-done.12.before_ref, ...), custom_call_target="tpu_custom_call" | custom-call | tf_op jit(solution)/shard_map/filter_and_fold/pallas_call | solution.py:465
  71.4 24.1 %all-to-all-start = ((f32[128,1,128]{2,1,0:T(1,128)}), f32[128,1,128]{2,1,0:T(1,128)S(1)}, u32[]{:S(2)}, u32[]{:S(2)}) async-start(f32[128,1,128]{2,1,0:T(1,128)} %bitcast.11), calls=%async_computation | async-start | bytes 131072 | tf_op jit(solution)/shard_map/all_to_all | solution.py:524
  95.6 0.8 reshape.33
  96.4 8.8 %all-to-all-done = f32[128,1,128]{2,1,0:T(1,128)S(1)} async-done(((f32[128,1,128]{2,1,0:T(1,128)}), f32[128,1,128]{2,1,0:T(1,128)S(1)}, u32[]{:S(2)}, u32[]{:S(2)}) %all-to-all-start) | async-done | bytes 65568 | tf_op jit(solution)/shard_map/all_to_all | solution.py:524
  105.2 0.5 constant_dynamic-slice_fusion
  105.7 0.7 reduce_sum.19
  (12 shorter events, 0.0 us)
Async XLA Ops:
  0.6 0.7 copy-start.7
  5.4 30.8 %copy-start.2 = (f32[1,131072]{1,0:T(1,128)S(1)}, f32[1,131072]{1,0:T(1,128)}, u32[]{:S(2)}) copy-start(f32[1,131072]{1,0:T(1,128)} %param.14) | copy-start | bytes 1572868
  5.4 57.2 %copy-start = (bf16[4,2,256,256]{3,2,1,0:T(8,128)(2,1)S(1)}, bf16[4,2,256,256]{3,2,1,0:T(8,128)(2,1)}, u32[]{:S(2)}) copy-start(bf16[4,2,256,256]{3,2,1,0:T(8,128)(2,1)} %constant.24.clone.rows_forward) | copy-start | bytes 3145732
  5.4 57.2 %copy-start.1 = (bf16[4,2,256,256]{3,2,1,0:T(8,128)(2,1)S(1)}, bf16[4,2,256,256]{3,2,1,0:T(8,128)(2,1)}, u32[]{:S(2)}) copy-start(bf16[4,2,256,256]{3,2,1,0:T(8,128)(2,1)} %constant.27.clone.rows_back) | copy-start | bytes 3145732
  5.4 57.2 %copy-start.3 = (bf16[2,2,256,256]{3,2,1,0:T(8,128)(2,1)S(1)}, bf16[2,2,256,256]{3,2,1,0:T(8,128)(2,1)}, u32[]{:S(2)}) copy-start(bf16[2,2,256,256]{3,2,1,0:T(8,128)(2,1)} %constant.25.clone.columns_forward) | copy-start | bytes 1572868
  5.5 57.2 %copy-start.4 = (bf16[2,2,256,256]{3,2,1,0:T(8,128)(2,1)S(1)}, bf16[2,2,256,256]{3,2,1,0:T(8,128)(2,1)}, u32[]{:S(2)}) copy-start(bf16[2,2,256,256]{3,2,1,0:T(8,128)(2,1)} %constant.26.clone.columns_back) | copy-start | bytes 1572868
  5.5 57.2 %copy-start.5 = (s32[65536]{0:T(1024)S(1)}, s32[65536]{0:T(1024)}, u32[]{:S(2)}) copy-start(s32[65536]{0:T(1024)} %param.17) | copy-start | bytes 786436
  5.5 57.2 %copy-start.6 = (f32[256,256]{1,0:T(8,128)S(1)}, f32[256,256]{1,0:T(8,128)}, u32[]{:S(2)}) copy-start(f32[256,256]{1,0:T(8,128)} %constant.29.clone.group) | copy-start | bytes 786436
  5.5 57.2 %copy-start.8 = (s32[1,64]{1,0:T(1,128)S(1)}, s32[1,64]{1,0:T(1,128)}, u32[]{:S(2)}) copy-start(s32[1,64]{1,0:T(1,128)} %flags_ref.1) | copy-start | bytes 772
  12.8 15.8 %collective-permute-start.1 = (s16[4,272,256]{2,1,0:T(8,128)(2,1)S(1)}, s16[4,272,256]{2,1,0:T(8,128)(2,1)S(1)}, u32[]{:S(2)}, u32[]{:S(2)}) collective-permute-start(s16[4,272,256]{2,1,0:T(8,128)(2,1)S(1)} %get-tuple-element.39), channel_id=1, source_target_pairs={{0,4},{1,5},{2,6},{3,7},{4,8},{5,9},{6,10},{7,11},{8,12},{9,13},{1... | collective-permute-start | bytes 1671176 | tf_op jit(solution)/shard_map/ppermute | solution.py:481
  15.0 23.3 %collective-permute-start.2 = (s16[4,272,256]{2,1,0:T(8,128)(2,1)S(1)}, s16[4,272,256]{2,1,0:T(8,128)(2,1)S(1)}, u32[]{:S(2)}, u32[]{:S(2)}) collective-permute-start(s16[4,272,256]{2,1,0:T(8,128)(2,1)S(1)} %get-tuple-element.40), channel_id=1, source_target_pairs={{0,12},{1,13},{2,14},{3,15},{4,0},{5,1},{6,2},{7,3},{8,4},{9,5},{1... | collective-permute-start | bytes 1671176 | tf_op jit(solution)/shard_map/ppermute | solution.py:481
  16.5 21.8 %collective-permute-start.4 = (s16[4,272,256]{2,1,0:T(8,128)(2,1)S(1)}, s16[4,272,256]{2,1,0:T(8,128)(2,1)S(1)}, u32[]{:S(2)}, u32[]{:S(2)}) collective-permute-start(s16[4,272,256]{2,1,0:T(8,128)(2,1)S(1)} %get-tuple-element.44), channel_id=1, source_target_pairs={{0,1},{1,2},{2,3},{3,0},{4,5},{5,6},{6,7},{7,4},{8,9},{9,10},{10,1... | collective-permute-start | bytes 1671176 | tf_op jit(solution)/shard_map/ppermute | solution.py:481
  17.7 20.6 %collective-permute-start.5 = (s16[4,272,256]{2,1,0:T(8,128)(2,1)S(1)}, s16[4,272,256]{2,1,0:T(8,128)(2,1)S(1)}, u32[]{:S(2)}, u32[]{:S(2)}) collective-permute-start(s16[4,272,256]{2,1,0:T(8,128)(2,1)S(1)} %get-tuple-element.45), channel_id=1, source_target_pairs={{0,3},{1,0},{2,1},{3,2},{4,7},{5,4},{6,5},{7,6},{8,11},{9,8},{10,9... | collective-permute-start | bytes 1671176 | tf_op jit(solution)/shard_map/ppermute | solution.py:481
  19.2 22.4 %collective-permute-start = (s16[4,272,256]{2,1,0:T(8,128)(2,1)S(1)}, s16[4,272,256]{2,1,0:T(8,128)(2,1)S(1)}, u32[]{:S(2)}, u32[]{:S(2)}) collective-permute-start(s16[4,272,256]{2,1,0:T(8,128)(2,1)S(1)} %get-tuple-element.37), channel_id=1, source_target_pairs={{0,8},{1,9},{2,10},{3,11},{4,12},{5,13},{6,14},{7,15},{8,0},{9,1},... | collective-permute-start | bytes 1671176 | tf_op jit(solution)/shard_map/ppermute | solution.py:481
  28.6 15.3 %collective-permute-start.3 = (s16[4,272,256]{2,1,0:T(8,128)(2,1)S(1)}, s16[4,272,256]{2,1,0:T(8,128)(2,1)S(1)}, u32[]{:S(2)}, u32[]{:S(2)}) collective-permute-start(s16[4,272,256]{2,1,0:T(8,128)(2,1)S(1)} %get-tuple-element.43), channel_id=1, source_target_pairs={{0,2},{1,3},{2,0},{3,1},{4,6},{5,7},{6,4},{7,5},{8,10},{9,11},{10,... | collective-permute-start | bytes 1671176 | tf_op jit(solution)/shard_map/ppermute | solution.py:481
  44.6 5.4 %collective-permute-start.10 = (s16[272,256]{1,0:T(8,128)(2,1)S(1)}, s16[272,256]{1,0:T(8,128)(2,1)S(1)}, u32[]{:S(2)}, u32[]{:S(2)}) collective-permute-start(s16[272,256]{1,0:T(8,128)(2,1)S(1)} %get-tuple-element.61), channel_id=1, source_target_pairs={{0,4},{1,5},{2,6},{3,7},{4,8},{5,9},{6,10},{7,11},{8,12},{9,13},{1... | collective-permute-start | bytes 417800 | tf_op jit(solution)/shard_map/ppermute | solution.py:481
  44.7 7.7 %collective-permute-start.11 = (s16[272,256]{1,0:T(8,128)(2,1)S(1)}, s16[272,256]{1,0:T(8,128)(2,1)S(1)}, u32[]{:S(2)}, u32[]{:S(2)}) collective-permute-start(s16[272,256]{1,0:T(8,128)(2,1)S(1)} %get-tuple-element.62), channel_id=1, source_target_pairs={{0,12},{1,13},{2,14},{3,15},{4,0},{5,1},{6,2},{7,3},{8,4},{9,5},{1... | collective-permute-start | bytes 417800 | tf_op jit(solution)/shard_map/ppermute | solution.py:481
  47.4 5.5 %collective-permute-start.9 = (s16[272,256]{1,0:T(8,128)(2,1)S(1)}, s16[272,256]{1,0:T(8,128)(2,1)S(1)}, u32[]{:S(2)}, u32[]{:S(2)}) collective-permute-start(s16[272,256]{1,0:T(8,128)(2,1)S(1)} %get-tuple-element.60), channel_id=1, source_target_pairs={{0,8},{1,9},{2,10},{3,11},{4,12},{5,13},{6,14},{7,15},{8,0},{9,1},... | collective-permute-start | bytes 417800 | tf_op jit(solution)/shard_map/ppermute | solution.py:481
  48.1 5.5 %collective-permute-start.6 = (s16[272,256]{1,0:T(8,128)(2,1)S(1)}, s16[272,256]{1,0:T(8,128)(2,1)S(1)}, u32[]{:S(2)}, u32[]{:S(2)}) collective-permute-start(s16[272,256]{1,0:T(8,128)(2,1)S(1)} %get-tuple-element.52), channel_id=1, source_target_pairs={{0,2},{1,3},{2,0},{3,1},{4,6},{5,7},{6,4},{7,5},{8,10},{9,11},{10,... | collective-permute-start | bytes 417800 | tf_op jit(solution)/shard_map/ppermute | solution.py:481
  49.8 5.4 %collective-permute-start.7 = (s16[272,256]{1,0:T(8,128)(2,1)S(1)}, s16[272,256]{1,0:T(8,128)(2,1)S(1)}, u32[]{:S(2)}, u32[]{:S(2)}) collective-permute-start(s16[272,256]{1,0:T(8,128)(2,1)S(1)} %get-tuple-element.53), channel_id=1, source_target_pairs={{0,1},{1,2},{2,3},{3,0},{4,5},{5,6},{6,7},{7,4},{8,9},{9,10},{10,1... | collective-permute-start | bytes 417800 | tf_op jit(solution)/shard_map/ppermute | solution.py:481
  50.1 5.1 %collective-permute-start.8 = (s16[272,256]{1,0:T(8,128)(2,1)S(1)}, s16[272,256]{1,0:T(8,128)(2,1)S(1)}, u32[]{:S(2)}, u32[]{:S(2)}) collective-permute-start(s16[272,256]{1,0:T(8,128)(2,1)S(1)} %get-tuple-element.54), channel_id=1, source_target_pairs={{0,3},{1,0},{2,1},{3,2},{4,7},{5,4},{6,5},{7,6},{8,11},{9,8},{10,9... | collective-permute-start | bytes 417800 | tf_op jit(solution)/shard_map/ppermute | solution.py:481
  55.5 7.1 %collective-permute-start.12 = (s16[2,272,256]{2,1,0:T(8,128)(2,1)S(1)}, s16[2,272,256]{2,1,0:T(8,128)(2,1)S(1)}, u32[]{:S(2)}, u32[]{:S(2)}) collective-permute-start(s16[2,272,256]{2,1,0:T(8,128)(2,1)S(1)} %get-tuple-element.64), channel_id=1, source_target_pairs={{0,1},{1,2},{2,3},{3,4},{4,5},{5,6},{6,7},{7,8},{8,9},{9,10},{10,1... | collective-permute-start | bytes 835592 | tf_op jit(solution)/shard_map/ppermute | solution.py:515
  57.9 4.7 %collective-permute-start.13 = (f32[2,16,256]{2,1,0:T(8,128)S(1)}, f32[2,16,256]{2,1,0:T(8,128)S(1)}, u32[]{:S(2)}, u32[]{:S(2)}) collective-permute-start(f32[2,16,256]{2,1,0:T(8,128)S(1)} %get-tuple-element.65), channel_id=1, source_target_pairs={{1,0},{2,1},{3,2},{4,3},{5,4},{6,5},{7,6},{8,7},{9,8},{10,9},{11,1... | collective-permute-start | bytes 98312 | tf_op jit(solution)/shard_map/ppermute | solution.py:516
  71.4 33.7 %all-to-all-start = ((f32[128,1,128]{2,1,0:T(1,128)}), f32[128,1,128]{2,1,0:T(1,128)S(1)}, u32[]{:S(2)}, u32[]{:S(2)}) async-start(f32[128,1,128]{2,1,0:T(1,128)} %bitcast.11), calls=%async_computation | async-start | bytes 131072 | tf_op jit(solution)/shard_map/all_to_all | solution.py:524

commit v4 on v3

--- a/solution.py
+++ b/solution.py
@@ -78,7 +78,7 @@
 
 
 CODE_TOP = 32000.0
-HEADER = 16
+HEADER = 8
 ROWS = 2 * 128 + HEADER
 
 
@@ -88,8 +88,7 @@
     level = jnp.floor(4.0 * jnp.log2(CODE_TOP / jnp.maximum(top, 1e-30)))
     scale = jnp.exp2(0.25 * level)[0:1]
     whole = lambda value: jnp.round(value).astype(jnp.int32).astype(jnp.int16)
-    header = jnp.concatenate([level, level], axis=0)
-    return whole(real * scale), whole(imag * scale), whole(header)
+    return whole(real * scale), whole(imag * scale), whole(level)
 
 
 def decode(block_ref, *lead):
@@ -102,10 +101,10 @@
     return parts
 
 
-def beam_body(messages, gains, samples, *refs):
-    table, buffer, arrived = refs[-3:]
-    outs = refs[-4 - len(messages) : -4]
-    refs[-4][...] = jnp.zeros((8, LANES), F32)
+def beam_body(messages, gains_hbm, samples, *refs):
+    table, buffer, planes, gains, arrived = refs[-5:]
+    outs = refs[-6 - len(messages) : -6]
+    refs[-6][...] = jnp.zeros((8, LANES), F32)
     index = lax.axis_index("tm").astype(jnp.int32)
     down_at = index // GRID_SIDE
     across_at = index % GRID_SIDE
@@ -121,12 +120,15 @@
             samples.at[:, pl.ds(first, 1024), :], buffer.at[slot], arrived.at[slot]
         )
 
+    fetch = pltpu.make_async_copy(gains_hbm, gains, arrived.at[4 * len(messages)])
+    fetch.start()
     copies = []
     for number, (half, step) in enumerate(messages):
         copies.append([copy_of(number * 4 + j, half, step, j) for j in range(4)])
         for copy in copies[-1]:
             copy.start()
 
+    fetch.wait()
     shape = (128, 256)
     row = lax.broadcasted_iota(jnp.int32, shape, 0)
     col = lax.broadcasted_iota(jnp.int32, shape, 1)
@@ -151,31 +153,39 @@
     high = value.astype(BF16).astype(F32)
     table[...] = jnp.where(part == 0, high, value - high).astype(BF16)
 
-    for number in range(len(messages)):
-        for j in range(4):
-            copies[number][j].wait()
-            weights = table[...]
-            at = number * 4 + j
-            columns = []
-            for group in range(8):
-                rows = pl.ds(group * 128, 128)
-                columns.append(
-                    jnp.concatenate([buffer[at, 0, rows, :], buffer[at, 1, rows, :]], axis=0)
-                )
-            product = jnp.dot(
-                weights, jnp.concatenate(columns, axis=1), preferred_element_type=F32
+    def combine(at):
+        copies[at // 4][at % 4].wait()
+        columns = []
+        for group in range(8):
+            rows = pl.ds(group * 128, 128)
+            columns.append(
+                jnp.concatenate([buffer[at, 0, rows, :], buffer[at, 1, rows, :]], axis=0)
             )
-            both = product[:64] + product[64:]
-            planes = []
-            for comp in (0, 1):
-                lanes = lambda base: jnp.concatenate(
-                    [both[base : base + 16, g * 128 : g * 128 + 128] for g in range(8)], axis=0
-                )
-                planes.append(
-                    jnp.concatenate([lanes(comp * 32), lanes(comp * 32 + 16)], axis=1)
-                )
-            out = outs[number]
-            out[j, 0:128], out[j, 128:256], out[j, 256:272] = encode(*planes)
+        product = jnp.dot(
+            table[...], jnp.concatenate(columns, axis=1), preferred_element_type=F32
+        )
+        both = product[:64] + product[64:]
+        for comp in (0, 1):
+            for side in (0, 1):
+                base = comp * 32 + side * 16
+                lanes = slice(side * LANES, side * LANES + LANES)
+                for group in range(8):
+                    rows = pl.ds(group * 16, 16)
+                    part = both[base : base + 16, group * 128 : group * 128 + 128]
+                    planes[at % 2, comp, rows, lanes] = part
+
+    def finish(at):
+        out, j = outs[at // 4], at % 4
+        out[j, 0:128], out[j, 128:256], out[j, 256:264] = encode(
+            planes[at % 2, 0], planes[at % 2, 1]
+        )
+
+    count = 4 * len(messages)
+    combine(0)
+    for at in range(1, count):
+        combine(at)
+        finish(at - 1)
+    finish(count - 1)
 
 
 def beamform(gains, samples, messages, ready=()):
@@ -183,7 +193,7 @@
     return pl.pallas_call(
         lambda *refs: beam_body(messages, *refs),
         in_specs=[
-            pl.BlockSpec(memory_space=pltpu.VMEM),
+            pl.BlockSpec(memory_space=pltpu.HBM),
             pl.BlockSpec(memory_space=pltpu.HBM),
         ]
         + [pl.BlockSpec(memory_space=pltpu.VMEM)] * len(ready),
@@ -192,7 +202,9 @@
         scratch_shapes=[
             pltpu.VMEM((128, 256), BF16),
             pltpu.VMEM((count * 4, 2, 1024, LANES), BF16),
-            pltpu.SemaphoreType.DMA((count * 4,)),
+            pltpu.VMEM((2, 2, 128, SIDE), F32),
+            pltpu.VMEM((2, 1, 64), F32),
+            pltpu.SemaphoreType.DMA((count * 4 + 1,)),
         ],
         compiler_params=pltpu.CompilerParams(vmem_limit_bytes=50 * 1024 * 1024),
         name="beamform",
@@ -207,7 +219,7 @@
             more = decode(part, second)
             total = [total[0] + more[0], total[1] + more[1]]
         if second:
-            out[0:128], out[128:256], out[256:272] = encode(*total)
+            out[0:128], out[128:256], out[256:264] = encode(*total)
         else:
             out[0], out[1] = total
 
@@ -236,7 +248,7 @@
             total = [total[0] + more[0], total[1] + more[1]]
         rows = pl.ds(half * 128, 128)
         own[0, rows], own[1, rows] = total
-        ahead[half, 0:128], ahead[half, 128:256], ahead[half, 256:272] = encode(*total)
+        ahead[half, 0:128], ahead[half, 128:256], ahead[half, 256:264] = encode(*total)
         if half == 0:
             behind[0], behind[1] = total[0][0:16], total[1][0:16]
 
@@ -497,14 +509,17 @@
     def second_send(half, step, value):
         return send(value, 0, step) if half == 0 else send(value, step, 0)
 
-    response = make_response(offsets, chirp_phase.reshape(8 * LANES, LANES))
     got = [[], []]
     ready = ()
-    for messages in (((0, 2), (1, 2)), ((0, 1), (1, 1), (0, 3), (1, 3)), ((0, 0), (1, 0))):
+    for messages in (((0, 2), (1, 2)), ((1, 1), (1, 3), (0, 1), (0, 3)), ((0, 0), (1, 0))):
+        if messages[0][1] == 0:
+            held = (ready, got[0][0], got[1][0], chirp_phase)
+            ready, got[0][0], got[1][0], chirp_phase = lax.optimization_barrier(held)
         made = beamform(gains, samples, messages, ready)
         ready = (made[-1],)
         for (half, step), value in zip(messages, made):
             got[half].append(first_send(half, step, value) if step else value)
+    response = make_response(offsets, chirp_phase.reshape(8 * LANES, LANES))
     got, response = lax.optimization_barrier((got, response))
     landed = [[], []]
     for half in (0, 1):
@@ -522,8 +537,7 @@
     dedispersed = filtered.reshape(2, 1, HALF)
     sk_weight = weight[:, :64]
     arrived = lax.all_to_all(partial_profile, ("chan", "tm"), 0, 0, tiled=True)
-    arrived = arrived.reshape(CHANNELS, N_TM, LANES)
-    by_channel = jnp.sum(arrived, axis=1)
+    by_channel = jnp.sum(arrived.reshape(CHANNELS, N_TM, LANES), axis=1)
     profile = lax.dynamic_slice_in_dim(by_channel, lax.axis_index("chan"), 1, 0)
     band_profile = jnp.sum(by_channel, axis=0)
     return (dedispersed, sk_weight, profile, band_profile)

time: 107 us -> 91.5 us (0.86)
  starting transfers between devices: 45.5 us -> 39.2 us
  waiting for transfers between devices: 28.3 us -> 23.3 us
  Pallas kernels: 28.4 us -> 24.6 us
    all_to_all x1, starting transfers between devices: 24.1 us -> 15.2 us  [on_device(): arrived = lax.all_to_all(partial_profile, ('chan', 'tm'), 0, 0, tiled=True)]
    ppermute x12, waiting for transfers between devices: 16.1 us -> 11.1 us  [send(): return lax.ppermute(value, 'tm', steps(down, across))]
    ppermute x12, starting transfers between devices: 17.6 us -> 21.4 us  [send(): return lax.ppermute(value, 'tm', steps(down, across))]
    pallas_call x3, Pallas kernels: 15.7 us -> 11.9 us  [beamform(): pl.pallas_call(lambda *refs: beam_body(messages, *refs), in_specs=[pl.Blo...]
    ppermute x1, starting transfers between devices: 2.43 us -> 1.31 us  [on_device(): before = lax.ppermute(ahead, 'tm', [(s, s + 1) for s in range(N_TM - 1)])]
  transfers between devices with their start and end apart: 15 -> 15, of which waited for: 8 -> 6; matrix products, arithmetic and copies ran while one was open for 1% -> 1% of each run, Pallas kernels for 7% -> 13%
where the time goes in v4:
time: 91.5 us; the launch traced here: 91.3 us
  starting transfers between devices  39.2 us (43%)
  Pallas kernels  24.6 us (27%)
  waiting for transfers between devices  23.3 us (25%)
  local copies, waits for them, and re-layouts  2.01 us (2%)
  between operations  1.48 us (2%)
    ppermute x12, starting transfers between devices, send(): return lax.ppermute(value, 'tm', steps(down, across))  21.4 us
    all_to_all x1, starting transfers between devices, on_device(): arrived = lax.all_to_all(partial_profile, ('chan', 'tm'), 0, 0, tiled=True)  15.2 us
    pallas_call x3, Pallas kernels, beamform(): pl.pallas_call(lambda *refs: beam_body(messages, *refs), in_specs=[pl.Blo...  11.9 us
    ppermute x12, waiting for transfers between devices, send(): return lax.ppermute(value, 'tm', steps(down, across))  11.1 us
    all_to_all x1, waiting for transfers between devices, on_device(): arrived = lax.all_to_all(partial_profile, ('chan', 'tm'), 0, 0, tiled=True)  8.79 us
    pallas_call x1, Pallas kernels, filter_and_fold(): pl.pallas_call(main_body, in_specs=[pl.BlockSpec(memory_space=pltpu.SMEM)...  8.78 us
    ppermute x1, waiting for transfers between devices, on_device(): after = lax.ppermute(behind, 'tm', [(s + 1, s) for s in range(N_TM - 1)])  3.36 us
    pallas_call x1, Pallas kernels, make_response(): pl.pallas_call(response_body, in_specs=[pl.BlockSpec(memory_space=pltpu.S...  2.05 us
  transfers between devices with their start and end apart: 15, of which 6 were waited for; matrix products, arithmetic and copies ran while one was open for 1% of the time, Pallas kernels for 13%

profile of v4, /device:TPU:1, one launch (start us, length us, event | category | flops | bytes accessed | tf_op | source)
XLA Modules:
  0.0 91.3 jit_solution(728826775057714487)
XLA Ops:
  0.6 0.7 copy-done.7
  1.3 3.2 %beamform.3 = (s16[4,264,256]{2,1,0:T(8,128)(2,1)S(1)}, s16[4,264,256]{2,1,0:T(8,128)(2,1)S(1)}, f32[8,128]{1,0:T(8,128)S(1)}) custom-call(f32[2,1,64]{2,1,0:T(1,128)S(1)} %bitcast.19, bf16[2,32768,128]{2,1,0:T(8,128)(2,1)} %bitcast.22), custom_call_target="tpu_custom_call" | custom-call | tf_op jit(solution)/shard_map/beamform/pallas_call | solution.py:193
  4.5 3.8 %collective-permute-start = (s16[4,264,256]{2,1,0:T(8,128)(2,1)S(1)}, s16[4,264,256]{2,1,0:T(8,128)(2,1)S(1)}, u32[]{:S(2)}, u32[]{:S(2)}) collective-permute-start(s16[4,264,256]{2,1,0:T(8,128)(2,1)S(1)} %get-tuple-element.43), channel_id=1, source_target_pairs={{0,8},{1,9},{2,10},{3,11},{4,12},{5,13},{6,14},{7,15},{8,0},{9,1},... | collective-permute-start | bytes 1622024 | tf_op jit(solution)/shard_map/ppermute | solution.py:493
  8.3 2.7 %collective-permute-start.1 = (s16[4,264,256]{2,1,0:T(8,128)(2,1)S(1)}, s16[4,264,256]{2,1,0:T(8,128)(2,1)S(1)}, u32[]{:S(2)}, u32[]{:S(2)}) collective-permute-start(s16[4,264,256]{2,1,0:T(8,128)(2,1)S(1)} %get-tuple-element.44), channel_id=1, source_target_pairs={{0,2},{1,3},{2,0},{3,1},{4,6},{5,7},{6,4},{7,5},{8,10},{9,11},{10,... | collective-permute-start | bytes 1622024 | tf_op jit(solution)/shard_map/ppermute | solution.py:493
  11.1 0.0 copy-start.4
  11.1 0.0 copy-start.5
  11.1 0.0 copy-start.6
  11.1 0.0 copy-start.8
  11.1 5.3 %beamform.4 = (s16[4,264,256]{2,1,0:T(8,128)(2,1)S(1)}, s16[4,264,256]{2,1,0:T(8,128)(2,1)S(1)}, s16[4,264,256]{2,1,0:T(8,128)(2,1)S(1)}, s16[4,264,256]{2,1,0:T(8,128)(2,1)S(1)}, f32[8,128]{1,0:T(8,128)S(1)}) custom-call(f32[2,1,64]{2,1,0:T(1,128)S(1)} %bitcast.20, bf16[2,32768,128]{2,1,0:T(8,128)(2,1)} %bitcast.23, f32[8,128]{1,0:T(8,128)S(1)} %get-tuple-element.41.refs_2_), custom_call_target="tpu_custom_call" | custom-call | tf_op jit(solution)/shard_map/beamform/pallas_call | solution.py:193
  16.5 0.5 collective-permute-start.2
  16.9 2.3 %collective-permute-start.3 = (s16[4,264,256]{2,1,0:T(8,128)(2,1)S(1)}, s16[4,264,256]{2,1,0:T(8,128)(2,1)S(1)}, u32[]{:S(2)}, u32[]{:S(2)}) collective-permute-start(s16[4,264,256]{2,1,0:T(8,128)(2,1)S(1)} %get-tuple-element.47), channel_id=1, source_target_pairs={{0,12},{1,13},{2,14},{3,15},{4,0},{5,1},{6,2},{7,3},{8,4},{9,5},{1... | collective-permute-start | bytes 1622024 | tf_op jit(solution)/shard_map/ppermute | solution.py:493
  19.2 0.3 collective-permute-start.4
  19.5 0.5 collective-permute-done.refs_0_
  20.0 2.5 %collective-permute-start.5 = (s16[4,264,256]{2,1,0:T(8,128)(2,1)S(1)}, s16[4,264,256]{2,1,0:T(8,128)(2,1)S(1)}, u32[]{:S(2)}, u32[]{:S(2)}) collective-permute-start(s16[4,264,256]{2,1,0:T(8,128)(2,1)S(1)} %get-tuple-element.52), channel_id=1, source_target_pairs={{0,3},{1,0},{2,1},{3,2},{4,7},{5,4},{6,5},{7,6},{8,11},{9,8},{10,9... | collective-permute-start | bytes 1622024 | tf_op jit(solution)/shard_map/ppermute | solution.py:493
  23.2 0.0 collective-permute-done.1.refs_0_
  23.2 3.4 %beamform.5 = (s16[4,264,256]{2,1,0:T(8,128)(2,1)S(1)}, s16[4,264,256]{2,1,0:T(8,128)(2,1)S(1)}, f32[8,128]{1,0:T(8,128)}) custom-call(f32[2,1,64]{2,1,0:T(1,128)S(1)} %bitcast.21, bf16[2,32768,128]{2,1,0:T(8,128)(2,1)} %bitcast.24, f32[8,128]{1,0:T(8,128)S(1)} %get-tuple-element.48.refs_2_), custom_call_target="tpu_custom_call" | custom-call | tf_op jit(solution)/shard_map/beamform/pallas_call | solution.py:193
  26.6 2.1 %response.1 = f32[2,2,512,128]{3,2,1,0:T(8,128)S(1)} custom-call(s32[1]{0:T(128)S(6)} %copy.25.offset, f32[1024,128]{1,0:T(8,128)S(1)} %bitcast.17), custom_call_target="tpu_custom_call" | custom-call | tf_op jit(solution)/shard_map/response/pallas_call | solution.py:288
  28.7 3.3 %collective-permute-done.2.refs_1_ = s16[4,264,256]{2,1,0:T(8,128)(2,1)S(1)} collective-permute-done((s16[4,264,256]{2,1,0:T(8,128)(2,1)S(1)}, s16[4,264,256]{2,1,0:T(8,128)(2,1)S(1)}, u32[]{:S(2)}, u32[]{:S(2)}) %collective-permute-start.2) | collective-permute-done | bytes 540704 | tf_op jit(solution)/shard_map/ppermute | solution.py:493
  32.0 0.0 collective-permute-done.3.refs_2_
  32.0 2.7 %collective-permute-done.4.refs_1_ = s16[4,264,256]{2,1,0:T(8,128)(2,1)S(1)} collective-permute-done((s16[4,264,256]{2,1,0:T(8,128)(2,1)S(1)}, s16[4,264,256]{2,1,0:T(8,128)(2,1)S(1)}, u32[]{:S(2)}, u32[]{:S(2)}) %collective-permute-start.4) | collective-permute-done | bytes 540704 | tf_op jit(solution)/shard_map/ppermute | solution.py:493
  34.7 0.0 collective-permute-done.5.refs_2_
  34.7 0.8 middle.3
  35.5 0.6 collective-permute-start.10
  36.1 2.2 %collective-permute-start.11 = (s16[264,256]{1,0:T(8,128)(2,1)S(1)}, s16[264,256]{1,0:T(8,128)(2,1)S(1)}, u32[]{:S(2)}, u32[]{:S(2)}) collective-permute-start(s16[264,256]{1,0:T(8,128)(2,1)S(1)} %get-tuple-element.70), channel_id=1, source_target_pairs={{0,12},{1,13},{2,14},{3,15},{4,0},{5,1},{6,2},{7,3},{8,4},{9,5},{1... | collective-permute-start | bytes 405512 | tf_op jit(solution)/shard_map/ppermute | solution.py:493
  38.2 0.0 collective-permute-start.9
  38.3 0.8 middle.2
  39.0 3.9 %collective-permute-start.6 = (s16[264,256]{1,0:T(8,128)(2,1)S(1)}, s16[264,256]{1,0:T(8,128)(2,1)S(1)}, u32[]{:S(2)}, u32[]{:S(2)}) collective-permute-start(s16[264,256]{1,0:T(8,128)(2,1)S(1)} %get-tuple-element.60), channel_id=1, source_target_pairs={{0,2},{1,3},{2,0},{3,1},{4,6},{5,7},{6,4},{7,5},{8,10},{9,11},{10,... | collective-permute-start | bytes 405512 | tf_op jit(solution)/shard_map/ppermute | solution.py:493
  42.9 0.0 collective-permute-start.7
  42.9 0.0 collective-permute-done.10.refs_6_
  42.9 2.7 %collective-permute-start.8 = (s16[264,256]{1,0:T(8,128)(2,1)S(1)}, s16[264,256]{1,0:T(8,128)(2,1)S(1)}, u32[]{:S(2)}, u32[]{:S(2)}) collective-permute-start(s16[264,256]{1,0:T(8,128)(2,1)S(1)} %get-tuple-element.62), channel_id=1, source_target_pairs={{0,3},{1,0},{2,1},{3,2},{4,7},{5,4},{6,5},{7,6},{8,11},{9,8},{10,9... | collective-permute-start | bytes 405512 | tf_op jit(solution)/shard_map/ppermute | solution.py:493
  45.5 0.0 collective-permute-done.11.refs_7_
  45.6 0.0 collective-permute-done.9.refs_5_
  45.6 0.0 collective-permute-done.6.refs_1_
  45.6 4.5 %collective-permute-done.7.refs_2_ = s16[264,256]{1,0:T(8,128)(2,1)S(1)} collective-permute-done((s16[264,256]{1,0:T(8,128)(2,1)S(1)}, s16[264,256]{1,0:T(8,128)(2,1)S(1)}, u32[]{:S(2)}, u32[]{:S(2)}) %collective-permute-start.7) | collective-permute-done | bytes 135200 | tf_op jit(solution)/shard_map/ppermute | solution.py:493
  50.1 0.0 collective-permute-done.8.refs_3_
  50.1 0.4 last.1
  50.5 1.3 %collective-permute-start.12 = (s16[2,264,256]{2,1,0:T(8,128)(2,1)S(1)}, s16[2,264,256]{2,1,0:T(8,128)(2,1)S(1)}, u32[]{:S(2)}, u32[]{:S(2)}) collective-permute-start(s16[2,264,256]{2,1,0:T(8,128)(2,1)S(1)} %get-tuple-element.72), channel_id=1, source_target_pairs={{0,1},{1,2},{2,3},{3,4},{4,5},{5,6},{6,7},{7,8},{8,9},{9,10},{10,1... | collective-permute-start | bytes 811016 | tf_op jit(solution)/shard_map/ppermute | solution.py:530
  51.8 1.3 %collective-permute-start.13 = (f32[2,16,256]{2,1,0:T(8,128)S(1)}, f32[2,16,256]{2,1,0:T(8,128)S(1)}, u32[]{:S(2)}, u32[]{:S(2)}) collective-permute-start(f32[2,16,256]{2,1,0:T(8,128)S(1)} %get-tuple-element.73), channel_id=1, source_target_pairs={{1,0},{2,1},{3,2},{4,3},{5,4},{6,5},{7,6},{8,7},{9,8},{10,9},{11,1... | collective-permute-start | bytes 98312 | tf_op jit(solution)/shard_map/ppermute | solution.py:531
  53.1 3.4 %collective-permute-done.13.after_ref = f32[2,16,256]{2,1,0:T(8,128)S(1)} collective-permute-done((f32[2,16,256]{2,1,0:T(8,128)S(1)}, f32[2,16,256]{2,1,0:T(8,128)S(1)}, u32[]{:S(2)}, u32[]{:S(2)}) %collective-permute-start.13) | collective-permute-done | bytes 32800 | tf_op jit(solution)/shard_map/ppermute | solution.py:531
  56.4 0.0 collective-permute-done.12.before_ref
  56.4 0.0 copy-done.1
  56.4 0.0 copy-done.3
  56.5 8.8 %filter_and_fold.1 = (bf16[2,256,256]{2,1,0:T(8,128)(2,1)S(1)}, f32[1,128]{1,0:T(1,128)}, f32[128,128]{1,0:T(8,128)}) custom-call(s32[1]{0:T(128)S(6)} %copy.25.offset, f32[2,256,256]{2,1,0:T(8,128)S(1)} %get-tuple-element.71.own_ref, s16[2,264,256]{2,1,0:T(8,128)(2,1)S(1)} %collective-permute-done.12.before_ref, ...), custom_call_target="tpu_custom_call" | custom-call | tf_op jit(solution)/shard_map/filter_and_fold/pallas_call | solution.py:477
  65.3 15.2 %all-to-all-start = ((f32[128,1,128]{2,1,0:T(1,128)}), f32[128,1,128]{2,1,0:T(1,128)S(1)}, u32[]{:S(2)}, u32[]{:S(2)}) async-start(f32[128,1,128]{2,1,0:T(1,128)} %bitcast.11), calls=%async_computation | async-start | bytes 131072 | tf_op jit(solution)/shard_map/all_to_all | solution.py:539
  80.5 0.8 reshape.33
  81.3 8.8 %all-to-all-done = f32[128,1,128]{2,1,0:T(1,128)S(1)} async-done(((f32[128,1,128]{2,1,0:T(1,128)}), f32[128,1,128]{2,1,0:T(1,128)S(1)}, u32[]{:S(2)}, u32[]{:S(2)}) %all-to-all-start) | async-done | bytes 65568 | tf_op jit(solution)/shard_map/all_to_all | solution.py:539
  90.1 0.5 constant_dynamic-slice_fusion
  90.6 0.7 reduce_sum.19
  (12 shorter events, 0.0 us)
Async XLA Ops:
  0.6 0.7 copy-start.7
  4.5 15.5 %collective-permute-start = (s16[4,264,256]{2,1,0:T(8,128)(2,1)S(1)}, s16[4,264,256]{2,1,0:T(8,128)(2,1)S(1)}, u32[]{:S(2)}, u32[]{:S(2)}) collective-permute-start(s16[4,264,256]{2,1,0:T(8,128)(2,1)S(1)} %get-tuple-element.43), channel_id=1, source_target_pairs={{0,8},{1,9},{2,10},{3,11},{4,12},{5,13},{6,14},{7,15},{8,0},{9,1},... | collective-permute-start | bytes 1622024 | tf_op jit(solution)/shard_map/ppermute | solution.py:493
  8.3 14.9 %collective-permute-start.1 = (s16[4,264,256]{2,1,0:T(8,128)(2,1)S(1)}, s16[4,264,256]{2,1,0:T(8,128)(2,1)S(1)}, u32[]{:S(2)}, u32[]{:S(2)}) collective-permute-start(s16[4,264,256]{2,1,0:T(8,128)(2,1)S(1)} %get-tuple-element.44), channel_id=1, source_target_pairs={{0,2},{1,3},{2,0},{3,1},{4,6},{5,7},{6,4},{7,5},{8,10},{9,11},{10,... | collective-permute-start | bytes 1622024 | tf_op jit(solution)/shard_map/ppermute | solution.py:493
  11.1 15.6 %copy-start.2 = (f32[1,131072]{1,0:T(1,128)S(1)}, f32[1,131072]{1,0:T(1,128)}, u32[]{:S(2)}) copy-start(f32[1,131072]{1,0:T(1,128)} %param.14) | copy-start | bytes 1572868
  11.1 45.4 %copy-start = (bf16[4,2,256,256]{3,2,1,0:T(8,128)(2,1)S(1)}, bf16[4,2,256,256]{3,2,1,0:T(8,128)(2,1)}, u32[]{:S(2)}) copy-start(bf16[4,2,256,256]{3,2,1,0:T(8,128)(2,1)} %constant.24.clone.rows_forward) | copy-start | bytes 3145732
  11.1 45.4 %copy-start.1 = (bf16[4,2,256,256]{3,2,1,0:T(8,128)(2,1)S(1)}, bf16[4,2,256,256]{3,2,1,0:T(8,128)(2,1)}, u32[]{:S(2)}) copy-start(bf16[4,2,256,256]{3,2,1,0:T(8,128)(2,1)} %constant.27.clone.rows_back) | copy-start | bytes 3145732
  11.1 45.4 %copy-start.3 = (bf16[2,2,256,256]{3,2,1,0:T(8,128)(2,1)S(1)}, bf16[2,2,256,256]{3,2,1,0:T(8,128)(2,1)}, u32[]{:S(2)}) copy-start(bf16[2,2,256,256]{3,2,1,0:T(8,128)(2,1)} %constant.25.clone.columns_forward) | copy-start | bytes 1572868
  11.1 45.4 %copy-start.4 = (bf16[2,2,256,256]{3,2,1,0:T(8,128)(2,1)S(1)}, bf16[2,2,256,256]{3,2,1,0:T(8,128)(2,1)}, u32[]{:S(2)}) copy-start(bf16[2,2,256,256]{3,2,1,0:T(8,128)(2,1)} %constant.26.clone.columns_back) | copy-start | bytes 1572868
  11.1 45.4 %copy-start.5 = (s32[65536]{0:T(1024)S(1)}, s32[65536]{0:T(1024)}, u32[]{:S(2)}) copy-start(s32[65536]{0:T(1024)} %param.17) | copy-start | bytes 786436
  11.1 45.4 %copy-start.6 = (f32[256,256]{1,0:T(8,128)S(1)}, f32[256,256]{1,0:T(8,128)}, u32[]{:S(2)}) copy-start(f32[256,256]{1,0:T(8,128)} %constant.29.clone.group) | copy-start | bytes 786436
  11.1 45.4 %copy-start.8 = (s32[1,64]{1,0:T(1,128)S(1)}, s32[1,64]{1,0:T(1,128)}, u32[]{:S(2)}) copy-start(s32[1,64]{1,0:T(1,128)} %flags_ref.1) | copy-start | bytes 772
  16.5 15.6 %collective-permute-start.2 = (s16[4,264,256]{2,1,0:T(8,128)(2,1)S(1)}, s16[4,264,256]{2,1,0:T(8,128)(2,1)S(1)}, u32[]{:S(2)}, u32[]{:S(2)}) collective-permute-start(s16[4,264,256]{2,1,0:T(8,128)(2,1)S(1)} %get-tuple-element.46), channel_id=1, source_target_pairs={{0,4},{1,5},{2,6},{3,7},{4,8},{5,9},{6,10},{7,11},{8,12},{9,13},{1... | collective-permute-start | bytes 1622024 | tf_op jit(solution)/shard_map/ppermute | solution.py:493
  16.9 15.1 %collective-permute-start.3 = (s16[4,264,256]{2,1,0:T(8,128)(2,1)S(1)}, s16[4,264,256]{2,1,0:T(8,128)(2,1)S(1)}, u32[]{:S(2)}, u32[]{:S(2)}) collective-permute-start(s16[4,264,256]{2,1,0:T(8,128)(2,1)S(1)} %get-tuple-element.47), channel_id=1, source_target_pairs={{0,12},{1,13},{2,14},{3,15},{4,0},{5,1},{6,2},{7,3},{8,4},{9,5},{1... | collective-permute-start | bytes 1622024 | tf_op jit(solution)/shard_map/ppermute | solution.py:493
  19.2 15.5 %collective-permute-start.4 = (s16[4,264,256]{2,1,0:T(8,128)(2,1)S(1)}, s16[4,264,256]{2,1,0:T(8,128)(2,1)S(1)}, u32[]{:S(2)}, u32[]{:S(2)}) collective-permute-start(s16[4,264,256]{2,1,0:T(8,128)(2,1)S(1)} %get-tuple-element.51), channel_id=1, source_target_pairs={{0,1},{1,2},{2,3},{3,0},{4,5},{5,6},{6,7},{7,4},{8,9},{9,10},{10,1... | collective-permute-start | bytes 1622024 | tf_op jit(solution)/shard_map/ppermute | solution.py:493
  20.0 14.7 %collective-permute-start.5 = (s16[4,264,256]{2,1,0:T(8,128)(2,1)S(1)}, s16[4,264,256]{2,1,0:T(8,128)(2,1)S(1)}, u32[]{:S(2)}, u32[]{:S(2)}) collective-permute-start(s16[4,264,256]{2,1,0:T(8,128)(2,1)S(1)} %get-tuple-element.52), channel_id=1, source_target_pairs={{0,3},{1,0},{2,1},{3,2},{4,7},{5,4},{6,5},{7,6},{8,11},{9,8},{10,9... | collective-permute-start | bytes 1622024 | tf_op jit(solution)/shard_map/ppermute | solution.py:493
  35.5 7.4 %collective-permute-start.10 = (s16[264,256]{1,0:T(8,128)(2,1)S(1)}, s16[264,256]{1,0:T(8,128)(2,1)S(1)}, u32[]{:S(2)}, u32[]{:S(2)}) collective-permute-start(s16[264,256]{1,0:T(8,128)(2,1)S(1)} %get-tuple-element.69), channel_id=1, source_target_pairs={{0,4},{1,5},{2,6},{3,7},{4,8},{5,9},{6,10},{7,11},{8,12},{9,13},{1... | collective-permute-start | bytes 405512 | tf_op jit(solution)/shard_map/ppermute | solution.py:493
  36.1 9.5 %collective-permute-start.11 = (s16[264,256]{1,0:T(8,128)(2,1)S(1)}, s16[264,256]{1,0:T(8,128)(2,1)S(1)}, u32[]{:S(2)}, u32[]{:S(2)}) collective-permute-start(s16[264,256]{1,0:T(8,128)(2,1)S(1)} %get-tuple-element.70), channel_id=1, source_target_pairs={{0,12},{1,13},{2,14},{3,15},{4,0},{5,1},{6,2},{7,3},{8,4},{9,5},{1... | collective-permute-start | bytes 405512 | tf_op jit(solution)/shard_map/ppermute | solution.py:493
  38.2 7.3 %collective-permute-start.9 = (s16[264,256]{1,0:T(8,128)(2,1)S(1)}, s16[264,256]{1,0:T(8,128)(2,1)S(1)}, u32[]{:S(2)}, u32[]{:S(2)}) collective-permute-start(s16[264,256]{1,0:T(8,128)(2,1)S(1)} %get-tuple-element.68), channel_id=1, source_target_pairs={{0,8},{1,9},{2,10},{3,11},{4,12},{5,13},{6,14},{7,15},{8,0},{9,1},... | collective-permute-start | bytes 405512 | tf_op jit(solution)/shard_map/ppermute | solution.py:493
  39.0 6.6 %collective-permute-start.6 = (s16[264,256]{1,0:T(8,128)(2,1)S(1)}, s16[264,256]{1,0:T(8,128)(2,1)S(1)}, u32[]{:S(2)}, u32[]{:S(2)}) collective-permute-start(s16[264,256]{1,0:T(8,128)(2,1)S(1)} %get-tuple-element.60), channel_id=1, source_target_pairs={{0,2},{1,3},{2,0},{3,1},{4,6},{5,7},{6,4},{7,5},{8,10},{9,11},{10,... | collective-permute-start | bytes 405512 | tf_op jit(solution)/shard_map/ppermute | solution.py:493
  42.9 7.2 %collective-permute-start.7 = (s16[264,256]{1,0:T(8,128)(2,1)S(1)}, s16[264,256]{1,0:T(8,128)(2,1)S(1)}, u32[]{:S(2)}, u32[]{:S(2)}) collective-permute-start(s16[264,256]{1,0:T(8,128)(2,1)S(1)} %get-tuple-element.61), channel_id=1, source_target_pairs={{0,1},{1,2},{2,3},{3,0},{4,5},{5,6},{6,7},{7,4},{8,9},{9,10},{10,1... | collective-permute-start | bytes 405512 | tf_op jit(solution)/shard_map/ppermute | solution.py:493
  42.9 7.2 %collective-permute-start.8 = (s16[264,256]{1,0:T(8,128)(2,1)S(1)}, s16[264,256]{1,0:T(8,128)(2,1)S(1)}, u32[]{:S(2)}, u32[]{:S(2)}) collective-permute-start(s16[264,256]{1,0:T(8,128)(2,1)S(1)} %get-tuple-element.62), channel_id=1, source_target_pairs={{0,3},{1,0},{2,1},{3,2},{4,7},{5,4},{6,5},{7,6},{8,11},{9,8},{10,9... | collective-permute-start | bytes 405512 | tf_op jit(solution)/shard_map/ppermute | solution.py:493
  50.5 6.0 %collective-permute-start.12 = (s16[2,264,256]{2,1,0:T(8,128)(2,1)S(1)}, s16[2,264,256]{2,1,0:T(8,128)(2,1)S(1)}, u32[]{:S(2)}, u32[]{:S(2)}) collective-permute-start(s16[2,264,256]{2,1,0:T(8,128)(2,1)S(1)} %get-tuple-element.72), channel_id=1, source_target_pairs={{0,1},{1,2},{2,3},{3,4},{4,5},{5,6},{6,7},{7,8},{8,9},{9,10},{10,1... | collective-permute-start | bytes 811016 | tf_op jit(solution)/shard_map/ppermute | solution.py:530
  51.8 4.7 %collective-permute-start.13 = (f32[2,16,256]{2,1,0:T(8,128)S(1)}, f32[2,16,256]{2,1,0:T(8,128)S(1)}, u32[]{:S(2)}, u32[]{:S(2)}) collective-permute-start(f32[2,16,256]{2,1,0:T(8,128)S(1)} %get-tuple-element.73), channel_id=1, source_target_pairs={{1,0},{2,1},{3,2},{4,3},{5,4},{6,5},{7,6},{8,7},{9,8},{10,9},{11,1... | collective-permute-start | bytes 98312 | tf_op jit(solution)/shard_map/ppermute | solution.py:531
  65.3 24.8 %all-to-all-start = ((f32[128,1,128]{2,1,0:T(1,128)}), f32[128,1,128]{2,1,0:T(1,128)S(1)}, u32[]{:S(2)}, u32[]{:S(2)}) async-start(f32[128,1,128]{2,1,0:T(1,128)} %bitcast.11), calls=%async_computation | async-start | bytes 131072 | tf_op jit(solution)/shard_map/all_to_all | solution.py:539

commit v5 on v4

--- a/solution.py
+++ b/solution.py
@@ -239,28 +239,27 @@
 
 
 def last_body(*refs):
-    parts, (own, ahead, behind) = refs[:8], refs[8:]
-    for half in (0, 1):
-        mine = parts[half * 4]
-        total = [mine[0], mine[1]]
-        for part in parts[half * 4 + 1 : half * 4 + 4]:
-            more = decode(part)
-            total = [total[0] + more[0], total[1] + more[1]]
-        rows = pl.ds(half * 128, 128)
-        own[0, rows], own[1, rows] = total
-        ahead[half, 0:128], ahead[half, 128:256], ahead[half, 256:264] = encode(*total)
-        if half == 0:
-            behind[0], behind[1] = total[0][0:16], total[1][0:16]
-
-
-def last(parts):
+    parts, outs = refs[:4], refs[4:]
+    total = [parts[0][0], parts[0][1]]
+    for part in parts[1:]:
+        more = decode(part)
+        total = [total[0] + more[0], total[1] + more[1]]
+    own, ahead = outs[:2]
+    own[0], own[1] = total
+    ahead[0:128], ahead[128:256], ahead[256:264] = encode(*total)
+    if len(outs) > 2:
+        outs[2][0], outs[2][1] = total[0][0:16], total[1][0:16]
+
+
+def last(parts, half):
+    behind = (jax.ShapeDtypeStruct((2, 16, SIDE), F32),) if half == 0 else ()
     return pl.pallas_call(
         last_body,
         out_shape=(
-            jax.ShapeDtypeStruct((2, SIDE, SIDE), F32),
-            jax.ShapeDtypeStruct((2, ROWS, SIDE), jnp.int16),
-            jax.ShapeDtypeStruct((2, 16, SIDE), F32),
-        ),
+            jax.ShapeDtypeStruct((2, 128, SIDE), F32),
+            jax.ShapeDtypeStruct((ROWS, SIDE), jnp.int16),
+        )
+        + behind,
         compiler_params=pltpu.CompilerParams(vmem_limit_bytes=16 * 1024 * 1024),
         name="last",
     )(*parts)
@@ -346,12 +345,15 @@
 
 def main_body(
     offset,
-    own_ref,
-    before_ref,
+    own_first,
+    own_last,
+    before_first,
+    before_last,
     after_ref,
     response,
     flags_ref,
-    bins_ref,
+    high_marks,
+    low_marks,
     rows_forward,
     columns_forward,
     columns_back,
@@ -361,16 +363,13 @@
     out_ref,
     weight_ref,
     profile_ref,
-    high_ref,
-    low_ref,
     value_ref,
     total_ref,
 ):
-    own = [own_ref[0], own_ref[1]]
     row = lax.broadcasted_iota(jnp.int32, (16, SIDE), 0)
     col = lax.broadcasted_iota(jnp.int32, (16, SIDE), 1)
     wrapped = row * SIDE + col < offset[0]
-    earlier = [decode(before_ref, 0), decode(before_ref, 1)]
+    earlier = [decode(before_first), decode(before_last)]
     before = []
     for comp in (0, 1):
         head = jnp.where(wrapped, after_ref[comp], earlier[0][comp][0:16])
@@ -378,8 +377,8 @@
     quarters = [
         tuple(before),
         tuple(earlier[1]),
-        (own_ref[0, 0:QUARTER, :], own_ref[1, 0:QUARTER, :]),
-        (own_ref[0, QUARTER:, :], own_ref[1, QUARTER:, :]),
+        (own_first[0], own_first[1]),
+        (own_last[0], own_last[1]),
     ]
     sums, differences = [], []
     for r, pair in enumerate(four_point(quarters, -1)):
@@ -431,31 +430,17 @@
         jnp.concatenate([weight, weight], axis=1) * power
     ).astype(BF16).astype(F32)
 
-    for side in (0, 1):
-        bins = bins_ref[pl.ds(side, SIDE, stride=2), :]
-        lanes = slice(side * LANES, side * LANES + LANES)
-        high_ref[:, lanes] = (bins // LOW_BINS).astype(F32)
-        low_ref[:, lanes] = (bins % LOW_BINS).astype(F32)
-
-    per_step = 32
-    rows = lax.broadcasted_iota(jnp.int32, (LOW_BINS, SIDE), 0).astype(F32).astype(BF16)
-    one, zero = jnp.ones((), BF16), jnp.zeros((), BF16)
+    per_step = 64
 
     def fold(step, total):
         start = pl.multiple_of(step * per_step, per_step)
-        blocks = [
-            ref[pl.ds(start, per_step), :] for ref in (high_ref, low_ref, value_ref)
-        ]
+        block = value_ref[pl.ds(start, per_step), :]
         spreads, marks = [], []
         for r in range(per_step):
-            high, low, value = [
-                jnp.broadcast_to(block[r : r + 1], (16, SIDE)).astype(BF16) for block in blocks
-            ]
-            high = jnp.concatenate([high] * (HIGH_BINS // 16), axis=0)
+            value = jnp.broadcast_to(block[r : r + 1], (16, SIDE)).astype(BF16)
             value = jnp.concatenate([value] * (HIGH_BINS // 16), axis=0)
-            low = jnp.concatenate([low] * (LOW_BINS // 16), axis=0)
-            spreads.append(jnp.where(high == rows[:HIGH_BINS], value, zero))
-            marks.append(jnp.where(low == rows, one, zero))
+            spreads.append(high_marks[start + r] * value)
+            marks.append(low_marks[start + r])
         return total + lax.dot_general(
             jnp.concatenate(spreads, axis=1),
             jnp.concatenate(marks, axis=1),
@@ -472,21 +457,71 @@
         profile_ref[pl.ds(channel * N_TM, N_TM), :] = own
 
 
-def filter_and_fold(offset, own, before, after, response, flags, bins, tables):
+def mark_body(bins_ref, high_marks, low_marks, high_ref, low_ref):
+    for side in (0, 1):
+        bins = bins_ref[pl.ds(side, SIDE, stride=2), :]
+        lanes = slice(side * LANES, side * LANES + LANES)
+        high_ref[:, lanes] = (bins // LOW_BINS).astype(F32)
+        low_ref[:, lanes] = (bins % LOW_BINS).astype(F32)
+    per_step = 16
+    rows = lax.broadcasted_iota(jnp.int32, (LOW_BINS, SIDE), 0).astype(F32).astype(BF16)
+    one, zero = jnp.ones((), BF16), jnp.zeros((), BF16)
+
+    def mark(step, carry):
+        start = pl.multiple_of(step * per_step, per_step)
+        for ref, out, count in (
+            (high_ref, high_marks, HIGH_BINS),
+            (low_ref, low_marks, LOW_BINS),
+        ):
+            block = ref[pl.ds(start, per_step), :]
+            for r in range(per_step):
+                wide = jnp.broadcast_to(block[r : r + 1], (16, SIDE)).astype(BF16)
+                wide = jnp.concatenate([wide] * (count // 16), axis=0)
+                out[start + r] = jnp.where(wide == rows[:count], one, zero)
+        return carry
+
+    lax.fori_loop(0, SIDE // per_step, mark, 0)
+
+
+def mark_bins(bins):
+    return pl.pallas_call(
+        mark_body,
+        out_shape=(
+            jax.ShapeDtypeStruct((SIDE, HIGH_BINS, SIDE), BF16),
+            jax.ShapeDtypeStruct((SIDE, LOW_BINS, SIDE), BF16),
+        ),
+        scratch_shapes=[pltpu.VMEM((SIDE, SIDE), F32)] * 2,
+        compiler_params=pltpu.CompilerParams(vmem_limit_bytes=16 * 1024 * 1024),
+        name="mark_bins",
+    )(bins)
+
+
+def filter_and_fold(offset, own_first, own_last, before_first, before_last, after, response, flags, marks, tables):
     vmem = pl.BlockSpec(memory_space=pltpu.VMEM)
     return pl.pallas_call(
         main_body,
-        in_specs=[pl.BlockSpec(memory_space=pltpu.SMEM)] + [vmem] * (6 + len(tables)),
+        in_specs=[pl.BlockSpec(memory_space=pltpu.SMEM)] + [vmem] * (9 + len(tables)),
         out_shape=(
             jax.ShapeDtypeStruct((2, SIDE, SIDE), BF16),
             jax.ShapeDtypeStruct((1, LANES), F32),
             jax.ShapeDtypeStruct((CHANNELS * N_TM, LANES), F32),
         ),
-        scratch_shapes=[pltpu.VMEM((SIDE, SIDE), F32)] * 3
+        scratch_shapes=[pltpu.VMEM((SIDE, SIDE), F32)]
         + [pltpu.VMEM((HIGH_BINS, LANES), F32)],
-        compiler_params=pltpu.CompilerParams(vmem_limit_bytes=48 * 1024 * 1024),
+        compiler_params=pltpu.CompilerParams(vmem_limit_bytes=20 * 1024 * 1024),
         name="filter_and_fold",
-    )(offset, own, before, after, response, flags, bins, *tables)
+    )(
+        offset,
+        own_first,
+        own_last,
+        before_first,
+        before_last,
+        after,
+        response,
+        flags,
+        *marks,
+        *tables,
+    )
 
 
 def send(value, down, across):
@@ -526,13 +561,19 @@
         made = middle(got[half], order)
         for step, value in zip(order, made):
             landed[half].append(second_send(half, step, value) if step else value)
-    own, ahead, behind = last([landed[half][i] for half in (0, 1) for i in (3, 0, 1, 2)])
-    before = lax.ppermute(ahead, "tm", [(s, s + 1) for s in range(N_TM - 1)])
-    after = lax.ppermute(behind, "tm", [(s + 1, s) for s in range(N_TM - 1)])
-
-    bins = sample_phase_bins.reshape(512, LANES)
+    forward = [(s, s + 1) for s in range(N_TM - 1)]
+    own, before = [], []
+    for half in (0, 1):
+        mine, ahead, *behind = last([landed[half][i] for i in (3, 0, 1, 2)], half)
+        own.append(mine)
+        before.append(lax.ppermute(ahead, "tm", forward))
+        if behind:
+            after = lax.ppermute(behind[0], "tm", [(s + 1, s) for s in range(N_TM - 1)])
+            landed[1], after = lax.optimization_barrier((landed[1], after))
+
+    marks = mark_bins(sample_phase_bins.reshape(512, LANES))
     filtered, weight, partial_profile = filter_and_fold(
-        offsets, own, before, after, response, flags, bins, tables
+        offsets, *own, *before, after, response, flags, marks, tables
     )
     dedispersed = filtered.reshape(2, 1, HALF)
     sk_weight = weight[:, :64]

time: 91.5 us -> 88.7 us (0.969)
  waiting for transfers between devices: 23.3 us -> 17.4 us
  starting transfers between devices: 39.2 us -> 42.4 us
    ppermute x2 -> x3, starting transfers between devices: 2.6 us -> 7.81 us  [the longest x2 6.52 us: on_device(): before.append(lax.ppermute(ahead, 'tm', forward))]
    ppermute x12, waiting for transfers between devices: 11.1 us -> 7.04 us  [send(): return lax.ppermute(value, 'tm', steps(down, across))]
    all_to_all x1, starting transfers between devices: 15.2 us -> 13.1 us  [on_device(): arrived = lax.all_to_all(partial_profile, ('chan', 'tm'), 0, 0, tiled=True)]
    pallas_call x1, Pallas kernels: 8.78 us -> 6.76 us  [filter_and_fold(): pl.pallas_call(main_body, in_specs=[pl.BlockSpec(memory_space=pltpu.SMEM)...]
    pallas_call x1 -> x3, Pallas kernels: 0.39 us -> 2.19 us  [the longest x1 1.69 us: mark_bins(): pl.pallas_call(mark_body, out_shape=(jax.ShapeDtypeStruct((SIDE, HIGH_BIN...]
    ppermute x2 -> x3, waiting for transfers between devices: 3.36 us -> 1.6 us  [the longest x2 1.6 us: on_device(): before.append(lax.ppermute(ahead, 'tm', forward))]
  transfers between devices with their start and end apart: 15 -> 16, of which waited for: 6 -> 7; matrix products, arithmetic and copies ran while one was open for 1% -> 1% of each run, Pallas kernels for 13% -> 15%
where the time goes in v5:
time: 88.7 us; the launch traced here: 88.5 us
  starting transfers between devices  42.4 us (48%)
  Pallas kernels  24.4 us (28%)
  waiting for transfers between devices  17.4 us (20%)
  local copies, waits for them, and re-layouts  2.03 us (2%)
  between operations  1.57 us (2%)
    ppermute x12, starting transfers between devices, send(): return lax.ppermute(value, 'tm', steps(down, across))  21.5 us
    all_to_all x1, starting transfers between devices, on_device(): arrived = lax.all_to_all(partial_profile, ('chan', 'tm'), 0, 0, tiled=True)  13.1 us
    pallas_call x3, Pallas kernels, beamform(): pl.pallas_call(lambda *refs: beam_body(messages, *refs), in_specs=[pl.Blo...  11.9 us
    all_to_all x1, waiting for transfers between devices, on_device(): arrived = lax.all_to_all(partial_profile, ('chan', 'tm'), 0, 0, tiled=True)  8.8 us
    ppermute x12, waiting for transfers between devices, send(): return lax.ppermute(value, 'tm', steps(down, across))  7.04 us
    pallas_call x1, Pallas kernels, filter_and_fold(): pl.pallas_call(main_body, in_specs=[pl.BlockSpec(memory_space=pltpu.SMEM)...  6.76 us
    ppermute x2, starting transfers between devices, on_device(): before.append(lax.ppermute(ahead, 'tm', forward))  6.52 us
    pallas_call x1, Pallas kernels, make_response(): pl.pallas_call(response_body, in_specs=[pl.BlockSpec(memory_space=pltpu.S...  2.05 us
  transfers between devices with their start and end apart: 16, of which 7 were waited for; matrix products, arithmetic and copies ran while one was open for 1% of the time, Pallas kernels for 15%

profile of v5, /device:TPU:1, one launch (start us, length us, event | category | flops | bytes accessed | tf_op | source)
XLA Modules:
  0.0 88.5 jit_solution(10838349176047170146)
XLA Ops:
  0.6 0.7 copy-done.8
  1.3 3.2 %beamform.3 = (s16[4,264,256]{2,1,0:T(8,128)(2,1)S(1)}, s16[4,264,256]{2,1,0:T(8,128)(2,1)S(1)}, f32[8,128]{1,0:T(8,128)S(1)}) custom-call(f32[2,1,64]{2,1,0:T(1,128)S(1)} %bitcast.19, bf16[2,32768,128]{2,1,0:T(8,128)(2,1)} %bitcast.22), custom_call_target="tpu_custom_call" | custom-call | tf_op jit(solution)/shard_map/beamform/pallas_call | solution.py:193
  4.5 3.8 %collective-permute-start = (s16[4,264,256]{2,1,0:T(8,128)(2,1)S(1)}, s16[4,264,256]{2,1,0:T(8,128)(2,1)S(1)}, u32[]{:S(2)}, u32[]{:S(2)}) collective-permute-start(s16[4,264,256]{2,1,0:T(8,128)(2,1)S(1)} %get-tuple-element.52), channel_id=1, source_target_pairs={{0,8},{1,9},{2,10},{3,11},{4,12},{5,13},{6,14},{7,15},{8,0},{9,1},... | collective-permute-start | bytes 1622024 | tf_op jit(solution)/shard_map/ppermute | solution.py:528
  8.3 2.7 %collective-permute-start.1 = (s16[4,264,256]{2,1,0:T(8,128)(2,1)S(1)}, s16[4,264,256]{2,1,0:T(8,128)(2,1)S(1)}, u32[]{:S(2)}, u32[]{:S(2)}) collective-permute-start(s16[4,264,256]{2,1,0:T(8,128)(2,1)S(1)} %get-tuple-element.53), channel_id=1, source_target_pairs={{0,2},{1,3},{2,0},{3,1},{4,6},{5,7},{6,4},{7,5},{8,10},{9,11},{10,... | collective-permute-start | bytes 1622024 | tf_op jit(solution)/shard_map/ppermute | solution.py:528
  11.1 5.2 %beamform.4 = (s16[4,264,256]{2,1,0:T(8,128)(2,1)S(1)}, s16[4,264,256]{2,1,0:T(8,128)(2,1)S(1)}, s16[4,264,256]{2,1,0:T(8,128)(2,1)S(1)}, s16[4,264,256]{2,1,0:T(8,128)(2,1)S(1)}, f32[8,128]{1,0:T(8,128)S(1)}) custom-call(f32[2,1,64]{2,1,0:T(1,128)S(1)} %bitcast.20, bf16[2,32768,128]{2,1,0:T(8,128)(2,1)} %bitcast.23, f32[8,128]{1,0:T(8,128)S(1)} %get-tuple-element.50.refs_2_), custom_call_target="tpu_custom_call" | custom-call | tf_op jit(solution)/shard_map/beamform/pallas_call | solution.py:193
  16.2 0.5 collective-permute-start.2
  16.7 2.3 %collective-permute-start.3 = (s16[4,264,256]{2,1,0:T(8,128)(2,1)S(1)}, s16[4,264,256]{2,1,0:T(8,128)(2,1)S(1)}, u32[]{:S(2)}, u32[]{:S(2)}) collective-permute-start(s16[4,264,256]{2,1,0:T(8,128)(2,1)S(1)} %get-tuple-element.56), channel_id=1, source_target_pairs={{0,12},{1,13},{2,14},{3,15},{4,0},{5,1},{6,2},{7,3},{8,4},{9,5},{1... | collective-permute-start | bytes 1622024 | tf_op jit(solution)/shard_map/ppermute | solution.py:528
  19.0 0.3 collective-permute-start.4
  19.3 0.8 collective-permute-done.refs_0_
  20.0 2.5 %collective-permute-start.5 = (s16[4,264,256]{2,1,0:T(8,128)(2,1)S(1)}, s16[4,264,256]{2,1,0:T(8,128)(2,1)S(1)}, u32[]{:S(2)}, u32[]{:S(2)}) collective-permute-start(s16[4,264,256]{2,1,0:T(8,128)(2,1)S(1)} %get-tuple-element.61), channel_id=1, source_target_pairs={{0,3},{1,0},{2,1},{3,2},{4,7},{5,4},{6,5},{7,6},{8,11},{9,8},{10,9... | collective-permute-start | bytes 1622024 | tf_op jit(solution)/shard_map/ppermute | solution.py:528
  23.2 0.0 copy-start.5
  23.2 0.0 copy-start.7
  23.2 0.0 copy-start
  23.2 0.0 copy-start.1
  23.2 0.0 copy-start.2
  23.2 0.0 copy-start.3
  23.3 0.0 copy-start.4
  23.3 0.0 copy-start.6
  23.3 0.0 copy-start.9
  23.3 3.6 %beamform.5 = (s16[4,264,256]{2,1,0:T(8,128)(2,1)S(1)}, s16[4,264,256]{2,1,0:T(8,128)(2,1)S(1)}, f32[8,128]{1,0:T(8,128)}) custom-call(f32[2,1,64]{2,1,0:T(1,128)S(1)} %bitcast.21, bf16[2,32768,128]{2,1,0:T(8,128)(2,1)} %bitcast.24, f32[8,128]{1,0:T(8,128)S(1)} %get-tuple-element.57.refs_2_), custom_call_target="tpu_custom_call" | custom-call | tf_op jit(solution)/shard_map/beamform/pallas_call | solution.py:193
  26.9 2.1 %response.1 = f32[2,2,512,128]{3,2,1,0:T(8,128)S(1)} custom-call(s32[1]{0:T(128)S(6)} %copy.25.offset, f32[1024,128]{1,0:T(8,128)S(1)} %bitcast.17), custom_call_target="tpu_custom_call" | custom-call | tf_op jit(solution)/shard_map/response/pallas_call | solution.py:287
  28.9 3.0 %collective-permute-done.2.refs_1_ = s16[4,264,256]{2,1,0:T(8,128)(2,1)S(1)} collective-permute-done((s16[4,264,256]{2,1,0:T(8,128)(2,1)S(1)}, s16[4,264,256]{2,1,0:T(8,128)(2,1)S(1)}, u32[]{:S(2)}, u32[]{:S(2)}) %collective-permute-start.2) | collective-permute-done | bytes 540704 | tf_op jit(solution)/shard_map/ppermute | solution.py:528
  31.9 0.1 collective-permute-done.3.refs_2_
  32.0 2.7 %collective-permute-done.4.refs_1_ = s16[4,264,256]{2,1,0:T(8,128)(2,1)S(1)} collective-permute-done((s16[4,264,256]{2,1,0:T(8,128)(2,1)S(1)}, s16[4,264,256]{2,1,0:T(8,128)(2,1)S(1)}, u32[]{:S(2)}, u32[]{:S(2)}) %collective-permute-start.4) | collective-permute-done | bytes 540704 | tf_op jit(solution)/shard_map/ppermute | solution.py:528
  34.6 0.0 collective-permute-done.5.refs_2_
  34.6 0.8 middle.2
  35.4 3.8 %collective-permute-start.6 = (s16[264,256]{1,0:T(8,128)(2,1)S(1)}, s16[264,256]{1,0:T(8,128)(2,1)S(1)}, u32[]{:S(2)}, u32[]{:S(2)}) collective-permute-start(s16[264,256]{1,0:T(8,128)(2,1)S(1)} %get-tuple-element.69), channel_id=1, source_target_pairs={{0,2},{1,3},{2,0},{3,1},{4,6},{5,7},{6,4},{7,5},{8,10},{9,11},{10,... | collective-permute-start | bytes 405512 | tf_op jit(solution)/shard_map/ppermute | solution.py:528
  39.2 0.0 collective-permute-start.7
  39.2 2.7 %collective-permute-start.8 = (s16[264,256]{1,0:T(8,128)(2,1)S(1)}, s16[264,256]{1,0:T(8,128)(2,1)S(1)}, u32[]{:S(2)}, u32[]{:S(2)}) collective-permute-start(s16[264,256]{1,0:T(8,128)(2,1)S(1)} %get-tuple-element.71), channel_id=1, source_target_pairs={{0,3},{1,0},{2,1},{3,2},{4,7},{5,4},{6,5},{7,6},{8,11},{9,8},{10,9... | collective-permute-start | bytes 405512 | tf_op jit(solution)/shard_map/ppermute | solution.py:528
  41.9 0.8 middle.3
  42.6 0.6 collective-permute-start.10
  43.3 2.3 %collective-permute-start.11 = (s16[264,256]{1,0:T(8,128)(2,1)S(1)}, s16[264,256]{1,0:T(8,128)(2,1)S(1)}, u32[]{:S(2)}, u32[]{:S(2)}) collective-permute-start(s16[264,256]{1,0:T(8,128)(2,1)S(1)} %get-tuple-element.79), channel_id=1, source_target_pairs={{0,12},{1,13},{2,14},{3,15},{4,0},{5,1},{6,2},{7,3},{8,4},{9,5},{1... | collective-permute-start | bytes 405512 | tf_op jit(solution)/shard_map/ppermute | solution.py:528
  45.5 0.0 collective-permute-done.6.refs_1_
  45.5 0.0 collective-permute-start.9
  45.5 0.6 collective-permute-done.7.refs_2_
  46.1 0.2 last.2
  46.4 1.3 %collective-permute-start.12 = (f32[2,16,256]{2,1,0:T(8,128)S(1)}, f32[2,16,256]{2,1,0:T(8,128)S(1)}, u32[]{:S(2)}, u32[]{:S(2)}) collective-permute-start(f32[2,16,256]{2,1,0:T(8,128)S(1)} %get-tuple-element.81), channel_id=1, source_target_pairs={{1,0},{2,1},{3,2},{4,3},{5,4},{6,5},{7,6},{8,7},{9,8},{10,9},{11,1... | collective-permute-start | bytes 98312 | tf_op jit(solution)/shard_map/ppermute | solution.py:571
  47.7 4.0 %collective-permute-start.13 = (s16[264,256]{1,0:T(8,128)(2,1)S(1)}, s16[264,256]{1,0:T(8,128)(2,1)S(1)}, u32[]{:S(2)}, u32[]{:S(2)}) collective-permute-start(s16[264,256]{1,0:T(8,128)(2,1)S(1)} %get-tuple-element.87), channel_id=1, source_target_pairs={{0,1},{1,2},{2,3},{3,4},{4,5},{5,6},{6,7},{7,8},{8,9},{9,10},{10,1... | collective-permute-start | bytes 405512 | tf_op jit(solution)/shard_map/ppermute | solution.py:569
  51.7 0.2 last.3
  52.0 2.5 %collective-permute-start.14 = (s16[264,256]{1,0:T(8,128)(2,1)S(1)}, s16[264,256]{1,0:T(8,128)(2,1)S(1)}, u32[]{:S(2)}, u32[]{:S(2)}) collective-permute-start(s16[264,256]{1,0:T(8,128)(2,1)S(1)} %get-tuple-element.88), channel_id=1, source_target_pairs={{0,1},{1,2},{2,3},{3,4},{4,5},{5,6},{6,7},{7,8},{8,9},{9,10},{10,1... | collective-permute-start | bytes 405512 | tf_op jit(solution)/shard_map/ppermute | solution.py:569
  54.5 1.7 %mark_bins.1 = (bf16[256,32,256]{2,1,0:T(8,128)(2,1)S(1)}, bf16[256,64,256]{2,1,0:T(8,128)(2,1)S(1)}) custom-call(s32[512,128]{1,0:T(8,128)S(1)} %bitcast.18), custom_call_target="tpu_custom_call" | custom-call | tf_op jit(solution)/shard_map/mark_bins/pallas_call | solution.py:487
  56.2 1.6 %collective-permute-done.14.before_last = s16[264,256]{1,0:T(8,128)(2,1)S(1)} collective-permute-done((s16[264,256]{1,0:T(8,128)(2,1)S(1)}, s16[264,256]{1,0:T(8,128)(2,1)S(1)}, u32[]{:S(2)}, u32[]{:S(2)}) %collective-permute-start.14) | collective-permute-done | bytes 135200 | tf_op jit(solution)/shard_map/ppermute | solution.py:569
  57.9 6.8 %filter_and_fold.1 = (bf16[2,256,256]{2,1,0:T(8,128)(2,1)S(1)}, f32[1,128]{1,0:T(1,128)}, f32[128,128]{1,0:T(8,128)}) custom-call(s32[1]{0:T(128)S(6)} %copy.25.offset, f32[2,128,256]{2,1,0:T(8,128)S(1)} %get-tuple-element.72.own_first, f32[2,128,256]{2,1,0:T(8,128)S(1)} %get-tuple-element.86.own_last, ...), custom_call_target="tpu_custom_call" | custom-call | tf_op jit(solution)/shard_map/filter_and_fold/pallas_call | solution.py:501
  64.6 13.1 %all-to-all-start = ((f32[128,1,128]{2,1,0:T(1,128)}), f32[128,1,128]{2,1,0:T(1,128)S(1)}, u32[]{:S(2)}, u32[]{:S(2)}) async-start(f32[128,1,128]{2,1,0:T(1,128)} %bitcast.11), calls=%async_computation | async-start | bytes 131072 | tf_op jit(solution)/shard_map/all_to_all | solution.py:580
  77.7 0.8 reshape.33
  78.5 8.8 %all-to-all-done = f32[128,1,128]{2,1,0:T(1,128)S(1)} async-done(((f32[128,1,128]{2,1,0:T(1,128)}), f32[128,1,128]{2,1,0:T(1,128)S(1)}, u32[]{:S(2)}, u32[]{:S(2)}) %all-to-all-start) | async-done | bytes 65568 | tf_op jit(solution)/shard_map/all_to_all | solution.py:580
  87.3 0.5 constant_dynamic-slice_fusion
  87.9 0.7 reduce_sum.19
  (18 shorter events, 0.1 us)
Async XLA Ops:
  0.6 0.7 copy-start.8
  4.5 15.5 %collective-permute-start = (s16[4,264,256]{2,1,0:T(8,128)(2,1)S(1)}, s16[4,264,256]{2,1,0:T(8,128)(2,1)S(1)}, u32[]{:S(2)}, u32[]{:S(2)}) collective-permute-start(s16[4,264,256]{2,1,0:T(8,128)(2,1)S(1)} %get-tuple-element.52), channel_id=1, source_target_pairs={{0,8},{1,9},{2,10},{3,11},{4,12},{5,13},{6,14},{7,15},{8,0},{9,1},... | collective-permute-start | bytes 1622024 | tf_op jit(solution)/shard_map/ppermute | solution.py:528
  8.3 14.9 %collective-permute-start.1 = (s16[4,264,256]{2,1,0:T(8,128)(2,1)S(1)}, s16[4,264,256]{2,1,0:T(8,128)(2,1)S(1)}, u32[]{:S(2)}, u32[]{:S(2)}) collective-permute-start(s16[4,264,256]{2,1,0:T(8,128)(2,1)S(1)} %get-tuple-element.53), channel_id=1, source_target_pairs={{0,2},{1,3},{2,0},{3,1},{4,6},{5,7},{6,4},{7,5},{8,10},{9,11},{10,... | collective-permute-start | bytes 1622024 | tf_op jit(solution)/shard_map/ppermute | solution.py:528
  16.2 15.7 %collective-permute-start.2 = (s16[4,264,256]{2,1,0:T(8,128)(2,1)S(1)}, s16[4,264,256]{2,1,0:T(8,128)(2,1)S(1)}, u32[]{:S(2)}, u32[]{:S(2)}) collective-permute-start(s16[4,264,256]{2,1,0:T(8,128)(2,1)S(1)} %get-tuple-element.55), channel_id=1, source_target_pairs={{0,4},{1,5},{2,6},{3,7},{4,8},{5,9},{6,10},{7,11},{8,12},{9,13},{1... | collective-permute-start | bytes 1622024 | tf_op jit(solution)/shard_map/ppermute | solution.py:528
  16.7 15.3 %collective-permute-start.3 = (s16[4,264,256]{2,1,0:T(8,128)(2,1)S(1)}, s16[4,264,256]{2,1,0:T(8,128)(2,1)S(1)}, u32[]{:S(2)}, u32[]{:S(2)}) collective-permute-start(s16[4,264,256]{2,1,0:T(8,128)(2,1)S(1)} %get-tuple-element.56), channel_id=1, source_target_pairs={{0,12},{1,13},{2,14},{3,15},{4,0},{5,1},{6,2},{7,3},{8,4},{9,5},{1... | collective-permute-start | bytes 1622024 | tf_op jit(solution)/shard_map/ppermute | solution.py:528
  19.0 15.7 %collective-permute-start.4 = (s16[4,264,256]{2,1,0:T(8,128)(2,1)S(1)}, s16[4,264,256]{2,1,0:T(8,128)(2,1)S(1)}, u32[]{:S(2)}, u32[]{:S(2)}) collective-permute-start(s16[4,264,256]{2,1,0:T(8,128)(2,1)S(1)} %get-tuple-element.60), channel_id=1, source_target_pairs={{0,1},{1,2},{2,3},{3,0},{4,5},{5,6},{6,7},{7,4},{8,9},{9,10},{10,1... | collective-permute-start | bytes 1622024 | tf_op jit(solution)/shard_map/ppermute | solution.py:528
  20.0 14.6 %collective-permute-start.5 = (s16[4,264,256]{2,1,0:T(8,128)(2,1)S(1)}, s16[4,264,256]{2,1,0:T(8,128)(2,1)S(1)}, u32[]{:S(2)}, u32[]{:S(2)}) collective-permute-start(s16[4,264,256]{2,1,0:T(8,128)(2,1)S(1)} %get-tuple-element.61), channel_id=1, source_target_pairs={{0,3},{1,0},{2,1},{3,2},{4,7},{5,4},{6,5},{7,6},{8,11},{9,8},{10,9... | collective-permute-start | bytes 1622024 | tf_op jit(solution)/shard_map/ppermute | solution.py:528
  23.2 3.7 %copy-start.5 = (f32[1,131072]{1,0:T(1,128)S(1)}, f32[1,131072]{1,0:T(1,128)}, u32[]{:S(2)}) copy-start(f32[1,131072]{1,0:T(1,128)} %param.14) | copy-start | bytes 1572868
  23.2 31.3 %copy-start.7 = (s32[65536]{0:T(1024)S(1)}, s32[65536]{0:T(1024)}, u32[]{:S(2)}) copy-start(s32[65536]{0:T(1024)} %param.17) | copy-start | bytes 786436
  23.2 34.6 %copy-start = (bf16[4,2,256,256]{3,2,1,0:T(8,128)(2,1)S(1)}, bf16[4,2,256,256]{3,2,1,0:T(8,128)(2,1)}, u32[]{:S(2)}) copy-start(bf16[4,2,256,256]{3,2,1,0:T(8,128)(2,1)} %constant.24.clone.rows_forward) | copy-start | bytes 3145732
  23.2 34.6 %copy-start.1 = (bf16[4,2,256,256]{3,2,1,0:T(8,128)(2,1)S(1)}, bf16[4,2,256,256]{3,2,1,0:T(8,128)(2,1)}, u32[]{:S(2)}) copy-start(bf16[4,2,256,256]{3,2,1,0:T(8,128)(2,1)} %constant.27.clone.rows_back) | copy-start | bytes 3145732
  23.2 34.6 %copy-start.2 = (f32[4,2,128,256]{3,2,1,0:T(8,128)S(1)}, f32[4,2,128,256]{3,2,1,0:T(8,128)}, u32[]{:S(2)}) copy-start(f32[4,2,128,256]{3,2,1,0:T(8,128)} %constant.28.clone.twist) | copy-start | bytes 3145732
  23.2 34.6 %copy-start.3 = (bf16[2,2,256,256]{3,2,1,0:T(8,128)(2,1)S(1)}, bf16[2,2,256,256]{3,2,1,0:T(8,128)(2,1)}, u32[]{:S(2)}) copy-start(bf16[2,2,256,256]{3,2,1,0:T(8,128)(2,1)} %constant.25.clone.columns_forward) | copy-start | bytes 1572868
  23.3 34.6 %copy-start.4 = (bf16[2,2,256,256]{3,2,1,0:T(8,128)(2,1)S(1)}, bf16[2,2,256,256]{3,2,1,0:T(8,128)(2,1)}, u32[]{:S(2)}) copy-start(bf16[2,2,256,256]{3,2,1,0:T(8,128)(2,1)} %constant.26.clone.columns_back) | copy-start | bytes 1572868
  23.3 34.6 %copy-start.6 = (f32[256,256]{1,0:T(8,128)S(1)}, f32[256,256]{1,0:T(8,128)}, u32[]{:S(2)}) copy-start(f32[256,256]{1,0:T(8,128)} %constant.29.clone.group) | copy-start | bytes 786436
  23.3 34.6 %copy-start.9 = (s32[1,64]{1,0:T(1,128)S(1)}, s32[1,64]{1,0:T(1,128)}, u32[]{:S(2)}) copy-start(s32[1,64]{1,0:T(1,128)} %flags_ref.1) | copy-start | bytes 772
  35.4 10.2 %collective-permute-start.6 = (s16[264,256]{1,0:T(8,128)(2,1)S(1)}, s16[264,256]{1,0:T(8,128)(2,1)S(1)}, u32[]{:S(2)}, u32[]{:S(2)}) collective-permute-start(s16[264,256]{1,0:T(8,128)(2,1)S(1)} %get-tuple-element.69), channel_id=1, source_target_pairs={{0,2},{1,3},{2,0},{3,1},{4,6},{5,7},{6,4},{7,5},{8,10},{9,11},{10,... | collective-permute-start | bytes 405512 | tf_op jit(solution)/shard_map/ppermute | solution.py:528
  39.2 6.9 %collective-permute-start.7 = (s16[264,256]{1,0:T(8,128)(2,1)S(1)}, s16[264,256]{1,0:T(8,128)(2,1)S(1)}, u32[]{:S(2)}, u32[]{:S(2)}) collective-permute-start(s16[264,256]{1,0:T(8,128)(2,1)S(1)} %get-tuple-element.70), channel_id=1, source_target_pairs={{0,1},{1,2},{2,3},{3,0},{4,5},{5,6},{6,7},{7,4},{8,9},{9,10},{10,1... | collective-permute-start | bytes 405512 | tf_op jit(solution)/shard_map/ppermute | solution.py:528
  39.2 6.9 %collective-permute-start.8 = (s16[264,256]{1,0:T(8,128)(2,1)S(1)}, s16[264,256]{1,0:T(8,128)(2,1)S(1)}, u32[]{:S(2)}, u32[]{:S(2)}) collective-permute-start(s16[264,256]{1,0:T(8,128)(2,1)S(1)} %get-tuple-element.71), channel_id=1, source_target_pairs={{0,3},{1,0},{2,1},{3,2},{4,7},{5,4},{6,5},{7,6},{8,11},{9,8},{10,9... | collective-permute-start | bytes 405512 | tf_op jit(solution)/shard_map/ppermute | solution.py:528
  42.6 9.1 %collective-permute-start.10 = (s16[264,256]{1,0:T(8,128)(2,1)S(1)}, s16[264,256]{1,0:T(8,128)(2,1)S(1)}, u32[]{:S(2)}, u32[]{:S(2)}) collective-permute-start(s16[264,256]{1,0:T(8,128)(2,1)S(1)} %get-tuple-element.78), channel_id=1, source_target_pairs={{0,4},{1,5},{2,6},{3,7},{4,8},{5,9},{6,10},{7,11},{8,12},{9,13},{1... | collective-permute-start | bytes 405512 | tf_op jit(solution)/shard_map/ppermute | solution.py:528
  43.3 8.4 %collective-permute-start.11 = (s16[264,256]{1,0:T(8,128)(2,1)S(1)}, s16[264,256]{1,0:T(8,128)(2,1)S(1)}, u32[]{:S(2)}, u32[]{:S(2)}) collective-permute-start(s16[264,256]{1,0:T(8,128)(2,1)S(1)} %get-tuple-element.79), channel_id=1, source_target_pairs={{0,12},{1,13},{2,14},{3,15},{4,0},{5,1},{6,2},{7,3},{8,4},{9,5},{1... | collective-permute-start | bytes 405512 | tf_op jit(solution)/shard_map/ppermute | solution.py:528
  45.5 6.2 %collective-permute-start.9 = (s16[264,256]{1,0:T(8,128)(2,1)S(1)}, s16[264,256]{1,0:T(8,128)(2,1)S(1)}, u32[]{:S(2)}, u32[]{:S(2)}) collective-permute-start(s16[264,256]{1,0:T(8,128)(2,1)S(1)} %get-tuple-element.77), channel_id=1, source_target_pairs={{0,8},{1,9},{2,10},{3,11},{4,12},{5,13},{6,14},{7,15},{8,0},{9,1},... | collective-permute-start | bytes 405512 | tf_op jit(solution)/shard_map/ppermute | solution.py:528
  46.4 5.3 %collective-permute-start.12 = (f32[2,16,256]{2,1,0:T(8,128)S(1)}, f32[2,16,256]{2,1,0:T(8,128)S(1)}, u32[]{:S(2)}, u32[]{:S(2)}) collective-permute-start(f32[2,16,256]{2,1,0:T(8,128)S(1)} %get-tuple-element.81), channel_id=1, source_target_pairs={{1,0},{2,1},{3,2},{4,3},{5,4},{6,5},{7,6},{8,7},{9,8},{10,9},{11,1... | collective-permute-start | bytes 98312 | tf_op jit(solution)/shard_map/ppermute | solution.py:571
  47.7 8.5 %collective-permute-start.13 = (s16[264,256]{1,0:T(8,128)(2,1)S(1)}, s16[264,256]{1,0:T(8,128)(2,1)S(1)}, u32[]{:S(2)}, u32[]{:S(2)}) collective-permute-start(s16[264,256]{1,0:T(8,128)(2,1)S(1)} %get-tuple-element.87), channel_id=1, source_target_pairs={{0,1},{1,2},{2,3},{3,4},{4,5},{5,6},{6,7},{7,8},{8,9},{9,10},{10,1... | collective-permute-start | bytes 405512 | tf_op jit(solution)/shard_map/ppermute | solution.py:569
  52.0 5.9 %collective-permute-start.14 = (s16[264,256]{1,0:T(8,128)(2,1)S(1)}, s16[264,256]{1,0:T(8,128)(2,1)S(1)}, u32[]{:S(2)}, u32[]{:S(2)}) collective-permute-start(s16[264,256]{1,0:T(8,128)(2,1)S(1)} %get-tuple-element.88), channel_id=1, source_target_pairs={{0,1},{1,2},{2,3},{3,4},{4,5},{5,6},{6,7},{7,8},{8,9},{9,10},{10,1... | collective-permute-start | bytes 405512 | tf_op jit(solution)/shard_map/ppermute | solution.py:569
  64.6 22.7 %all-to-all-start = ((f32[128,1,128]{2,1,0:T(1,128)}), f32[128,1,128]{2,1,0:T(1,128)S(1)}, u32[]{:S(2)}, u32[]{:S(2)}) async-start(f32[128,1,128]{2,1,0:T(1,128)} %bitcast.11), calls=%async_computation | async-start | bytes 131072 | tf_op jit(solution)/shard_map/all_to_all | solution.py:580

commit v6 on v5

--- a/solution.py
+++ b/solution.py
@@ -453,8 +453,10 @@
     total_ref[...] = jnp.concatenate([total, jnp.zeros_like(total)], axis=1)
     pair = [total_ref[pl.ds(side, N_TM, stride=2), :][:, :LOW_BINS] for side in (0, 1)]
     own = jnp.concatenate(pair, axis=1)
-    for channel in range(CHANNELS):
-        profile_ref[pl.ds(channel * N_TM, N_TM), :] = own
+    for shard in range(N_TM):
+        profile_ref[pl.ds(shard * CHANNELS, CHANNELS), :] = jnp.broadcast_to(
+            own[shard : shard + 1], (CHANNELS, LANES)
+        )
 
 
 def mark_body(bins_ref, high_marks, low_marks, high_ref, low_ref):
@@ -536,7 +538,7 @@
         .reshape(2, TIME_CHUNKS * 4, LANES)
     )
     gains = antenna_gains.transpose(0, 2, 1)
-    order = (2, 1, 3, 0)
+    order = (1, 3, 2, 0)
 
     def first_send(half, step, value):
         return send(value, step, 0) if half == 0 else send(value, 0, step)
@@ -577,8 +579,8 @@
     )
     dedispersed = filtered.reshape(2, 1, HALF)
     sk_weight = weight[:, :64]
-    arrived = lax.all_to_all(partial_profile, ("chan", "tm"), 0, 0, tiled=True)
-    by_channel = jnp.sum(arrived.reshape(CHANNELS, N_TM, LANES), axis=1)
+    arrived = lax.all_to_all(partial_profile, ("tm", "chan"), 0, 0, tiled=True)
+    by_channel = jnp.sum(arrived.reshape(N_TM, CHANNELS, LANES), axis=0)
     profile = lax.dynamic_slice_in_dim(by_channel, lax.axis_index("chan"), 1, 0)
     band_profile = jnp.sum(by_channel, axis=0)
     return (dedispersed, sk_weight, profile, band_profile)

time: 88.7 us -> 88.2 us (level)
  waiting for transfers between devices: 17.4 us -> 16.5 us
    all_to_all x1, starting transfers between devices: 13.1 us -> 15.5 us  [on_device(): arrived = lax.all_to_all(partial_profile, ('tm', 'chan'), 0, 0, tiled=True)]
    ppermute x12, starting transfers between devices: 21.5 us -> 19.8 us  [send(): return lax.ppermute(value, 'tm', steps(down, across))]
  transfers between devices with their start and end apart: 16 -> 16, of which waited for: 7 -> 7; matrix products, arithmetic and copies ran while one was open for 1% -> 1% of each run, Pallas kernels for 15% -> 16%
where the time goes in v6:
time: 88.2 us; the launch traced here: 87.9 us
  starting transfers between devices  42.8 us (49%)
  Pallas kernels  24.4 us (28%)
  waiting for transfers between devices  16.5 us (19%)
  local copies, waits for them, and re-layouts  2.02 us (2%)
  between operations  1.57 us (2%)
    ppermute x12, starting transfers between devices, send(): return lax.ppermute(value, 'tm', steps(down, across))  19.8 us
    all_to_all x1, starting transfers between devices, on_device(): arrived = lax.all_to_all(partial_profile, ('tm', 'chan'), 0, 0, tiled=True)  15.5 us
    pallas_call x3, Pallas kernels, beamform(): pl.pallas_call(lambda *refs: beam_body(messages, *refs), in_specs=[pl.Blo...  11.9 us
    all_to_all x1, waiting for transfers between devices, on_device(): arrived = lax.all_to_all(partial_profile, ('tm', 'chan'), 0, 0, tiled=True)  8.63 us
    ppermute x12, waiting for transfers between devices, send(): return lax.ppermute(value, 'tm', steps(down, across))  7.07 us
    pallas_call x1, Pallas kernels, filter_and_fold(): pl.pallas_call(main_body, in_specs=[pl.BlockSpec(memory_space=pltpu.SMEM)...  6.77 us
    ppermute x2, starting transfers between devices, on_device(): before.append(lax.ppermute(ahead, 'tm', forward))  6.19 us
    pallas_call x1, Pallas kernels, make_response(): pl.pallas_call(response_body, in_specs=[pl.BlockSpec(memory_space=pltpu.S...  2.05 us
  transfers between devices with their start and end apart: 16, of which 7 were waited for; matrix products, arithmetic and copies ran while one was open for 1% of the time, Pallas kernels for 16%

profile of v6, /device:TPU:1, one launch (start us, length us, event | category | flops | bytes accessed | tf_op | source)
XLA Modules:
  0.0 87.9 jit_solution(5165888733933900807)
XLA Ops:
  0.6 0.7 copy-done.8
  1.3 3.2 %beamform.3 = (s16[4,264,256]{2,1,0:T(8,128)(2,1)S(1)}, s16[4,264,256]{2,1,0:T(8,128)(2,1)S(1)}, f32[8,128]{1,0:T(8,128)S(1)}) custom-call(f32[2,1,64]{2,1,0:T(1,128)S(1)} %bitcast.19, bf16[2,32768,128]{2,1,0:T(8,128)(2,1)} %bitcast.22), custom_call_target="tpu_custom_call" | custom-call | tf_op jit(solution)/shard_map/beamform/pallas_call | solution.py:193
  4.5 3.8 %collective-permute-start = (s16[4,264,256]{2,1,0:T(8,128)(2,1)S(1)}, s16[4,264,256]{2,1,0:T(8,128)(2,1)S(1)}, u32[]{:S(2)}, u32[]{:S(2)}) collective-permute-start(s16[4,264,256]{2,1,0:T(8,128)(2,1)S(1)} %get-tuple-element.52), channel_id=1, source_target_pairs={{0,8},{1,9},{2,10},{3,11},{4,12},{5,13},{6,14},{7,15},{8,0},{9,1},... | collective-permute-start | bytes 1622024 | tf_op jit(solution)/shard_map/ppermute | solution.py:530
  8.3 2.7 %collective-permute-start.1 = (s16[4,264,256]{2,1,0:T(8,128)(2,1)S(1)}, s16[4,264,256]{2,1,0:T(8,128)(2,1)S(1)}, u32[]{:S(2)}, u32[]{:S(2)}) collective-permute-start(s16[4,264,256]{2,1,0:T(8,128)(2,1)S(1)} %get-tuple-element.53), channel_id=1, source_target_pairs={{0,2},{1,3},{2,0},{3,1},{4,6},{5,7},{6,4},{7,5},{8,10},{9,11},{10,... | collective-permute-start | bytes 1622024 | tf_op jit(solution)/shard_map/ppermute | solution.py:530
  11.1 5.2 %beamform.4 = (s16[4,264,256]{2,1,0:T(8,128)(2,1)S(1)}, s16[4,264,256]{2,1,0:T(8,128)(2,1)S(1)}, s16[4,264,256]{2,1,0:T(8,128)(2,1)S(1)}, s16[4,264,256]{2,1,0:T(8,128)(2,1)S(1)}, f32[8,128]{1,0:T(8,128)S(1)}) custom-call(f32[2,1,64]{2,1,0:T(1,128)S(1)} %bitcast.20, bf16[2,32768,128]{2,1,0:T(8,128)(2,1)} %bitcast.23, f32[8,128]{1,0:T(8,128)S(1)} %get-tuple-element.50.refs_2_), custom_call_target="tpu_custom_call" | custom-call | tf_op jit(solution)/shard_map/beamform/pallas_call | solution.py:193
  16.2 0.5 collective-permute-start.2
  16.7 2.3 %collective-permute-start.3 = (s16[4,264,256]{2,1,0:T(8,128)(2,1)S(1)}, s16[4,264,256]{2,1,0:T(8,128)(2,1)S(1)}, u32[]{:S(2)}, u32[]{:S(2)}) collective-permute-start(s16[4,264,256]{2,1,0:T(8,128)(2,1)S(1)} %get-tuple-element.56), channel_id=1, source_target_pairs={{0,12},{1,13},{2,14},{3,15},{4,0},{5,1},{6,2},{7,3},{8,4},{9,5},{1... | collective-permute-start | bytes 1622024 | tf_op jit(solution)/shard_map/ppermute | solution.py:530
  19.0 0.3 collective-permute-start.4
  19.3 0.8 collective-permute-done.refs_0_
  20.0 2.5 %collective-permute-start.5 = (s16[4,264,256]{2,1,0:T(8,128)(2,1)S(1)}, s16[4,264,256]{2,1,0:T(8,128)(2,1)S(1)}, u32[]{:S(2)}, u32[]{:S(2)}) collective-permute-start(s16[4,264,256]{2,1,0:T(8,128)(2,1)S(1)} %get-tuple-element.61), channel_id=1, source_target_pairs={{0,3},{1,0},{2,1},{3,2},{4,7},{5,4},{6,5},{7,6},{8,11},{9,8},{10,9... | collective-permute-start | bytes 1622024 | tf_op jit(solution)/shard_map/ppermute | solution.py:530
  23.2 0.0 collective-permute-done.1.refs_0_
  23.2 0.0 copy-start.5
  23.2 0.0 copy-start.7
  23.2 0.0 copy-start
  23.2 0.0 copy-start.1
  23.2 0.0 copy-start.2
  23.2 0.0 copy-start.3
  23.3 0.0 copy-start.4
  23.3 0.0 copy-start.6
  23.3 0.0 copy-start.9
  23.3 3.6 %beamform.5 = (s16[4,264,256]{2,1,0:T(8,128)(2,1)S(1)}, s16[4,264,256]{2,1,0:T(8,128)(2,1)S(1)}, f32[8,128]{1,0:T(8,128)}) custom-call(f32[2,1,64]{2,1,0:T(1,128)S(1)} %bitcast.21, bf16[2,32768,128]{2,1,0:T(8,128)(2,1)} %bitcast.24, f32[8,128]{1,0:T(8,128)S(1)} %get-tuple-element.57.refs_2_), custom_call_target="tpu_custom_call" | custom-call | tf_op jit(solution)/shard_map/beamform/pallas_call | solution.py:193
  26.9 2.1 %response.1 = f32[2,2,512,128]{3,2,1,0:T(8,128)S(1)} custom-call(s32[1]{0:T(128)S(6)} %copy.25.offset, f32[1024,128]{1,0:T(8,128)S(1)} %bitcast.17), custom_call_target="tpu_custom_call" | custom-call | tf_op jit(solution)/shard_map/response/pallas_call | solution.py:287
  28.9 3.0 %collective-permute-done.2.refs_1_ = s16[4,264,256]{2,1,0:T(8,128)(2,1)S(1)} collective-permute-done((s16[4,264,256]{2,1,0:T(8,128)(2,1)S(1)}, s16[4,264,256]{2,1,0:T(8,128)(2,1)S(1)}, u32[]{:S(2)}, u32[]{:S(2)}) %collective-permute-start.2) | collective-permute-done | bytes 540704 | tf_op jit(solution)/shard_map/ppermute | solution.py:530
  31.9 0.1 collective-permute-done.3.refs_2_
  32.0 2.7 %collective-permute-done.4.refs_1_ = s16[4,264,256]{2,1,0:T(8,128)(2,1)S(1)} collective-permute-done((s16[4,264,256]{2,1,0:T(8,128)(2,1)S(1)}, s16[4,264,256]{2,1,0:T(8,128)(2,1)S(1)}, u32[]{:S(2)}, u32[]{:S(2)}) %collective-permute-start.4) | collective-permute-done | bytes 540704 | tf_op jit(solution)/shard_map/ppermute | solution.py:530
  34.6 0.0 collective-permute-done.5.refs_2_
  34.6 0.8 middle.2
  35.4 1.3 %collective-permute-start.6 = (s16[264,256]{1,0:T(8,128)(2,1)S(1)}, s16[264,256]{1,0:T(8,128)(2,1)S(1)}, u32[]{:S(2)}, u32[]{:S(2)}) collective-permute-start(s16[264,256]{1,0:T(8,128)(2,1)S(1)} %get-tuple-element.69), channel_id=1, source_target_pairs={{0,1},{1,2},{2,3},{3,0},{4,5},{5,6},{6,7},{7,4},{8,9},{9,10},{10,1... | collective-permute-start | bytes 405512 | tf_op jit(solution)/shard_map/ppermute | solution.py:530
  36.6 1.5 %collective-permute-start.7 = (s16[264,256]{1,0:T(8,128)(2,1)S(1)}, s16[264,256]{1,0:T(8,128)(2,1)S(1)}, u32[]{:S(2)}, u32[]{:S(2)}) collective-permute-start(s16[264,256]{1,0:T(8,128)(2,1)S(1)} %get-tuple-element.70), channel_id=1, source_target_pairs={{0,3},{1,0},{2,1},{3,2},{4,7},{5,4},{6,5},{7,6},{8,11},{9,8},{10,9... | collective-permute-start | bytes 405512 | tf_op jit(solution)/shard_map/ppermute | solution.py:530
  38.1 2.5 %collective-permute-start.8 = (s16[264,256]{1,0:T(8,128)(2,1)S(1)}, s16[264,256]{1,0:T(8,128)(2,1)S(1)}, u32[]{:S(2)}, u32[]{:S(2)}) collective-permute-start(s16[264,256]{1,0:T(8,128)(2,1)S(1)} %get-tuple-element.71), channel_id=1, source_target_pairs={{0,2},{1,3},{2,0},{3,1},{4,6},{5,7},{6,4},{7,5},{8,10},{9,11},{10,... | collective-permute-start | bytes 405512 | tf_op jit(solution)/shard_map/ppermute | solution.py:530
  40.6 0.8 middle.3
  41.4 1.0 %collective-permute-start.10 = (s16[264,256]{1,0:T(8,128)(2,1)S(1)}, s16[264,256]{1,0:T(8,128)(2,1)S(1)}, u32[]{:S(2)}, u32[]{:S(2)}) collective-permute-start(s16[264,256]{1,0:T(8,128)(2,1)S(1)} %get-tuple-element.78), channel_id=1, source_target_pairs={{0,12},{1,13},{2,14},{3,15},{4,0},{5,1},{6,2},{7,3},{8,4},{9,5},{1... | collective-permute-start | bytes 405512 | tf_op jit(solution)/shard_map/ppermute | solution.py:530
  42.4 1.4 %collective-permute-start.11 = (s16[264,256]{1,0:T(8,128)(2,1)S(1)}, s16[264,256]{1,0:T(8,128)(2,1)S(1)}, u32[]{:S(2)}, u32[]{:S(2)}) collective-permute-start(s16[264,256]{1,0:T(8,128)(2,1)S(1)} %get-tuple-element.79), channel_id=1, source_target_pairs={{0,8},{1,9},{2,10},{3,11},{4,12},{5,13},{6,14},{7,15},{8,0},{9,1},... | collective-permute-start | bytes 405512 | tf_op jit(solution)/shard_map/ppermute | solution.py:530
  43.8 0.6 collective-permute-done.8.refs_3_
  44.5 0.2 last.2
  44.7 1.3 %collective-permute-start.12 = (f32[2,16,256]{2,1,0:T(8,128)S(1)}, f32[2,16,256]{2,1,0:T(8,128)S(1)}, u32[]{:S(2)}, u32[]{:S(2)}) collective-permute-start(f32[2,16,256]{2,1,0:T(8,128)S(1)} %get-tuple-element.81), channel_id=1, source_target_pairs={{1,0},{2,1},{3,2},{4,3},{5,4},{6,5},{7,6},{8,7},{9,8},{10,9},{11,1... | collective-permute-start | bytes 98312 | tf_op jit(solution)/shard_map/ppermute | solution.py:573
  46.0 4.0 %collective-permute-start.13 = (s16[264,256]{1,0:T(8,128)(2,1)S(1)}, s16[264,256]{1,0:T(8,128)(2,1)S(1)}, u32[]{:S(2)}, u32[]{:S(2)}) collective-permute-start(s16[264,256]{1,0:T(8,128)(2,1)S(1)} %get-tuple-element.87), channel_id=1, source_target_pairs={{0,1},{1,2},{2,3},{3,4},{4,5},{5,6},{6,7},{7,8},{8,9},{9,10},{10,1... | collective-permute-start | bytes 405512 | tf_op jit(solution)/shard_map/ppermute | solution.py:571
  50.0 0.0 collective-permute-done.10.refs_2_
  50.1 0.2 last.3
  50.3 2.2 %collective-permute-start.14 = (s16[264,256]{1,0:T(8,128)(2,1)S(1)}, s16[264,256]{1,0:T(8,128)(2,1)S(1)}, u32[]{:S(2)}, u32[]{:S(2)}) collective-permute-start(s16[264,256]{1,0:T(8,128)(2,1)S(1)} %get-tuple-element.88), channel_id=1, source_target_pairs={{0,1},{1,2},{2,3},{3,4},{4,5},{5,6},{6,7},{7,8},{8,9},{9,10},{10,1... | collective-permute-start | bytes 405512 | tf_op jit(solution)/shard_map/ppermute | solution.py:571
  52.5 1.7 %mark_bins.1 = (bf16[256,32,256]{2,1,0:T(8,128)(2,1)S(1)}, bf16[256,64,256]{2,1,0:T(8,128)(2,1)S(1)}) custom-call(s32[512,128]{1,0:T(8,128)S(1)} %bitcast.18), custom_call_target="tpu_custom_call" | custom-call | tf_op jit(solution)/shard_map/mark_bins/pallas_call | solution.py:489
  54.2 0.8 collective-permute-done.14.before_last
  55.1 6.8 %filter_and_fold.1 = (bf16[2,256,256]{2,1,0:T(8,128)(2,1)S(1)}, f32[1,128]{1,0:T(1,128)}, f32[128,128]{1,0:T(8,128)}) custom-call(s32[1]{0:T(128)S(6)} %copy.25.offset, f32[2,128,256]{2,1,0:T(8,128)S(1)} %get-tuple-element.72.own_first, f32[2,128,256]{2,1,0:T(8,128)S(1)} %get-tuple-element.86.own_last, ...), custom_call_target="tpu_custom_call" | custom-call | tf_op jit(solution)/shard_map/filter_and_fold/pallas_call | solution.py:503
  61.9 15.5 %all-to-all-start = ((f32[128,1,128]{2,1,0:T(1,128)}), f32[128,1,128]{2,1,0:T(1,128)S(1)}, u32[]{:S(2)}, u32[]{:S(2)}) async-start(f32[128,1,128]{2,1,0:T(1,128)} %bitcast.11), calls=%async_computation | async-start | bytes 131072 | tf_op jit(solution)/shard_map/all_to_all | solution.py:582
  77.3 0.8 reshape.33
  78.1 8.6 %all-to-all-done = f32[128,1,128]{2,1,0:T(1,128)S(1)} async-done(((f32[128,1,128]{2,1,0:T(1,128)}), f32[128,1,128]{2,1,0:T(1,128)S(1)}, u32[]{:S(2)}, u32[]{:S(2)}) %all-to-all-start) | async-done | bytes 65568 | tf_op jit(solution)/shard_map/all_to_all | solution.py:582
  86.8 0.5 constant_dynamic-slice_fusion
  87.3 0.7 reduce_sum.19
  (18 shorter events, 0.1 us)
Async XLA Ops:
  0.6 0.7 copy-start.8
  4.5 15.5 %collective-permute-start = (s16[4,264,256]{2,1,0:T(8,128)(2,1)S(1)}, s16[4,264,256]{2,1,0:T(8,128)(2,1)S(1)}, u32[]{:S(2)}, u32[]{:S(2)}) collective-permute-start(s16[4,264,256]{2,1,0:T(8,128)(2,1)S(1)} %get-tuple-element.52), channel_id=1, source_target_pairs={{0,8},{1,9},{2,10},{3,11},{4,12},{5,13},{6,14},{7,15},{8,0},{9,1},... | collective-permute-start | bytes 1622024 | tf_op jit(solution)/shard_map/ppermute | solution.py:530
  8.3 14.9 %collective-permute-start.1 = (s16[4,264,256]{2,1,0:T(8,128)(2,1)S(1)}, s16[4,264,256]{2,1,0:T(8,128)(2,1)S(1)}, u32[]{:S(2)}, u32[]{:S(2)}) collective-permute-start(s16[4,264,256]{2,1,0:T(8,128)(2,1)S(1)} %get-tuple-element.53), channel_id=1, source_target_pairs={{0,2},{1,3},{2,0},{3,1},{4,6},{5,7},{6,4},{7,5},{8,10},{9,11},{10,... | collective-permute-start | bytes 1622024 | tf_op jit(solution)/shard_map/ppermute | solution.py:530
  16.2 15.7 %collective-permute-start.2 = (s16[4,264,256]{2,1,0:T(8,128)(2,1)S(1)}, s16[4,264,256]{2,1,0:T(8,128)(2,1)S(1)}, u32[]{:S(2)}, u32[]{:S(2)}) collective-permute-start(s16[4,264,256]{2,1,0:T(8,128)(2,1)S(1)} %get-tuple-element.55), channel_id=1, source_target_pairs={{0,4},{1,5},{2,6},{3,7},{4,8},{5,9},{6,10},{7,11},{8,12},{9,13},{1... | collective-permute-start | bytes 1622024 | tf_op jit(solution)/shard_map/ppermute | solution.py:530
  16.7 15.3 %collective-permute-start.3 = (s16[4,264,256]{2,1,0:T(8,128)(2,1)S(1)}, s16[4,264,256]{2,1,0:T(8,128)(2,1)S(1)}, u32[]{:S(2)}, u32[]{:S(2)}) collective-permute-start(s16[4,264,256]{2,1,0:T(8,128)(2,1)S(1)} %get-tuple-element.56), channel_id=1, source_target_pairs={{0,12},{1,13},{2,14},{3,15},{4,0},{5,1},{6,2},{7,3},{8,4},{9,5},{1... | collective-permute-start | bytes 1622024 | tf_op jit(solution)/shard_map/ppermute | solution.py:530
  19.0 15.7 %collective-permute-start.4 = (s16[4,264,256]{2,1,0:T(8,128)(2,1)S(1)}, s16[4,264,256]{2,1,0:T(8,128)(2,1)S(1)}, u32[]{:S(2)}, u32[]{:S(2)}) collective-permute-start(s16[4,264,256]{2,1,0:T(8,128)(2,1)S(1)} %get-tuple-element.60), channel_id=1, source_target_pairs={{0,1},{1,2},{2,3},{3,0},{4,5},{5,6},{6,7},{7,4},{8,9},{9,10},{10,1... | collective-permute-start | bytes 1622024 | tf_op jit(solution)/shard_map/ppermute | solution.py:530
  20.0 14.6 %collective-permute-start.5 = (s16[4,264,256]{2,1,0:T(8,128)(2,1)S(1)}, s16[4,264,256]{2,1,0:T(8,128)(2,1)S(1)}, u32[]{:S(2)}, u32[]{:S(2)}) collective-permute-start(s16[4,264,256]{2,1,0:T(8,128)(2,1)S(1)} %get-tuple-element.61), channel_id=1, source_target_pairs={{0,3},{1,0},{2,1},{3,2},{4,7},{5,4},{6,5},{7,6},{8,11},{9,8},{10,9... | collective-permute-start | bytes 1622024 | tf_op jit(solution)/shard_map/ppermute | solution.py:530
  23.2 3.7 %copy-start.5 = (f32[1,131072]{1,0:T(1,128)S(1)}, f32[1,131072]{1,0:T(1,128)}, u32[]{:S(2)}) copy-start(f32[1,131072]{1,0:T(1,128)} %param.14) | copy-start | bytes 1572868
  23.2 29.3 %copy-start.7 = (s32[65536]{0:T(1024)S(1)}, s32[65536]{0:T(1024)}, u32[]{:S(2)}) copy-start(s32[65536]{0:T(1024)} %param.17) | copy-start | bytes 786436
  23.2 31.8 %copy-start = (bf16[4,2,256,256]{3,2,1,0:T(8,128)(2,1)S(1)}, bf16[4,2,256,256]{3,2,1,0:T(8,128)(2,1)}, u32[]{:S(2)}) copy-start(bf16[4,2,256,256]{3,2,1,0:T(8,128)(2,1)} %constant.24.clone.rows_forward) | copy-start | bytes 3145732
  23.2 31.8 %copy-start.1 = (bf16[4,2,256,256]{3,2,1,0:T(8,128)(2,1)S(1)}, bf16[4,2,256,256]{3,2,1,0:T(8,128)(2,1)}, u32[]{:S(2)}) copy-start(bf16[4,2,256,256]{3,2,1,0:T(8,128)(2,1)} %constant.27.clone.rows_back) | copy-start | bytes 3145732
  23.2 31.8 %copy-start.2 = (f32[4,2,128,256]{3,2,1,0:T(8,128)S(1)}, f32[4,2,128,256]{3,2,1,0:T(8,128)}, u32[]{:S(2)}) copy-start(f32[4,2,128,256]{3,2,1,0:T(8,128)} %constant.28.clone.twist) | copy-start | bytes 3145732
  23.2 31.8 %copy-start.3 = (bf16[2,2,256,256]{3,2,1,0:T(8,128)(2,1)S(1)}, bf16[2,2,256,256]{3,2,1,0:T(8,128)(2,1)}, u32[]{:S(2)}) copy-start(bf16[2,2,256,256]{3,2,1,0:T(8,128)(2,1)} %constant.25.clone.columns_forward) | copy-start | bytes 1572868
  23.3 31.8 %copy-start.4 = (bf16[2,2,256,256]{3,2,1,0:T(8,128)(2,1)S(1)}, bf16[2,2,256,256]{3,2,1,0:T(8,128)(2,1)}, u32[]{:S(2)}) copy-start(bf16[2,2,256,256]{3,2,1,0:T(8,128)(2,1)} %constant.26.clone.columns_back) | copy-start | bytes 1572868
  23.3 31.8 %copy-start.6 = (f32[256,256]{1,0:T(8,128)S(1)}, f32[256,256]{1,0:T(8,128)}, u32[]{:S(2)}) copy-start(f32[256,256]{1,0:T(8,128)} %constant.29.clone.group) | copy-start | bytes 786436
  23.3 31.8 %copy-start.9 = (s32[1,64]{1,0:T(1,128)S(1)}, s32[1,64]{1,0:T(1,128)}, u32[]{:S(2)}) copy-start(s32[1,64]{1,0:T(1,128)} %flags_ref.1) | copy-start | bytes 772
  35.4 8.4 %collective-permute-start.6 = (s16[264,256]{1,0:T(8,128)(2,1)S(1)}, s16[264,256]{1,0:T(8,128)(2,1)S(1)}, u32[]{:S(2)}, u32[]{:S(2)}) collective-permute-start(s16[264,256]{1,0:T(8,128)(2,1)S(1)} %get-tuple-element.69), channel_id=1, source_target_pairs={{0,1},{1,2},{2,3},{3,0},{4,5},{5,6},{6,7},{7,4},{8,9},{9,10},{10,1... | collective-permute-start | bytes 405512 | tf_op jit(solution)/shard_map/ppermute | solution.py:530
  36.6 7.2 %collective-permute-start.7 = (s16[264,256]{1,0:T(8,128)(2,1)S(1)}, s16[264,256]{1,0:T(8,128)(2,1)S(1)}, u32[]{:S(2)}, u32[]{:S(2)}) collective-permute-start(s16[264,256]{1,0:T(8,128)(2,1)S(1)} %get-tuple-element.70), channel_id=1, source_target_pairs={{0,3},{1,0},{2,1},{3,2},{4,7},{5,4},{6,5},{7,6},{8,11},{9,8},{10,9... | collective-permute-start | bytes 405512 | tf_op jit(solution)/shard_map/ppermute | solution.py:530
  38.1 6.3 %collective-permute-start.8 = (s16[264,256]{1,0:T(8,128)(2,1)S(1)}, s16[264,256]{1,0:T(8,128)(2,1)S(1)}, u32[]{:S(2)}, u32[]{:S(2)}) collective-permute-start(s16[264,256]{1,0:T(8,128)(2,1)S(1)} %get-tuple-element.71), channel_id=1, source_target_pairs={{0,2},{1,3},{2,0},{3,1},{4,6},{5,7},{6,4},{7,5},{8,10},{9,11},{10,... | collective-permute-start | bytes 405512 | tf_op jit(solution)/shard_map/ppermute | solution.py:530
  41.4 8.6 %collective-permute-start.10 = (s16[264,256]{1,0:T(8,128)(2,1)S(1)}, s16[264,256]{1,0:T(8,128)(2,1)S(1)}, u32[]{:S(2)}, u32[]{:S(2)}) collective-permute-start(s16[264,256]{1,0:T(8,128)(2,1)S(1)} %get-tuple-element.78), channel_id=1, source_target_pairs={{0,12},{1,13},{2,14},{3,15},{4,0},{5,1},{6,2},{7,3},{8,4},{9,5},{1... | collective-permute-start | bytes 405512 | tf_op jit(solution)/shard_map/ppermute | solution.py:530
  42.4 7.6 %collective-permute-start.11 = (s16[264,256]{1,0:T(8,128)(2,1)S(1)}, s16[264,256]{1,0:T(8,128)(2,1)S(1)}, u32[]{:S(2)}, u32[]{:S(2)}) collective-permute-start(s16[264,256]{1,0:T(8,128)(2,1)S(1)} %get-tuple-element.79), channel_id=1, source_target_pairs={{0,8},{1,9},{2,10},{3,11},{4,12},{5,13},{6,14},{7,15},{8,0},{9,1},... | collective-permute-start | bytes 405512 | tf_op jit(solution)/shard_map/ppermute | solution.py:530
  43.8 6.2 %collective-permute-start.9 = (s16[264,256]{1,0:T(8,128)(2,1)S(1)}, s16[264,256]{1,0:T(8,128)(2,1)S(1)}, u32[]{:S(2)}, u32[]{:S(2)}) collective-permute-start(s16[264,256]{1,0:T(8,128)(2,1)S(1)} %get-tuple-element.77), channel_id=1, source_target_pairs={{0,4},{1,5},{2,6},{3,7},{4,8},{5,9},{6,10},{7,11},{8,12},{9,13},{1... | collective-permute-start | bytes 405512 | tf_op jit(solution)/shard_map/ppermute | solution.py:530
  44.7 5.3 %collective-permute-start.12 = (f32[2,16,256]{2,1,0:T(8,128)S(1)}, f32[2,16,256]{2,1,0:T(8,128)S(1)}, u32[]{:S(2)}, u32[]{:S(2)}) collective-permute-start(f32[2,16,256]{2,1,0:T(8,128)S(1)} %get-tuple-element.81), channel_id=1, source_target_pairs={{1,0},{2,1},{3,2},{4,3},{5,4},{6,5},{7,6},{8,7},{9,8},{10,9},{11,1... | collective-permute-start | bytes 98312 | tf_op jit(solution)/shard_map/ppermute | solution.py:573
  46.0 8.2 %collective-permute-start.13 = (s16[264,256]{1,0:T(8,128)(2,1)S(1)}, s16[264,256]{1,0:T(8,128)(2,1)S(1)}, u32[]{:S(2)}, u32[]{:S(2)}) collective-permute-start(s16[264,256]{1,0:T(8,128)(2,1)S(1)} %get-tuple-element.87), channel_id=1, source_target_pairs={{0,1},{1,2},{2,3},{3,4},{4,5},{5,6},{6,7},{7,8},{8,9},{9,10},{10,1... | collective-permute-start | bytes 405512 | tf_op jit(solution)/shard_map/ppermute | solution.py:571
  50.3 4.7 %collective-permute-start.14 = (s16[264,256]{1,0:T(8,128)(2,1)S(1)}, s16[264,256]{1,0:T(8,128)(2,1)S(1)}, u32[]{:S(2)}, u32[]{:S(2)}) collective-permute-start(s16[264,256]{1,0:T(8,128)(2,1)S(1)} %get-tuple-element.88), channel_id=1, source_target_pairs={{0,1},{1,2},{2,3},{3,4},{4,5},{5,6},{6,7},{7,8},{8,9},{9,10},{10,1... | collective-permute-start | bytes 405512 | tf_op jit(solution)/shard_map/ppermute | solution.py:571
  61.9 24.9 %all-to-all-start = ((f32[128,1,128]{2,1,0:T(1,128)}), f32[128,1,128]{2,1,0:T(1,128)S(1)}, u32[]{:S(2)}, u32[]{:S(2)}) async-start(f32[128,1,128]{2,1,0:T(1,128)} %bitcast.11), calls=%async_computation | async-start | bytes 131072 | tf_op jit(solution)/shard_map/all_to_all | solution.py:582
